TPU v7x, 32 devices: a whole 2x2x4 slice. The times are simulated.
32 devices in a mesh: fsdp: 4 (over x, core), ctx: 2 (over y), tp: 4 (over z).
Axes of the slice: x: 2, y: 2, z: 4, core: 2. Of those that a mesh axis runs over, the one named last changes fastest.
Arguments:
- hidden_in: bfloat16 [4, 1024, 2048], P('fsdp', 'ctx'), may hold values from -6 to 6
- segment_ids: int32 [4, 1024], P('fsdp', 'ctx'), may hold values from 0 to 3, never falling along the last dimension, each value on 1 to 800 neighbouring positions
- adapter_ids: int32 [4], P('fsdp'), may hold values from 0 to 7
- attention_gain: bfloat16 [2048], replicated, may hold values from 0.099609375 to 1.8984375
- query_gain: bfloat16 [64], replicated, may hold values from 0.099609375 to 1.8984375
- key_gain: bfloat16 [64], replicated, may hold values from 0.099609375 to 1.8984375
- feedforward_gain: bfloat16 [2048], replicated, may hold values from 0.099609375 to 1.8984375
- query_weight: bfloat16 [2048, 2048], P('fsdp', 'tp'), may hold values from -0.125 to 0.125
- key_weight: bfloat16 [2048, 512], P('fsdp', 'tp'), may hold values from -0.125 to 0.125
- value_weight: bfloat16 [2048, 512], P('fsdp', 'tp'), may hold values from -0.125 to 0.125
- output_weight: bfloat16 [2048, 2048], P('tp', 'fsdp'), may hold values from -1 to 1
- gate_weight: bfloat16 [2048, 8192], P('fsdp', 'tp'), may hold values from -0.125 to 0.125
- linear_weight: bfloat16 [2048, 8192], P('fsdp', 'tp'), may hold values from -0.125 to 0.125
- reduce_weight: bfloat16 [8192, 2048], P('tp', 'fsdp'), may hold values from -0.0625 to 0.0625
- query_down: bfloat16 [8, 2048, 16], replicated, may hold values from -0.125 to 0.125
- query_lift: bfloat16 [8, 16, 2048], P(None, None, 'tp'), may hold values from -1.5 to 1.5
- key_down: bfloat16 [8, 2048, 16], replicated, may hold values from -0.125 to 0.125
- key_lift: bfloat16 [8, 16, 512], P(None, None, 'tp'), may hold values from -1.5 to 1.5
- value_down: bfloat16 [8, 2048, 16], replicated, may hold values from -0.125 to 0.125
- value_lift: bfloat16 [8, 16, 512], P(None, None, 'tp'), may hold values from -1.5 to 1.5
- output_down: bfloat16 [8, 2048, 16], P(None, 'tp'), may hold values from -1 to 1
- output_lift: bfloat16 [8, 16, 2048], replicated, may hold values from -1.5 to 1.5
- gate_down: bfloat16 [8, 2048, 16], replicated, may hold values from -0.125 to 0.125
- gate_lift: bfloat16 [8, 16, 8192], P(None, None, 'tp'), may hold values from -1.5 to 1.5
- linear_down: bfloat16 [8, 2048, 16], replicated, may hold values from -0.125 to 0.125
- linear_lift: bfloat16 [8, 16, 8192], P(None, None, 'tp'), may hold values from -1.5 to 1.5
- reduce_down: bfloat16 [8, 8192, 16], P(None, 'tp'), may hold values from -0.0625 to 0.0625
- reduce_lift: bfloat16 [8, 16, 2048], replicated, may hold values from -1.5 to 1.5
- output_cotangent: bfloat16 [4, 1024, 2048], P('fsdp', 'ctx'), may hold values from -6 to 6
Outputs:
- block_out: bfloat16 [4, 1024, 2048], P('fsdp', 'ctx', 'tp')
- input_grad: float32 [4, 1024, 2048], P('fsdp', 'ctx', 'tp')
- grad_query_down: float32 [8, 2048, 16], replicated
- grad_query_lift: float32 [8, 16, 2048], P(None, None, 'tp')
- grad_key_down: float32 [8, 2048, 16], replicated
- grad_key_lift: float32 [8, 16, 512], P(None, None, 'tp')
- grad_value_down: float32 [8, 2048, 16], replicated
- grad_value_lift: float32 [8, 16, 512], P(None, None, 'tp')
- grad_output_down: float32 [8, 2048, 16], P(None, 'tp')
- grad_output_lift: float32 [8, 16, 2048], replicated
- grad_gate_down: float32 [8, 2048, 16], replicated
- grad_gate_lift: float32 [8, 16, 8192], P(None, None, 'tp')
- grad_linear_down: float32 [8, 2048, 16], replicated
- grad_linear_lift: float32 [8, 16, 8192], P(None, None, 'tp')
- grad_reduce_down: float32 [8, 8192, 16], P(None, 'tp')
- grad_reduce_lift: float32 [8, 16, 2048], replicated
Inputs may be any that keep to these rules, and one draw needn't show every extreme that they name: `segment_ids`: within each sequence the ids start at 0 and never fall; each of the 4 documents holds 1 to 800 consecutive tokens, and one holds exactly 800.
All inputs are finite; a program needn't handle non-finite values.
Results may differ from a plain program's by a relative error of at most 0.02.
Values may be sent and summed in bfloat16 or wider, within the bound.
No kernel may reach another device: no remote copies, remote signals or barrier semaphores. Data moves between devices by JAX's collectives and lax.ppermute only.
A program may use at most 192 MiB of HBM per device.

v0:
```python
from functools import partial

import jax
import jax.numpy as jnp
from jax import lax
from jax.sharding import PartitionSpec as P

epsilon = 1e-05
rope_base = 1000000.0
masked_score = -1e30


def shifted(array, axis, by):
    count = lax.axis_size(axis)
    pairs = [(i, i + by) for i in range(count) if 0 <= i + by < count]
    return lax.ppermute(array, axis, pairs)


def root_norm(hidden, norm_gain):
    return (
        hidden * lax.rsqrt(jnp.mean(hidden * hidden, axis=-1, keepdims=True) + epsilon) * norm_gain
    )


def norm_back(hidden, norm_gain, upstream):
    inverse = lax.rsqrt(jnp.mean(hidden * hidden, axis=-1, keepdims=True) + epsilon)
    weighted = upstream * norm_gain
    inner_mean = jnp.mean(weighted * hidden, axis=-1, keepdims=True)
    return inverse * weighted - hidden * inverse**3 * inner_mean


def rotate(hidden, cosine, sine_table):
    half_width = hidden.shape[-1] // 2
    first_half = hidden[..., :half_width]
    second_half = hidden[..., half_width:]
    return jnp.concatenate(
        [
            first_half * cosine - second_half * sine_table,
            second_half * cosine + first_half * sine_table,
        ],
        axis=-1,
    )


def rotate_back(gradient, cosine, sine_table):
    half_width = gradient.shape[-1] // 2
    first_half = gradient[..., :half_width]
    second_half = gradient[..., half_width:]
    return jnp.concatenate(
        [
            first_half * cosine + second_half * sine_table,
            second_half * cosine - first_half * sine_table,
        ],
        axis=-1,
    )


def choose(picker, adapter_table):
    return jnp.einsum(
        "sa,amn->smn", picker, adapter_table.astype(jnp.float32), precision=lax.Precision.HIGHEST
    )


def spread(picker, gradient):
    return jnp.einsum("sa,smn->amn", picker, gradient, precision=lax.Precision.HIGHEST)


def project(inputs, weight, down_pick, lift_pick):
    base_part = jnp.einsum("slk,kn->sln", inputs, weight, preferred_element_type=jnp.float32)
    narrow = jnp.einsum("slk,skr->slr", inputs, down_pick, preferred_element_type=jnp.float32)
    lifted = jnp.einsum(
        "slr,srn->sln", narrow, lift_pick.astype(jnp.float32), precision=lax.Precision.HIGHEST
    )
    return (base_part + lifted, narrow)


def project_back(inputs, grad_low, weight, down_pick, lift_pick, narrow):
    input_part = jnp.einsum("sln,kn->slk", grad_low, weight, preferred_element_type=jnp.float32)
    narrow_grad = jnp.einsum(
        "sln,srn->slr", grad_low, lift_pick, preferred_element_type=jnp.float32
    )
    input_part = input_part + jnp.einsum(
        "slr,skr->slk", narrow_grad, down_pick.astype(jnp.float32), precision=lax.Precision.HIGHEST
    )
    down_grad = jnp.einsum(
        "slk,slr->skr", inputs.astype(jnp.float32), narrow_grad, precision=lax.Precision.HIGHEST
    )
    lift_grad = jnp.einsum(
        "slr,sln->srn", narrow, grad_low.astype(jnp.float32), precision=lax.Precision.HIGHEST
    )
    return (input_part, down_grad, lift_grad)


def score_rows(queries, key_rows, allowed, score_scale):
    raw_scores = (
        jnp.einsum("qgsd,kgd->gsqk", queries, key_rows, preferred_element_type=jnp.float32)
        * score_scale
    )
    return jnp.where(allowed[None, None], raw_scores, masked_score)


def attend(packed, score_scale):
    queries, key_rows, value_rows, allowed = packed
    scores = score_rows(queries, key_rows, allowed, score_scale)
    row_max = jnp.max(scores, axis=-1, keepdims=True)
    exponent = jnp.exp(scores - row_max)
    row_total = jnp.sum(exponent, axis=-1, keepdims=True)
    prob_rows = (exponent / row_total).astype(jnp.bfloat16)
    attended = jnp.einsum(
        "gsqk,kgd->qgsd", prob_rows, value_rows, preferred_element_type=jnp.float32
    )
    return (attended, row_max + jnp.log(row_total))


def attend_back(packed, score_scale):
    queries, key_rows, value_rows, allowed, log_total, upstream = packed
    scores = score_rows(queries, key_rows, allowed, score_scale)
    prob_rows = jnp.exp(scores - log_total)
    value_grad = jnp.einsum(
        "gsqk,qgsd->kgd",
        prob_rows.astype(jnp.bfloat16),
        upstream,
        preferred_element_type=jnp.float32,
    )
    prob_grad = jnp.einsum(
        "qgsd,kgd->gsqk", upstream, value_rows, preferred_element_type=jnp.float32
    )
    row_inner = jnp.sum(prob_rows * prob_grad, axis=-1, keepdims=True)
    score_grad = (prob_rows * (prob_grad - row_inner)).astype(jnp.bfloat16)
    query_grad = (
        jnp.einsum("gsqk,kgd->qgsd", score_grad, key_rows, preferred_element_type=jnp.float32)
        * score_scale
    )
    key_grad = (
        jnp.einsum("gsqk,qgsd->kgd", score_grad, queries, preferred_element_type=jnp.float32)
        * score_scale
    )
    return (query_grad, key_grad, value_grad)


def on_device(
    hidden_in,
    segment_ids,
    adapter_ids,
    attention_gain,
    query_gain,
    key_gain,
    feedforward_gain,
    query_weight,
    key_weight,
    value_weight,
    output_weight,
    gate_weight,
    linear_weight,
    reduce_weight,
    query_down,
    query_lift,
    key_down,
    key_lift,
    value_down,
    value_lift,
    output_down,
    output_lift,
    gate_down,
    gate_lift,
    linear_down,
    linear_lift,
    reduce_down,
    reduce_lift,
    output_cotangent,
):
    query_full, key_full, value_full, output_full = (
        lax.all_gather(query_weight, "fsdp", axis=0, tiled=True),
        lax.all_gather(key_weight, "fsdp", axis=0, tiled=True),
        lax.all_gather(value_weight, "fsdp", axis=0, tiled=True),
        lax.all_gather(output_weight, "fsdp", axis=1, tiled=True),
    )
    seqs_here, local_len, model_width = hidden_in.shape
    head_dim = query_gain.shape[0]
    heads_here = query_full.shape[1] // head_dim
    groups_here = key_full.shape[1] // head_dim
    group_share = heads_here // groups_here
    score_scale = head_dim ** (-0.5)
    context_index = lax.axis_index("ctx")
    tensor_index = lax.axis_index("tp")
    tensor_count = lax.axis_size("tp")
    columns = model_width // tensor_count
    positions = (context_index * local_len + jnp.arange(local_len)).astype(jnp.float32)
    frequency = rope_base ** (-2.0 * jnp.arange(head_dim // 2).astype(jnp.float32) / head_dim)
    angles = positions[:, None] * frequency[None, :]
    cosine = jnp.cos(angles)[None, :, None, :]
    sine_table = jnp.sin(angles)[None, :, None, :]
    picker = (adapter_ids[:, None] == jnp.arange(query_down.shape[0])[None, :]).astype(jnp.float32)
    (
        pick_query_down,
        pick_query_lift,
        pick_key_down,
        pick_key_lift,
        pick_value_down,
        pick_value_lift,
        pick_output_down,
        pick_output_lift,
        pick_gate_down,
        pick_gate_lift,
        pick_linear_down,
        pick_linear_lift,
        pick_reduce_down,
        pick_reduce_lift,
    ) = [
        choose(picker, adapter_table).astype(jnp.bfloat16)
        for adapter_table in (
            query_down,
            query_lift,
            key_down,
            key_lift,
            value_down,
            value_lift,
            output_down,
            output_lift,
            gate_down,
            gate_lift,
            linear_down,
            linear_lift,
            reduce_down,
            reduce_lift,
        )
    ]
    attention_norm = attention_gain.astype(jnp.float32)
    query_norm = query_gain.astype(jnp.float32)
    key_norm = key_gain.astype(jnp.float32)
    feedforward_norm = feedforward_gain.astype(jnp.float32)
    hidden_wide = hidden_in.astype(jnp.float32)
    normed = root_norm(hidden_wide, attention_norm).astype(jnp.bfloat16)
    query_pre, query_narrow = project(normed, query_full, pick_query_down, pick_query_lift)
    key_pre, key_narrow = project(normed, key_full, pick_key_down, pick_key_lift)
    value_pre, value_narrow = project(normed, value_full, pick_value_down, pick_value_lift)
    query_pre = query_pre.reshape(seqs_here, local_len, heads_here, head_dim)
    key_pre = key_pre.reshape(seqs_here, local_len, groups_here, head_dim)
    query_rot = (
        rotate(root_norm(query_pre, query_norm), cosine, sine_table)
        .astype(jnp.bfloat16)
        .reshape(seqs_here, local_len, groups_here, group_share, head_dim)
    )
    key_rot = rotate(root_norm(key_pre, key_norm), cosine, sine_table).astype(jnp.bfloat16)
    value_low = value_pre.astype(jnp.bfloat16).reshape(seqs_here, local_len, groups_here, head_dim)
    own_segment = segment_ids.astype(jnp.bfloat16)
    far_key, far_value, far_segment = shifted((key_rot, value_low, own_segment), "ctx", 1)
    token_index = jnp.arange(local_len)
    causal = token_index[:, None] >= token_index[None, :]
    far_allowed = (far_segment[:, None, :] == own_segment[:, :, None]) & (context_index > 0)
    near_allowed = (own_segment[:, None, :] == own_segment[:, :, None]) & causal[None]
    allowed = jnp.concatenate([far_allowed, near_allowed], axis=2)
    key_rows = jnp.concatenate([far_key, key_rot], axis=1)
    value_rows = jnp.concatenate([far_value, value_low], axis=1)
    attended, log_total = lax.map(
        partial(attend, score_scale=score_scale), (query_rot, key_rows, value_rows, allowed)
    )
    attended_low = attended.reshape(seqs_here, local_len, heads_here * head_dim).astype(
        jnp.bfloat16
    )
    branch_part, output_narrow = project(
        attended_low, output_full, pick_output_down, pick_output_lift
    )
    middle = hidden_wide + lax.psum(branch_part, "tp")
    middle_cols = lax.dynamic_slice_in_dim(middle, tensor_index * columns, columns, 2)
    ffn_normed = root_norm(middle, feedforward_norm).astype(jnp.bfloat16)
    gate_full, linear_full, reduce_full = (
        lax.all_gather(gate_weight, "fsdp", axis=0, tiled=True),
        lax.all_gather(linear_weight, "fsdp", axis=0, tiled=True),
        lax.all_gather(reduce_weight, "fsdp", axis=1, tiled=True),
    )
    gate_pre, gate_narrow = project(ffn_normed, gate_full, pick_gate_down, pick_gate_lift)
    linear_pre, linear_narrow = project(ffn_normed, linear_full, pick_linear_down, pick_linear_lift)
    activated = jax.nn.silu(gate_pre)
    inner_low = (activated * linear_pre).astype(jnp.bfloat16)
    reduce_part, reduce_narrow = project(inner_low, reduce_full, pick_reduce_down, pick_reduce_lift)
    block_out = (
        middle_cols
        + lax.psum_scatter(
            reduce_part.astype(jnp.bfloat16), "tp", scatter_dimension=2, tiled=True
        ).astype(jnp.float32)
    ).astype(jnp.bfloat16)
    cotangent_wide = output_cotangent.astype(jnp.float32)
    inner_grad, grad_reduce_down, grad_reduce_lift = project_back(
        inner_low, output_cotangent, reduce_full, pick_reduce_down, pick_reduce_lift, reduce_narrow
    )
    sigmoid_gate = jax.nn.sigmoid(gate_pre)
    gate_grad = (
        inner_grad * linear_pre * sigmoid_gate * (1.0 + gate_pre * (1.0 - sigmoid_gate))
    ).astype(jnp.bfloat16)
    linear_grad = (inner_grad * activated).astype(jnp.bfloat16)
    gate_input, grad_gate_down, grad_gate_lift = project_back(
        ffn_normed, gate_grad, gate_full, pick_gate_down, pick_gate_lift, gate_narrow
    )
    linear_input, grad_linear_down, grad_linear_lift = project_back(
        ffn_normed, linear_grad, linear_full, pick_linear_down, pick_linear_lift, linear_narrow
    )
    ffn_input_grad = lax.psum((gate_input + linear_input).astype(jnp.bfloat16), "tp").astype(
        jnp.float32
    )
    middle_grad = cotangent_wide + norm_back(middle, feedforward_norm, ffn_input_grad)
    middle_grad_cols = lax.dynamic_slice_in_dim(middle_grad, tensor_index * columns, columns, 2)
    branch_grad = middle_grad.astype(jnp.bfloat16)
    attended_grad, grad_output_down, grad_output_lift = project_back(
        attended_low, branch_grad, output_full, pick_output_down, pick_output_lift, output_narrow
    )
    attended_grad = attended_grad.astype(jnp.bfloat16).reshape(
        seqs_here, local_len, groups_here, group_share, head_dim
    )
    query_grad, key_grad_all, value_grad_all = lax.map(
        partial(attend_back, score_scale=score_scale),
        (query_rot, key_rows, value_rows, allowed, log_total, attended_grad),
    )
    key_return, value_return = (
        shifted(key_grad_all[:, :local_len].astype(jnp.bfloat16), "ctx", -1).astype(jnp.float32),
        shifted(value_grad_all[:, :local_len].astype(jnp.bfloat16), "ctx", -1).astype(jnp.float32),
    )
    key_grad = key_grad_all[:, local_len:] + key_return
    value_grad = value_grad_all[:, local_len:] + value_return
    query_grad = rotate_back(
        query_grad.reshape(seqs_here, local_len, heads_here, head_dim), cosine, sine_table
    )
    query_low = (
        norm_back(query_pre, query_norm, query_grad)
        .astype(jnp.bfloat16)
        .reshape(seqs_here, local_len, heads_here * head_dim)
    )
    key_low = (
        norm_back(key_pre, key_norm, rotate_back(key_grad, cosine, sine_table))
        .astype(jnp.bfloat16)
        .reshape(seqs_here, local_len, groups_here * head_dim)
    )
    value_grad_low = value_grad.astype(jnp.bfloat16).reshape(
        seqs_here, local_len, groups_here * head_dim
    )
    query_input, grad_query_down, grad_query_lift = project_back(
        normed, query_low, query_full, pick_query_down, pick_query_lift, query_narrow
    )
    key_input, grad_key_down, grad_key_lift = project_back(
        normed, key_low, key_full, pick_key_down, pick_key_lift, key_narrow
    )
    value_input, grad_value_down, grad_value_lift = project_back(
        normed, value_grad_low, value_full, pick_value_down, pick_value_lift, value_narrow
    )
    normed_part = query_input + key_input + value_input
    normed_grad = lax.psum(normed_part.astype(jnp.bfloat16), "tp").astype(jnp.float32)
    input_full = norm_back(hidden_wide, attention_norm, normed_grad)
    input_grad = middle_grad_cols + lax.dynamic_slice_in_dim(
        input_full, tensor_index * columns, columns, 2
    )
    full_sums = lax.psum(
        (
            spread(picker, grad_query_down),
            spread(picker, grad_key_down),
            spread(picker, grad_value_down),
            spread(picker, grad_output_lift),
            spread(picker, grad_gate_down),
            spread(picker, grad_linear_down),
            spread(picker, grad_reduce_lift),
        ),
        ("fsdp", "ctx", "tp"),
    )
    part_sums = (
        lax.psum(spread(picker, grad_query_lift).astype(jnp.bfloat16), ("fsdp", "ctx")).astype(
            jnp.float32
        ),
        lax.psum(spread(picker, grad_key_lift).astype(jnp.bfloat16), ("fsdp", "ctx")).astype(
            jnp.float32
        ),
        lax.psum(spread(picker, grad_value_lift).astype(jnp.bfloat16), ("fsdp", "ctx")).astype(
            jnp.float32
        ),
        lax.psum(spread(picker, grad_output_down).astype(jnp.bfloat16), ("fsdp", "ctx")).astype(
            jnp.float32
        ),
        lax.psum(spread(picker, grad_gate_lift).astype(jnp.bfloat16), ("fsdp", "ctx")).astype(
            jnp.float32
        ),
        lax.psum(spread(picker, grad_linear_lift).astype(jnp.bfloat16), ("fsdp", "ctx")).astype(
            jnp.float32
        ),
        lax.psum(spread(picker, grad_reduce_down).astype(jnp.bfloat16), ("fsdp", "ctx")).astype(
            jnp.float32
        ),
    )
    return (
        block_out,
        input_grad,
        full_sums[0],
        part_sums[0],
        full_sums[1],
        part_sums[1],
        full_sums[2],
        part_sums[2],
        part_sums[3],
        full_sums[3],
        full_sums[4],
        part_sums[4],
        full_sums[5],
        part_sums[5],
        part_sums[6],
        full_sums[6],
    )


def solution(mesh):
    in_specs = (
        P("fsdp", "ctx", None),
        P("fsdp", "ctx"),
        P("fsdp"),
        P(),
        P(),
        P(),
        P(),
        P("fsdp", "tp"),
        P("fsdp", "tp"),
        P("fsdp", "tp"),
        P("tp", "fsdp"),
        P("fsdp", "tp"),
        P("fsdp", "tp"),
        P("tp", "fsdp"),
        P(),
        P(None, None, "tp"),
        P(),
        P(None, None, "tp"),
        P(),
        P(None, None, "tp"),
        P(None, "tp", None),
        P(),
        P(),
        P(None, None, "tp"),
        P(),
        P(None, None, "tp"),
        P(None, "tp", None),
        P(),
        P("fsdp", "ctx", None),
    )
    out_specs = (
        P("fsdp", "ctx", "tp"),
        P("fsdp", "ctx", "tp"),
        P(),
        P(None, None, "tp"),
        P(),
        P(None, None, "tp"),
        P(),
        P(None, None, "tp"),
        P(None, "tp", None),
        P(),
        P(),
        P(None, None, "tp"),
        P(),
        P(None, None, "tp"),
        P(None, "tp", None),
        P(),
    )
    return jax.shard_map(
        on_device, mesh=mesh, in_specs=in_specs, out_specs=out_specs, check_vma=False
    )
```

profile of v0, /device:TPU:0, one launch (start us, length us, event | category | flops | bytes accessed | tf_op | source)
XLA Modules:
  0.0 1059.2 jit_solution(1010527670077854420)
XLA Ops:
  17.3 11.4 %all_gather.22 = bf16[2048,128]{1,0:T(8,128)(2,1)S(1)} all-gather(bf16[512,128]{1,0:T(8,128)(2,1)S(1)} %copy-done.90), channel_id=1, replica_groups=mesh['fsdp'=4,'ctx'=2,'tp'=4] {'fsdp'}, dimensions={0}, use_global_device_ids=true | all-gather | bytes 655360 | tf_op jit(solution)/shard_map/all_gather | solution.py:174
  32.1 4.2 collective-permute-start.2
  38.4 7.4 all_gather.21
  61.9 2.9 fusion.135
  67.5 8.6 fusion.134
  76.1 8.1 fusion.3
  84.2 8.9 fusion.28
  93.3 2.9 fusion.136
  96.3 3.9 add_bitcast_fusion
  117.7 2.9 fusion.23
  120.6 135.0 %all-reduce.10.cloned.1.call-done = f32[1,512,2048]{2,1,0:T(8,128)} async-done(((f32[1,512,2048]{2,1,0:T(8,128)}), f32[1,512,2048]{2,1,0:T(8,128)}) %all-reduce.10.cloned.1.call-update) | async-done | bytes 4194320 | tf_op jit(solution)/shard_map/psum | solution.py:264
  255.6 2.8 multiply_reduce_fusion.2
  262.4 52.0 %all-gather.12.cloned.1.call-done = bf16[2048,2048]{1,0:T(8,128)(2,1)} async-done(((bf16[512,2048]{1,0:T(8,128)(2,1)}), bf16[2048,2048]{1,0:T(8,128)(2,1)}) %all-gather.12.cloned.1.call-update) | async-done | bytes 8388624 | tf_op jit(solution)/shard_map/all_gather | solution.py:269
  314.4 7.0 fusion.138
  321.5 4.0 convolution_add_fusion
  325.4 48.8 %all-gather.14.cloned.1.call-done = bf16[2048,2048]{1,0:T(8,128)(2,1)} async-done(((bf16[2048,512]{1,0:T(8,128)(2,1)}), bf16[2048,2048]{1,0:T(8,128)(2,1)}) %all-gather.14.cloned.1.call-update) | async-done | bytes 8388624 | tf_op jit(solution)/shard_map/all_gather | solution.py:270
  374.3 7.6 fusion.25
  381.9 4.1 convolution_add_fusion.2
  386.0 48.1 %all-gather.10.cloned.1.call-done = bf16[2048,2048]{1,0:T(8,128)(2,1)} async-done(((bf16[512,2048]{1,0:T(8,128)(2,1)}), bf16[2048,2048]{1,0:T(8,128)(2,1)}) %all-gather.10.cloned.1.call-update) | async-done | bytes 8388624 | tf_op jit(solution)/shard_map/all_gather | solution.py:268
  434.0 7.0 fusion.137
  441.1 5.6 multiply_convert_fusion.1
  450.0 7.0 fusion.140
  456.9 7.0 fusion.141
  464.0 4.0 fusion.11
  468.5 2.7 fusion.152
  471.2 2.5 fusion.154
  480.1 74.5 %all-reduce.12.cloned.1.call-done = bf16[1,512,2048]{2,1,0:T(8,128)(2,1)} async-done(((bf16[1,512,2048]{2,1,0:T(8,128)(2,1)}), bf16[1,512,2048]{2,1,0:T(8,128)(2,1)}) %all-reduce.12.cloned.1.call-update) | async-done | bytes 2097168 | tf_op jit(solution)/shard_map/psum | solution.py:298
  554.6 3.6 multiply_reduce_fusion.1
  567.5 3.0 fusion.29
  570.5 8.6 fusion
  579.0 10.6 %fusion.2 = bf16[2,4,512,1024]{2,3,1,0:T(8,128)(2,1)} fusion(f32[2,1024,512,4]{2,1,3,0:T(8,128)} %get-tuple-element.127, f32[2,4,512,1024]{2,3,1,0:T(8,128)S(1)} %bitcast.324, f32[2,4,512]{2,1,0:T(4,128)S(1)} %get-tuple-element.126, f32[2,4,512]{2,1,0:T(4,128)S(1)} %bitcast.344), kind=kLoop, calls=%fused_computation.4 | loop fusion | flops 16777216 | bytes 41975808 | tf_op jit(solution)/shard_map/while/body/eval_jaxpr/convert_element_type | solution.py:129
  589.6 6.2 fusion.33
  595.9 2.6 convolution_multiply_fusion
  615.5 3.7 multiply_convert_fusion.5
  619.3 6.9 fusion.139
  626.3 3.2 fusion.10
  631.7 3.0 fusion.142
  639.2 2.6 fusion.12
  643.5 2.5 convert_element_type.312
  646.0 20.5 %all-reduce.18.cloned.1.call-done = (bf16[8,16,128]{2,1,0:T(8,128)(2,1)}, bf16[8,16,128]{2,1,0:T(8,128)(2,1)}) async-done(((bf16[8,16,128]{2,1,0:T(8,128)(2,1)}, bf16[8,16,128]{2,1,0:T(8,128)(2,1)}), (bf16[8,16,128]{2,1,0:T(8,128)(2,1)}, bf16[8,16,128]{2,1,0:T(8,128)(2,1)})) %all-reduce.18.cloned.1.call-update) | async-done | bytes 65552 | tf_op jit(solution)/shard_map/psum | solution.py:367
  669.3 62.9 %all-reduce.20.cloned.1.call-done = (bf16[8,16,512]{2,1,0:T(8,128)(2,1)}, bf16[8,512,16]{1,2,0:T(8,128)(2,1)}, bf16[8,16,2048]{2,1,0:T(8,128)(2,1)}, bf16[8,16,2048]{2,1,0:T(8,128)(2,1)}, bf16[8,2048,16]{1,2,0:T(8,128)(2,1)}) async-done(((bf16[8,16,512]{2,1,0:T(8,128)(2,1)}, bf16[8,512,16]{1,2,0:T(8,128)(2,1)}, bf16[8,16,2048]{2,1,0:T(8,128)(2,1)}, bf16[8,16,2048]{2,1,0:T(8,128)(2,1)}, ...) | async-done | bytes 1835024 | tf_op jit(solution)/shard_map/psum | solution.py:364
  740.1 37.4 %reduce-scatter.2.cloned.1.call-done = bf16[1,512,512]{2,1,0:T(8,128)(2,1)} async-done(((bf16[1,512,2048]{2,1,0:T(8,128)(2,1)}), bf16[1,512,512]{2,1,0:T(8,128)(2,1)}) %reduce-scatter.2.cloned.1.call-update) | async-done | bytes 524304 | tf_op jit(solution)/shard_map/reduce_scatter | solution.py:279
  779.8 86.0 %all-reduce.14.cloned.1.call-done = bf16[1,512,2048]{2,1,0:T(8,128)(2,1)} async-done(((bf16[1,512,2048]{2,1,0:T(8,128)(2,1)}), bf16[1,512,2048]{2,1,0:T(8,128)(2,1)}) %all-reduce.14.cloned.1.call-update) | async-done | bytes 2097168 | tf_op jit(solution)/shard_map/psum | solution.py:346
  865.8 2.3 multiply_reduce_fusion
  868.2 2.8 fusion.36
  871.0 171.3 %all-reduce.16.cloned.1.call-done = (f32[8,2048,16]{1,2,0:T(8,128)}, f32[8,2048,16]{1,2,0:T(8,128)}, f32[8,2048,16]{1,2,0:T(8,128)}, f32[8,16,2048]{2,1,0:T(8,12...) async-done(((f32[8,2048,16]{1,2,0:T(8,128)}, f32[8,2048,16]{1,2,0:T(8,128)}, f32[8,2048,16]{1,2,0:T(8,128)}, f32[8,16,2048]{2,1,0:T(8,128)}, ...) | async-done | bytes 7340048 | tf_op jit(solution)/shard_map/psum | solution.py:351
  1042.3 2.4 copy.148
  1044.7 2.4 copy.149
  (422 shorter events, 117.0 us)
Async XLA Ops:
  7.2 54.7 %all-gather.6.cloned.1.call-start = ((), (), s32[]{:S(2)}) async-start(), calls=%async_computation.1 | async-start | bytes 2621440 | tf_op jit(solution)/shard_map/all_gather | solution.py:173
  7.9 85.4 %all-gather.8.cloned.1.call-start = ((), (), s32[]{:S(2)}) async-start(), calls=%async_computation.2 | async-start | bytes 2621440 | tf_op jit(solution)/shard_map/all_gather | solution.py:176
  13.7 17.7 %copy-start.122 = (f32[64]{0:T(128)}, f32[64]{0:T(128)S(1)}, u32[]{:S(2)}) copy-start(f32[64]{0:T(128)S(1)} %convert_element_type.322) | copy-start | bytes 772
  15.8 46.1 %copy-start.2 = (bf16[512,2048]{1,0:T(8,128)(2,1)}, bf16[512,2048]{1,0:T(8,128)(2,1)S(1)}, u32[]{:S(2)}) copy-start(bf16[512,2048]{1,0:T(8,128)(2,1)S(1)} %fusion.13) | copy-start | bytes 6291460
  15.8 20.5 %copy-start.119 = (s32[1,512]{1,0:T(1,128)S(1)}, s32[1,512]{1,0:T(1,128)}, u32[]{:S(2)}) copy-start(s32[1,512]{1,0:T(1,128)} %param.30) | copy-start | bytes 6148
  15.8 21.8 %copy-start.56 = (bf16[8,2048,16]{1,2,0:T(8,128)(2,1)S(1)}, bf16[8,2048,16]{1,2,0:T(8,128)(2,1)}, u32[]{:S(2)}) copy-start(bf16[8,2048,16]{1,2,0:T(8,128)(2,1)} %param.47) | copy-start | bytes 1572868
  30.3 18.9 %copy-start.19 = (f32[512,128]{0,1:T(8,128)}, f32[512,128]{0,1:T(8,128)S(1)}, u32[]{:S(2)}) copy-start(f32[512,128]{0,1:T(8,128)S(1)} %convolution_add_fusion.5) | copy-start | bytes 786436
  31.3 36.0 %copy-start.38 = (f32[512,32]{0,1:T(8,128)}, f32[512,32]{0,1:T(8,128)S(1)}, u32[]{:S(2)}) copy-start(f32[512,32]{0,1:T(8,128)S(1)} %get-tuple-element.104) | copy-start | bytes 196612
  31.3 36.0 %copy-start.40 = (f32[512,32]{0,1:T(8,128)}, f32[512,32]{0,1:T(8,128)S(1)}, u32[]{:S(2)}) copy-start(f32[512,32]{0,1:T(8,128)S(1)} %get-tuple-element.105) | copy-start | bytes 196612
  32.1 35.4 %collective-permute-start.2 = (bf16[1,512,2,64]{1,3,2,0:T(8,128)(2,1)}, bf16[1,512,2,64]{1,3,2,0:T(8,128)(2,1)}, u32[]{:S(2)}, u32[]{:S(2)}) collective-permute-start(bf16[1,512,2,64]{1,3,2,0:T(8,128)(2,1)} %pad_maximum_fusion.5), channel_id=1, source_target_pairs={{0,4},{1,5},{2,6},{3,7},{8,12},{9,13},{10,14},{11,15},{16,20},{17,... | collective-permute-start | bytes 393224 | tf_op jit(solution)/shard_map/ppermute | solution.py:16
  36.3 24.3 %collective-permute-start.1 = (bf16[1,512]{1,0:T(2,128)(2,1)S(1)}, bf16[1,512]{1,0:T(2,128)(2,1)S(1)}, u32[]{:S(2)}, u32[]{:S(2)}) collective-permute-start(bf16[1,512]{1,0:T(2,128)(2,1)S(1)} %convert_element_type.318), channel_id=1, source_target_pairs={{0,4},{1,5},{2,6},{3,7},{8,12},{9,13},{10,14},{11,15},{16,20},{17,... | collective-permute-start | bytes 3080 | tf_op jit(solution)/shard_map/ppermute | solution.py:16
  38.4 14.6 %copy-start.27 = (bf16[1,2048,16]{2,1,0:T(8,128)(2,1)}, bf16[1,2048,16]{2,1,0:T(8,128)(2,1)S(1)}, u32[]{:S(2)}) copy-start(bf16[1,2048,16]{2,1,0:T(8,128)(2,1)S(1)} %copy.50) | copy-start | bytes 196612
  49.2 35.0 %collective-permute-start = (bf16[1,512,2,64]{1,3,2,0:T(8,128)(2,1)}, bf16[1,512,2,64]{1,3,2,0:T(8,128)(2,1)}, u32[]{:S(2)}, u32[]{:S(2)}) collective-permute-start(bf16[1,512,2,64]{1,3,2,0:T(8,128)(2,1)} %bitcast.7), channel_id=1, source_target_pairs={{0,4},{1,5},{2,6},{3,7},{8,12},{9,13},{10,14},{11,15},{16,20},{17,... | collective-permute-start | bytes 393224 | tf_op jit(solution)/shard_map/ppermute | solution.py:16
  51.1 204.4 %all-reduce.10.cloned.1.call-start = ((), (), s32[]{:S(2)}) async-start(), calls=%async_computation.3 | async-start | bytes 8388608 | tf_op jit(solution)/shard_map/psum | solution.py:264
  53.0 11.8 %copy-start.29 = (bf16[1,2048,16]{2,1,0:T(8,128)(2,1)}, bf16[1,2048,16]{2,1,0:T(8,128)(2,1)S(1)}, u32[]{:S(2)}) copy-start(bf16[1,2048,16]{2,1,0:T(8,128)(2,1)S(1)} %copy.58) | copy-start | bytes 196612
  84.2 8.9 copy-start.106
  100.2 214.2 %all-gather.12.cloned.1.call-start = ((), (), s32[]{:S(2)}) async-start(), calls=%async_computation.5 | async-start | bytes 10485760 | tf_op jit(solution)/shard_map/all_gather | solution.py:269
  100.8 273.4 %all-gather.14.cloned.1.call-start = ((), (), s32[]{:S(2)}) async-start(), calls=%async_computation.6 | async-start | bytes 10485760 | tf_op jit(solution)/shard_map/all_gather | solution.py:270
  101.4 332.6 %all-gather.10.cloned.1.call-start = ((), (), s32[]{:S(2)}) async-start(), calls=%async_computation.4 | async-start | bytes 10485760 | tf_op jit(solution)/shard_map/all_gather | solution.py:268
  102.0 153.6 %copy-start.7 = (bf16[1,512,2048]{2,1,0:T(8,128)(2,1)S(1)}, bf16[1,512,2048]{2,1,0:T(8,128)(2,1)}, u32[]{:S(2)}) copy-start(bf16[1,512,2048]{2,1,0:T(8,128)(2,1)} %param.29) | copy-start | bytes 6291460
  102.0 452.5 %all-reduce.12.cloned.1.call-start = ((), (), s32[]{:S(2)}) async-start(), calls=%async_computation.8 | async-start | bytes 4194304 | tf_op jit(solution)/shard_map/psum | solution.py:298
  102.1 156.9 %copy-start.95 = (f32[2048]{0:T(1024)}, f32[2048]{0:T(1024)S(1)}, u32[]{:S(2)}) copy-start(f32[2048]{0:T(1024)S(1)} %convert_element_type.334) | copy-start | bytes 24580
  446.7 10.2 copy-start.16
  468.0 198.5 %all-reduce.18.cloned.1.call-start = ((), (), s32[]{:S(2)}) async-start(), calls=%async_computation.11 | async-start | bytes 131072 | tf_op jit(solution)/shard_map/psum | solution.py:367
  475.3 79.2 %copy-start.96 = (f32[2048]{0:T(1024)S(1)}, f32[2048]{0:T(1024)}, u32[]{:S(2)}) copy-start(f32[2048]{0:T(1024)} %copy-done.95) | copy-start | bytes 24580
  479.1 79.1 %copy-start.75 = (f32[512,16]{0,1:T(8,128)}, f32[512,16]{0,1:T(8,128)S(1)}, u32[]{:S(2)}) copy-start(f32[512,16]{0,1:T(8,128)S(1)} %fusion.71) | copy-start | bytes 98308
  479.1 79.1 %copy-start.13 = (bf16[1,512,2048]{2,1,0:T(8,128)(2,1)S(1)}, bf16[1,512,2048]{2,1,0:T(8,128)(2,1)}, u32[]{:S(2)}) copy-start(bf16[1,512,2048]{2,1,0:T(8,128)(2,1)} %param.57) | copy-start | bytes 6291460
  479.1 79.1 %copy-start.114 = (f32[512]{0:T(512)S(1)}, f32[512]{0:T(512)}, u32[]{:S(2)}) copy-start(f32[512]{0:T(512)} %copy-done.113) | copy-start | bytes 6148
  479.1 79.1 %copy-start.120 = (f32[512]{0:T(512)S(1)}, f32[512]{0:T(512)}, u32[]{:S(2)}) copy-start(f32[512]{0:T(512)} %get-tuple-element.108) | copy-start | bytes 6148
  579.0 10.6 %copy-start.48 = (bf16[1,512,8,32]{1,3,2,0:T(8,128)(2,1)S(1)}, bf16[1,512,8,32]{1,3,2,0:T(8,128)(2,1)}, u32[]{:S(2)}) copy-start(bf16[1,512,8,32]{1,3,2,0:T(8,128)(2,1)} %copy-done.47) | copy-start | bytes 786436
  579.0 10.6 %copy-start.50 = (bf16[1,512,8,32]{1,3,2,0:T(8,128)(2,1)S(1)}, bf16[1,512,8,32]{1,3,2,0:T(8,128)(2,1)}, u32[]{:S(2)}) copy-start(bf16[1,512,8,32]{1,3,2,0:T(8,128)(2,1)} %copy-done.49) | copy-start | bytes 786436
  600.7 9.5 copy-start.20
  600.7 9.5 copy-start.123
  600.7 9.7 copy-start.109
  600.7 9.7 copy-start.115
  600.7 9.7 copy-start.126
  601.7 9.0 copy-start.83
  601.7 10.2 copy-start.100
  601.7 10.3 copy-start.85
  601.7 8.4 collective-permute-start.3
  603.2 8.6 collective-permute-start.4
  615.4 116.8 %all-reduce.20.cloned.1.call-start = ((), (), s32[]{:S(2)}) async-start(), calls=%async_computation.12 | async-start | bytes 3670016 | tf_op jit(solution)/shard_map/psum | solution.py:364
  619.3 158.2 %reduce-scatter.2.cloned.1.call-start = ((), (), s32[]{:S(2)}) async-start(), calls=%async_computation.7 | async-start | bytes 2621440 | tf_op jit(solution)/shard_map/reduce_scatter | solution.py:279
  629.5 236.2 %all-reduce.14.cloned.1.call-start = ((), (), s32[]{:S(2)}) async-start(), calls=%async_computation.9 | async-start | bytes 4194304 | tf_op jit(solution)/shard_map/psum | solution.py:346
  641.9 400.4 %all-reduce.16.cloned.1.call-start = ((), (), s32[]{:S(2)}) async-start(), calls=%async_computation.10 | async-start | bytes 14680064 | tf_op jit(solution)/shard_map/psum | solution.py:351
  646.0 219.8 %copy-start.102 = (f32[2048]{0:T(1024)S(1)}, f32[2048]{0:T(1024)}, u32[]{:S(2)}) copy-start(f32[2048]{0:T(1024)} %copy-done.101) | copy-start | bytes 24580
  779.8 88.4 %copy-start.112 = (f32[512]{0:T(512)S(1)}, f32[512]{0:T(512)}, u32[]{:S(2)}) copy-start(f32[512]{0:T(512)} %copy-done.111) | copy-start | bytes 6148
  779.8 88.4 %copy-start.117 = (f32[512]{0:T(512)S(1)}, f32[512]{0:T(512)}, u32[]{:S(2)}) copy-start(f32[512]{0:T(512)} %get-tuple-element.106) | copy-start | bytes 6148
  (101 other events, 442.3 us)
Sparse Core Ops, SparseCore 0:
  9.6 28.0 all-gather.5
  51.3 22.8 all-gather.7
  100.3 155.2 all-reduce.9
  257.1 57.2 all-gather.11
  315.9 58.3 all-gather.13
  375.8 58.2 all-gather.9
  468.1 86.3 all-reduce.11
  615.5 50.8 all-reduce.17
  671.4 60.7 all-reduce.19
  734.3 43.0 reduce-scatter.1
  779.9 85.8 all-reduce.13
  873.2 169.0 all-reduce.15
where the time goes:
time: 1070 us; the launch traced here: 1060 us
  waiting for transfers between devices  743 us (69%)
  matrix products  176 us (16%)
  other arithmetic  69.3 us (6%)
  local copies, waits for them, and re-layouts  24.2 us (2%)
  blocking collectives  18.8 us (2%)
  between operations  17 us (2%)
  starting transfers between devices  11.2 us (1%)
    psum x1, waiting for transfers between devices, on_device(): lax.psum((spread(picker, grad_query_down), spread(picker, grad_key_down),...  171 us
    psum x1, waiting for transfers between devices, on_device(): middle = hidden_wide + lax.psum(branch_part, 'tp')  135 us
    psum x1, waiting for transfers between devices, on_device(): lax.psum(normed_part.astype(jnp.bfloat16), 'tp').astype(jnp.float32)  86 us
    psum x1, waiting for transfers between devices, on_device(): lax.psum((gate_input + linear_input).astype(jnp.bfloat16), 'tp')  74.5 us
    psum x1, waiting for transfers between devices, on_device(): lax.psum(spread(picker, grad_query_lift).astype(jnp.bfloat16), ('fsdp', '...  62.9 us
    all_gather x1, waiting for transfers between devices, on_device(): lax.all_gather(linear_weight, 'fsdp', axis=0, tiled=True)  52 us
    all_gather x1, waiting for transfers between devices, on_device(): lax.all_gather(reduce_weight, 'fsdp', axis=1, tiled=True)  48.8 us
    all_gather x1, waiting for transfers between devices, on_device(): lax.all_gather(gate_weight, 'fsdp', axis=0, tiled=True)  48.1 us
  transfers between devices with their start and end apart: 17, of which 12 were waited for; matrix products, arithmetic and copies ran while one was open for 16% of the time, Pallas kernels for 0%

commit v1 on v0

v1 whole, which is shorter than its diff:
```python
from functools import partial

import jax
import jax.numpy as jnp
from jax import lax
from jax.experimental import pallas as pl
from jax.experimental.pallas import tpu as pltpu
from jax.sharding import PartitionSpec as P

epsilon = 1e-05
rope_base = 1000000.0
masked = -1e30
f32 = jnp.float32
bf16 = jnp.bfloat16
lanes = 128
half = 64
rank = 16
vmem_bytes = 58 * 1024 * 1024


def nn(left, right):
    return lax.dot_general(left, right, (((1,), (0,)), ((), ())), preferred_element_type=f32)


def nt(left, right):
    return lax.dot_general(left, right, (((1,), (1,)), ((), ())), preferred_element_type=f32)


def at(ref, index):
    return pl.multiple_of(ref[index], lanes)


def fixed(shape):
    return pl.BlockSpec(shape, lambda *_: (0,) * len(shape), pipeline_mode=pl.Buffered(1))


def result(shape, dtype):
    return jax.ShapeDtypeStruct(shape, dtype)


def lane_of(shape):
    return lax.broadcasted_iota(jnp.int32, shape, len(shape) - 1)


def head_mean_matrix():
    row = lax.broadcasted_iota(jnp.int32, (lanes, lanes), 0)
    col = lax.broadcasted_iota(jnp.int32, (lanes, lanes), 1)
    return jnp.where((row // half) == (col // half), 1.0 / half, 0.0).astype(bf16)


def head_mean(values, matrix):
    high = values.astype(bf16)
    low = (values - high.astype(f32)).astype(bf16)
    return nn(high, matrix) + nn(low, matrix)


def partner(values):
    first = (lane_of(values.shape) % half) < (half // 2)
    return jnp.where(
        first,
        pltpu.roll(values, lanes - half // 2, values.ndim - 1),
        pltpu.roll(values, half // 2, values.ndim - 1),
    )


def swap_halves(values):
    return pltpu.roll(values, half, values.ndim - 1)


def qkv_kernel(
    meta, hid, gain, q0, q1, q2, q3, kv0, kv1, kv2, kv3, aq, ak, av, bq, bk, bv, qg, kg, cos, sin,
    seg, normed, narrow, pre, qrot, kv, a_all, b_all,
):
    q_width, kv_width = bq.shape[2], bk.shape[2]

    @pl.when(pl.program_id(0) == 0)
    def _():
        a_all[...] = jnp.zeros_like(a_all)
        b_all[...] = jnp.zeros_like(b_all)
        a_all[0:rank, :] = aq[0]
        a_all[rank : 2 * rank, :] = ak[0]
        a_all[2 * rank : 3 * rank, :] = av[0]
        b_all[0:rank, 0:q_width] = bq[0]
        b_all[rank : 2 * rank, q_width : q_width + kv_width] = bk[0]
        b_all[2 * rank : 3 * rank, q_width + kv_width :] = bv[0]

    wide = hid[...].astype(f32)
    inverse = lax.rsqrt(jnp.mean(wide * wide, axis=-1, keepdims=True) + epsilon)
    normed[...] = (wide * inverse * gain[...].astype(f32)).astype(bf16)
    low = nt(normed[...], a_all[...]).astype(bf16)
    narrow[...] = low
    total = nn(low, b_all[...])
    q_total, kv_total = total[:, :q_width], total[:, q_width:]
    for index, (q_weight, kv_weight) in enumerate(((q0, kv0), (q1, kv1), (q2, kv2), (q3, kv3))):
        part = normed[:, pl.ds(at(meta, index), q_weight.shape[0])]
        q_total = q_total + nn(part, q_weight[...])
        kv_total = kv_total + nn(part, kv_weight[...])
    total = jnp.concatenate([q_total, kv_total], axis=1)
    pre[...] = total[:, : q_width + kv_width]
    matrix = head_mean_matrix()
    for start in range(0, q_width + kv_width, lanes):
        part = total[:, start : start + lanes]
        head_gain = qg if start < q_width else kg
        scaled = part * lax.rsqrt(head_mean(part * part, matrix) + epsilon) * head_gain[...]
        turned = (scaled * cos[...] + partner(scaled) * sin[...]).astype(bf16)
        if start < q_width:
            qrot[:, start : start + lanes] = turned
        else:
            kv[:, start - q_width : start - q_width + lanes] = turned
    kv[:, kv_width : 2 * kv_width] = total[:, q_width + kv_width :].astype(bf16)
    kv[:, 2 * kv_width :] = jnp.broadcast_to(seg[...].astype(f32), (seg.shape[0], lanes)).astype(bf16)


def qkv_forward(meta, hid, gain, weights, downs, lifts, q_gain, k_gain, cos, sin, seg):
    length, width = hid.shape
    q_width, kv_width = lifts[0].shape[2], lifts[1].shape[2]
    block = 256
    tile = lambda w: pl.BlockSpec((block, w), lambda i, m: (i, 0))
    pick = lambda a: pl.BlockSpec(
        (1,) + a.shape[1:], lambda i, m: (m[7], 0, 0), pipeline_mode=pl.Buffered(1)
    )
    return pl.pallas_call(
        qkv_kernel,
        name="qkv_forward",
        grid_spec=pltpu.PrefetchScalarGridSpec(
            num_scalar_prefetch=1,
            grid=(length // block,),
            in_specs=[tile(width), fixed(gain.shape)]
            + [fixed(w.shape) for w in weights]
            + [pick(a) for a in downs]
            + [pick(a) for a in lifts]
            + [fixed(q_gain.shape), fixed(k_gain.shape), tile(lanes), tile(lanes), tile(1)],
            out_specs=[
                tile(width), tile(lanes), tile(q_width + kv_width), tile(q_width),
                tile(2 * kv_width + lanes),
            ],
            scratch_shapes=[
                pltpu.VMEM((lanes, width), bf16),
                pltpu.VMEM((lanes, q_width + 2 * kv_width), bf16),
            ],
        ),
        out_shape=[
            result((length, width), bf16),
            result((length, lanes), bf16),
            result((length, q_width + kv_width), f32),
            result((length, q_width), bf16),
            result((length, 2 * kv_width + lanes), bf16),
        ],
        cost_estimate=pl.CostEstimate(flops=1024, transcendentals=0, bytes_accessed=1024),
        compiler_params=pltpu.CompilerParams(vmem_limit_bytes=vmem_bytes),
    )(meta, hid, gain, *weights, *downs, *lifts, q_gain, k_gain, cos, sin, seg)


def spread_keys(kv, kd, v0, v1, rows, size):
    lane = lane_of((size, lanes))
    key = kv[:, 0:lanes].astype(f32)
    other = swap_halves(key)
    kd[0, rows : rows + size, :] = jnp.where(lane < half, key, other).astype(bf16)
    kd[1, rows : rows + size, :] = jnp.where(lane < half, other, key).astype(bf16)
    value = kv[:, lanes : 2 * lanes].astype(f32)
    other = swap_halves(value)
    v0[0, rows : rows + size, :] = jnp.where(lane < half, value, 1.0).astype(bf16)
    v0[1, rows : rows + size, :] = jnp.where(lane < half, other, 1.0).astype(bf16)
    v1[0, rows : rows + size, :] = jnp.where(lane < half, 1.0, other).astype(bf16)
    v1[1, rows : rows + size, :] = jnp.where(lane < half, 1.0, value).astype(bf16)


def attention_kernel(
    meta, qrot, kvf, kvn, kvq, att, wide, inv, kd, v0, v1, bias, segk, *, log_scale, block,
):
    far = kvf.shape[0]
    pairs = qrot.shape[1] // lanes
    share = pairs // 2
    step = pl.program_id(0)

    @pl.when(step == 0)
    def _():
        spread_keys(kvf, kd, v0, v1, 0, far)
        spread_keys(kvn, kd, v0, v1, far, kvn.shape[0])
        away = kvf[:, 2 * lanes :].astype(f32).T[0:8]
        segk[:, 0:far] = jnp.where(meta[5] > 0, away, -1.0)
        segk[:, far:] = kvn[:, 2 * lanes :].astype(f32).T[0:8]

    def queries(number):
        keys = far + (number + 1) * block
        key = lax.broadcasted_iota(jnp.int32, (block, keys), 1)
        query = lax.broadcasted_iota(jnp.int32, (block, keys), 0) + (far + number * block)
        segq = kvq[:, 2 * lanes :].astype(f32)[:, 0:1]
        allowed = (segq == segk[0:1, 0:keys]) & (key <= query)
        bias[:, 0:keys] = jnp.where(allowed, 0.0, masked)
        lane = lane_of((block, lanes))

        def body(pair, carry):
            group = pair // share
            place = pl.ds(pl.multiple_of(pair * lanes, lanes), lanes)
            q = qrot[:, place].astype(f32)
            q0 = jnp.where(lane < half, q, 0.0).astype(bf16)
            q1 = jnp.where(lane < half, 0.0, q).astype(bf16)
            k = kd[group, 0:keys, :]
            e0 = jnp.exp2(nt(q0, k) * log_scale + bias[:, 0:keys]).astype(bf16)
            r0 = nn(e0, v0[group, 0:keys, :])
            e1 = jnp.exp2(nt(q1, k) * log_scale + bias[:, 0:keys]).astype(bf16)
            r1 = nn(e1, v1[group, 0:keys, :])
            inverse = 1.0 / jnp.where(lane < half, swap_halves(r0), swap_halves(r1))
            out = jnp.where(lane < half, r0, r1) * inverse
            wide[:, place] = out
            inv[:, place] = inverse
            att[:, place] = out.astype(bf16)
            return carry

        lax.fori_loop(0, pairs, body, 0)

    for number in range(kvn.shape[0] // block):
        pl.when(step == number)(partial(queries, number))


def attention_forward(meta, qrot, kvf, kvn, log_scale):
    length, q_width = qrot.shape
    block = 256
    keys = kvf.shape[0] + length
    tile = lambda w: pl.BlockSpec((block, w), lambda i, m: (i, 0))
    return pl.pallas_call(
        partial(attention_kernel, log_scale=log_scale, block=block),
        name="attention_forward",
        grid_spec=pltpu.PrefetchScalarGridSpec(
            num_scalar_prefetch=1,
            grid=(length // block,),
            in_specs=[tile(q_width), fixed(kvf.shape), fixed(kvn.shape), tile(kvn.shape[1])],
            out_specs=[tile(q_width), tile(q_width), tile(q_width)],
            scratch_shapes=[
                pltpu.VMEM((2, keys, lanes), bf16),
                pltpu.VMEM((2, keys, lanes), bf16),
                pltpu.VMEM((2, keys, lanes), bf16),
                pltpu.VMEM((block, keys), f32),
                pltpu.VMEM((8, keys), f32),
            ],
        ),
        out_shape=[
            result((length, q_width), bf16),
            result((length, q_width), f32),
            result((length, q_width), f32),
        ],
        cost_estimate=pl.CostEstimate(flops=1024, transcendentals=0, bytes_accessed=1024),
        compiler_params=pltpu.CompilerParams(vmem_limit_bytes=vmem_bytes),
    )(meta, qrot, kvf, kvn, kvn)


def output_kernel(meta, att, w0, w1, w2, w3, ao, bo, branch, narrow, a_all, b_all):
    @pl.when(pl.program_id(0) == 0)
    def _():
        a_all[...] = jnp.zeros_like(a_all)
        b_all[...] = jnp.zeros_like(b_all)
        a_all[0:rank, :] = ao[0]
        b_all[0:rank, :] = bo[0]

    own = att[...]
    low = nt(own, a_all[...]).astype(bf16)
    narrow[...] = low
    for index, weight in enumerate((w0, w1, w2, w3)):
        columns = pl.ds(at(meta, index), weight.shape[1])
        branch[:, columns] = (nn(own, weight[...]) + nn(low, b_all[:, columns])).astype(bf16)


def output_forward(meta, att, weights, down, lift):
    length, q_width = att.shape
    model = lift.shape[2]
    block = 256
    tile = lambda w: pl.BlockSpec((block, w), lambda i, m: (i, 0))
    pick = lambda a: pl.BlockSpec(
        (1,) + a.shape[1:], lambda i, m: (m[7], 0, 0), pipeline_mode=pl.Buffered(1)
    )
    return pl.pallas_call(
        output_kernel,
        name="output_forward",
        grid_spec=pltpu.PrefetchScalarGridSpec(
            num_scalar_prefetch=1,
            grid=(length // block,),
            in_specs=[tile(q_width)] + [fixed(w.shape) for w in weights] + [pick(down), pick(lift)],
            out_specs=[tile(model), tile(lanes)],
            scratch_shapes=[pltpu.VMEM((lanes, q_width), bf16), pltpu.VMEM((lanes, model), bf16)],
        ),
        out_shape=[result((length, model), bf16), result((length, lanes), bf16)],
        cost_estimate=pl.CostEstimate(flops=1024, transcendentals=0, bytes_accessed=1024),
        compiler_params=pltpu.CompilerParams(vmem_limit_bytes=vmem_bytes),
    )(meta, att, *weights, down, lift)


def picked(array):
    return pl.BlockSpec(
        (1,) + array.shape[1:], lambda i, m: (m[7], 0, 0), pipeline_mode=pl.Buffered(1)
    )


def strip(array, width):
    return pl.BlockSpec((1, rank, width), lambda j, m: (m[7], 0, j))


def params():
    return pltpu.CompilerParams(vmem_limit_bytes=vmem_bytes)


def ffn_kernel(meta, hid, branch, cot, gain, *refs, shards, chunk):
    gates, linears, reduces = (refs[i:j] for i, j in zip((0,) + shards[:-1], shards))
    refs = refs[shards[-1] :]
    ag, al, ar, bg, bl, br = refs[:6]
    back, inner_out, gate_out, linear_out, n_gl_t, m_gl_t, m_r_t = refs[6:13]
    x, grad_sum, n_gl, m_gl, m_r, a_gl, b_r, b_g, b_l, a_r = refs[13:]
    step = pl.program_id(0)
    length = hid.shape[0]
    count = length // chunk

    def rows_of(index):
        return pl.ds(pl.multiple_of(index * chunk, chunk), chunk)

    def chunks(body):
        def run(index, carry):
            body(rows_of(index))
            return carry

        lax.fori_loop(0, count, run, 0)

    def normal(rows):
        middle = hid[rows, :].astype(f32) + branch[rows, :].astype(f32)
        inverse = lax.rsqrt(jnp.mean(middle * middle, axis=-1, keepdims=True) + epsilon)
        return middle, inverse

    @pl.when(step == 0)
    def _():
        for ref in (a_gl, b_r, b_g, b_l, a_r):
            ref[...] = jnp.zeros_like(ref)
        a_gl[0:rank, :] = ag[0]
        a_gl[rank : 2 * rank, :] = al[0]
        b_r[0:rank, :] = br[0]

        def body(rows):
            back_low = nt(cot[rows, :], b_r[...])
            m_r[rows, :] = back_low.astype(bf16)
            m_r_t[:, rows] = back_low.T[0:rank].astype(bf16)
            middle, inverse = normal(rows)
            x[rows, :] = (middle * inverse * gain[...].astype(f32)).astype(bf16)
            low = nt(x[rows, :], a_gl[...])
            n_gl[rows, :] = low.astype(bf16)
            n_gl_t[:, rows] = low.T[0 : 2 * rank].astype(bf16)
            m_gl[rows, :] = jnp.zeros((chunk, lanes), f32)

        chunks(body)

    b_g[0:rank, :] = bg[0]
    b_l[rank : 2 * rank, :] = bl[0]
    a_r[0:rank, :] = ar[0]

    def place(index, weight, axis):
        return pl.ds(at(meta, index), weight.shape[axis])

    def body(rows, first):
        low = n_gl[rows, :]
        gate = nn(low, b_g[...])
        linear = nn(low, b_l[...])
        for index, weight in enumerate(gates):
            gate = gate + nn(x[rows, place(8 + index, weight, 0)], weight[...])
        for index, weight in enumerate(linears):
            linear = linear + nn(x[rows, place(index, weight, 0)], weight[...])
        upstream = nn(m_r[rows, :], a_r[...])
        for index, weight in enumerate(reduces):
            upstream = upstream + nt(cot[rows, place(index, weight, 1)], weight[...])
        sigmoid = jax.nn.sigmoid(gate)
        active = gate * sigmoid
        gate_grad = (upstream * linear * sigmoid * (1.0 + gate * (1.0 - sigmoid))).astype(bf16)
        linear_grad = (upstream * active).astype(bf16)
        inner_out[rows, :] = (active * linear).astype(bf16)
        gate_out[rows, :] = gate_grad
        linear_out[rows, :] = linear_grad
        m_gl[rows, :] += nt(gate_grad, b_g[...]) + nt(linear_grad, b_l[...])
        for index, weight in enumerate(linears):
            columns = place(index, weight, 0)
            backward = nt(linear_grad, weight[...])
            if first:
                grad_sum[rows, columns] = backward
            else:
                grad_sum[rows, columns] += backward
        for index, weight in enumerate(gates):
            grad_sum[rows, place(8 + index, weight, 0)] += nt(gate_grad, weight[...])

    pl.when(step == 0)(partial(chunks, partial(body, first=True)))
    pl.when(step > 0)(partial(chunks, partial(body, first=False)))

    @pl.when(step == pl.num_programs(0) - 1)
    def _():
        def finish(rows):
            upstream = grad_sum[rows, :] + nn(m_gl[rows, :].astype(bf16), a_gl[...])
            middle, inverse = normal(rows)
            weighted = upstream * gain[...].astype(f32)
            mean = jnp.mean(weighted * middle, axis=-1, keepdims=True)
            back[rows, :] = (
                inverse * weighted - middle * (inverse * inverse * inverse * mean)
            ).astype(bf16)

        chunks(finish)
        m_gl_t[...] = m_gl[...].T[0 : 2 * rank].astype(bf16)


def ffn(
    meta, hid, branch, cot, gain, gates, linears, reduces, downs, lifts, width=512, chunk=512
):
    length, model = hid.shape
    hidden = gates[0].shape[1]
    rows = [*gates, *linears]
    shards = (len(gates), len(rows), len(rows) + len(reduces))
    column = lambda: pl.BlockSpec((length, width), lambda j, m: (0, j))
    return pl.pallas_call(
        partial(ffn_kernel, shards=shards, chunk=chunk),
        name="feed_forward",
        grid_spec=pltpu.PrefetchScalarGridSpec(
            num_scalar_prefetch=1,
            grid=(hidden // width,),
            in_specs=[fixed(hid.shape), fixed(branch.shape), fixed(cot.shape), fixed(gain.shape)]
            + [pl.BlockSpec((w.shape[0], width), lambda j, m: (0, j)) for w in rows]
            + [pl.BlockSpec((width, w.shape[1]), lambda j, m: (j, 0)) for w in reduces]
            + [picked(downs[0]), picked(downs[1]), strip(downs[2], width)]
            + [strip(lifts[0], width), strip(lifts[1], width), picked(lifts[2])],
            out_specs=[
                fixed((length, model)), column(), column(), column(),
                fixed((2 * rank, length)), fixed((2 * rank, length)), fixed((rank, length)),
            ],
            scratch_shapes=[
                pltpu.VMEM((length, model), bf16),
                pltpu.VMEM((length, model), f32),
                pltpu.VMEM((length, lanes), bf16),
                pltpu.VMEM((length, lanes), f32),
                pltpu.VMEM((length, lanes), bf16),
                pltpu.VMEM((lanes, model), bf16),
                pltpu.VMEM((lanes, model), bf16),
                pltpu.VMEM((lanes, width), bf16),
                pltpu.VMEM((lanes, width), bf16),
                pltpu.VMEM((lanes, width), bf16),
            ],
        ),
        out_shape=[result((length, model), bf16)]
        + [result((length, hidden), bf16)] * 3
        + [result((2 * rank, length), bf16)] * 2
        + [result((rank, length), bf16)],
        cost_estimate=pl.CostEstimate(
            flops=8 * length * model * hidden, transcendentals=length * hidden,
            bytes_accessed=4 * model * hidden + 14 * length * model,
        ),
        compiler_params=params(),
    )(meta, hid, branch, cot, gain, *rows, *reduces, *downs, *lifts)


def ffn_adapter_kernel(
    meta, hid, branch, cot, gain, inner, gate_grad, linear_grad, n_gl_t, m_gl_t, m_r_t, ar,
    part_pack, full_pack, n_r, low_sum, a_r,
):
    step = pl.program_id(0)

    @pl.when(step == 0)
    def _():
        a_r[...] = jnp.zeros_like(a_r)
        low_sum[...] = jnp.zeros_like(low_sum)

    a_r[0:rank, :] = ar[0]
    part_pack[0:rank, :] = nn(n_gl_t[...], gate_grad[...])[0:rank].astype(bf16)
    part_pack[rank : 2 * rank, :] = nn(n_gl_t[...], linear_grad[...])[rank:].astype(bf16)
    part_pack[2 * rank :, :] = nn(m_r_t[...], inner[...]).astype(bf16)
    low_sum[...] += nt(inner[...], a_r[...])

    @pl.when(step == pl.num_programs(0) - 1)
    def _():
        low = low_sum[...]
        n_r[...] = low.astype(bf16)
        full_pack[2 * rank :, :] = nn(low.T[0:rank].astype(bf16), cot[...]).astype(bf16)
        middle = hid[...].astype(f32) + branch[...].astype(f32)
        inverse = lax.rsqrt(jnp.mean(middle * middle, axis=-1, keepdims=True) + epsilon)
        x = (middle * inverse * gain[...].astype(f32)).astype(bf16)
        full_pack[0 : 2 * rank, :] = nn(m_gl_t[...], x).astype(bf16)


def ffn_adapters(meta, hid, branch, cot, gain, inner, gate_grad, linear_grad, n_gl_t, m_gl_t, m_r_t, down):
    length, model = hid.shape
    hidden = inner.shape[1]
    width = 512
    column = lambda: pl.BlockSpec((length, width), lambda j, m: (0, j))
    return pl.pallas_call(
        ffn_adapter_kernel,
        name="feed_forward_adapters",
        grid_spec=pltpu.PrefetchScalarGridSpec(
            num_scalar_prefetch=1,
            grid=(hidden // width,),
            in_specs=[fixed(hid.shape), fixed(branch.shape), fixed(cot.shape), fixed(gain.shape)]
            + [column(), column(), column()]
            + [fixed(n_gl_t.shape), fixed(m_gl_t.shape), fixed(m_r_t.shape), strip(down, width)],
            out_specs=[
                pl.BlockSpec((3 * rank, width), lambda j, m: (0, j)),
                fixed((3 * rank, model)),
                fixed((length, lanes)),
            ],
            scratch_shapes=[pltpu.VMEM((length, lanes), f32), pltpu.VMEM((lanes, width), bf16)],
        ),
        out_shape=[
            result((3 * rank, hidden), bf16),
            result((3 * rank, model), bf16),
            result((length, lanes), bf16),
        ],
        cost_estimate=pl.CostEstimate(
            flops=512 * length * hidden, transcendentals=0, bytes_accessed=12 * length * model
        ),
        compiler_params=params(),
    )(meta, hid, branch, cot, gain, inner, gate_grad, linear_grad, n_gl_t, m_gl_t, m_r_t, down)


def reduce_kernel(meta, inner, n_r, *refs):
    *weights, br, out, b_r = refs
    b_r[...] = jnp.zeros_like(b_r)
    b_r[0:rank, :] = br[0]
    for index, weight in enumerate(weights):
        columns = pl.ds(at(meta, index), weight.shape[1])
        out[:, columns] = (nn(inner[...], weight[...]) + nn(n_r[...], b_r[:, columns])).astype(bf16)


def reduce_forward(meta, inner, n_r, reduces, lift):
    length = inner.shape[0]
    model = lift.shape[2]
    return pl.pallas_call(
        reduce_kernel,
        name="reduce_forward",
        grid_spec=pltpu.PrefetchScalarGridSpec(
            num_scalar_prefetch=1,
            grid=(1,),
            in_specs=[fixed(inner.shape), fixed(n_r.shape)]
            + [fixed(w.shape) for w in reduces]
            + [picked(lift)],
            out_specs=fixed((length, model)),
            scratch_shapes=[pltpu.VMEM((lanes, model), bf16)],
        ),
        out_shape=result((length, model), bf16),
        cost_estimate=pl.CostEstimate(
            flops=2 * length * model * inner.shape[1], transcendentals=0,
            bytes_accessed=12 * 1024 * 1024,
        ),
        compiler_params=params(),
    )(meta, inner, n_r, *reduces, lift)


def attention_back(
    qrot, dop, mixed, kd, v0, v1, kt, bias, dq_t, dk, dv, rows, block, keys, log_scale, fresh,
):
    pairs = qrot.shape[1] // lanes
    share = pairs // 2
    lane = lane_of((block, lanes))
    queries = pl.ds(rows, block)

    def body(pair, carry):
        group = pair // share
        start = pl.multiple_of(pair * lanes, lanes)
        place = pl.ds(start, lanes)
        q = qrot[queries, place].astype(f32)
        up = dop[queries, place].astype(f32)
        mix = mixed[queries, place].astype(f32)
        k = kd[group, 0:keys, :]
        k_t = kt[group, :, 0:keys]
        dk_sum = dk[group, 0:keys, :]
        dv_sum = dv[group, 0:keys, :]
        for head, values in enumerate((v0, v1)):
            own = (lane < half) if head == 0 else (lane >= half)
            q_head = jnp.where(own, q, 0.0).astype(bf16)
            up_head = jnp.where(own, up, 0.0).astype(bf16)
            seen = jnp.where(own, up, mix).astype(bf16)
            e = jnp.exp2(nt(k, q_head) * log_scale + bias[0:keys, queries])
            ds = (e * nt(values[group, 0:keys, :], seen)).astype(bf16)
            dv_sum = dv_sum + nn(e.astype(bf16), up_head)
            dk_sum = dk_sum + nn(ds, q_head)
            piece = nn(k_t, ds)
            target = pl.ds(pl.multiple_of(start + head * half, half), half)
            if fresh:
                dq_t[target, queries] = piece
            else:
                dq_t[target, queries] += piece
        dk[group, 0:keys, :] = dk_sum
        dv[group, 0:keys, :] = dv_sum
        return carry

    lax.fori_loop(0, pairs, body, 0)


def fold_pairs(sums):
    lane = lane_of(sums.shape[1:])
    first = sums[0]
    second = sums[1]
    return jnp.where(lane < half, first + swap_halves(first), second + swap_halves(second))


def transposed_keys(kv, kt):
    key = kv[:, 0:lanes].astype(f32).T
    kt[0] = key[0:half].astype(bf16)
    kt[1] = key[half:].astype(bf16)


def far_kernel(
    meta, cot, summed, att, wide, inv, narrow, qrot, kv, segq, w0, w1, w2, w3, ao, bo,
    dop, mixed, dq_t, dkv, part_pack, full_pack,
    up, a_all, b_all, kd, v0, v1, kt, bias, dk, dv, *, log_scale, block,
):
    length = cot.shape[0]
    a_all[...] = jnp.zeros_like(a_all)
    b_all[...] = jnp.zeros_like(b_all)
    a_all[0:rank, :] = ao[0]
    b_all[0:rank, :] = bo[0]

    def body(index, carry):
        part_sum, full_sum = carry
        rows = pl.ds(pl.multiple_of(index * block, block), block)
        up[rows, :] = (cot[rows, :].astype(f32) + summed[rows, :].astype(f32)).astype(bf16)
        low = nt(up[rows, :], b_all[...])
        grad = nn(low.astype(bf16), a_all[...])
        for number, weight in enumerate((w0, w1, w2, w3)):
            columns = pl.ds(at(meta, number), weight.shape[1])
            grad = grad + nt(up[rows, columns], weight[...])
        scaled = (grad.astype(bf16).astype(f32) * inv[rows, :]).astype(bf16)
        dop[rows, :] = scaled
        inner = scaled.astype(f32) * wide[rows, :]
        for start in range(0, inner.shape[1], lanes):
            mixed[rows, start : start + lanes] = (
                -swap_halves(inner[:, start : start + lanes])
            ).astype(bf16)
        part_sum = part_sum + nn(low.T[0:rank].astype(bf16), att[rows, :])
        full_sum = full_sum + nn(narrow[rows, :].astype(f32).T[0:rank].astype(bf16), up[rows, :])
        return part_sum, full_sum

    part_sum, full_sum = lax.fori_loop(
        0,
        length // block,
        body,
        (jnp.zeros((rank, att.shape[1]), f32), jnp.zeros((rank, cot.shape[1]), f32)),
    )
    part_pack[...] = part_sum.astype(bf16)
    full_pack[...] = full_sum.astype(bf16)
    spread_keys(kv, kd, v0, v1, 0, length)
    transposed_keys(kv, kt)
    segk = jnp.where(meta[5] > 0, kv[:, 2 * lanes :].astype(f32)[:, 0:1], -1.0)
    bias[...] = jnp.where(segk == segq[...].astype(f32), 0.0, masked)
    dk[...] = jnp.zeros_like(dk)
    dv[...] = jnp.zeros_like(dv)
    for start in range(0, length, block):
        attention_back(
            qrot, dop, mixed, kd, v0, v1, kt, bias, dq_t, dk, dv, start, block, length, log_scale, True
        )
    dkv[:, 0:lanes] = (fold_pairs(dk[...]) * (half**-0.5)).astype(bf16)
    dkv[:, lanes:] = fold_pairs(dv[...]).astype(bf16)


def near_kernel(
    meta, dop, mixed, qrot, kv, segq, dq_far,
    dq_t, dkv, kd, v0, v1, kt, bias, dk, dv, *, log_scale, block,
):
    length = qrot.shape[0]
    spread_keys(kv, kd, v0, v1, 0, length)
    transposed_keys(kv, kt)
    key = lax.broadcasted_iota(jnp.int32, (length, length), 0)
    query = lax.broadcasted_iota(jnp.int32, (length, length), 1)
    segk = kv[:, 2 * lanes :].astype(f32)[:, 0:1]
    bias[...] = jnp.where((segk == segq[...].astype(f32)) & (key <= query), 0.0, masked)
    dk[...] = jnp.zeros_like(dk)
    dv[...] = jnp.zeros_like(dv)
    dq_t[...] = dq_far[...]
    for start in range(0, length, block):
        attention_back(
            qrot, dop, mixed, kd, v0, v1, kt, bias, dq_t, dk, dv, start, block, start + block,
            log_scale, False,
        )
    dkv[:, 0:lanes] = fold_pairs(dk[...]) * (half**-0.5)
    dkv[:, lanes:] = fold_pairs(dv[...])


def back_scratch(length):
    return [
        pltpu.VMEM((2, length, lanes), bf16),
        pltpu.VMEM((2, length, lanes), bf16),
        pltpu.VMEM((2, length, lanes), bf16),
        pltpu.VMEM((2, half, length), bf16),
        pltpu.VMEM((length, length), f32),
        pltpu.VMEM((2, length, lanes), f32),
        pltpu.VMEM((2, length, lanes), f32),
    ]


def attention_backward_far(
    meta, cot, summed, att, wide, inv, narrow, qrot, kv, segq, weights, down, lift, log_scale
):
    length, model = cot.shape
    q_width = qrot.shape[1]
    pick = lambda a: pl.BlockSpec(
        (1,) + a.shape[1:], lambda i, m: (m[7], 0, 0), pipeline_mode=pl.Buffered(1)
    )
    plain = (cot, summed, att, wide, inv, narrow, qrot, kv, segq, *weights)
    shapes = [
        result((length, q_width), bf16),
        result((length, q_width), bf16),
        result((q_width, length), f32),
        result((length, 2 * lanes), bf16),
        result((rank, q_width), bf16),
        result((rank, model), bf16),
    ]
    return pl.pallas_call(
        partial(far_kernel, log_scale=log_scale, block=256),
        name="attention_backward_far",
        grid_spec=pltpu.PrefetchScalarGridSpec(
            num_scalar_prefetch=1,
            grid=(1,),
            in_specs=[fixed(a.shape) for a in plain] + [pick(down), pick(lift)],
            out_specs=[fixed(s.shape) for s in shapes],
            scratch_shapes=[
                pltpu.VMEM((length, model), bf16),
                pltpu.VMEM((lanes, q_width), bf16),
                pltpu.VMEM((lanes, model), bf16),
            ]
            + back_scratch(length),
        ),
        out_shape=shapes,
        cost_estimate=pl.CostEstimate(
            flops=20 * length * length * q_width, transcendentals=length * length * 8,
            bytes_accessed=16 * 1024 * 1024,
        ),
        compiler_params=pltpu.CompilerParams(vmem_limit_bytes=vmem_bytes),
    )(meta, *plain, down, lift)


def attention_backward_near(meta, dop, mixed, qrot, kv, segq, dq_far, log_scale):
    length, q_width = qrot.shape
    plain = (dop, mixed, qrot, kv, segq, dq_far)
    shapes = [result((q_width, length), f32), result((length, 2 * lanes), f32)]
    return pl.pallas_call(
        partial(near_kernel, log_scale=log_scale, block=256),
        name="attention_backward_near",
        grid_spec=pltpu.PrefetchScalarGridSpec(
            num_scalar_prefetch=1,
            grid=(1,),
            in_specs=[fixed(a.shape) for a in plain],
            out_specs=[fixed(s.shape) for s in shapes],
            scratch_shapes=back_scratch(length),
        ),
        out_shape=shapes,
        cost_estimate=pl.CostEstimate(
            flops=20 * length * length * q_width, transcendentals=length * length * 8,
            bytes_accessed=6 * 1024 * 1024,
        ),
        compiler_params=pltpu.CompilerParams(vmem_limit_bytes=vmem_bytes),
    )(meta, *plain)


def qkv_grad_kernel(
    meta, normed, narrow, pre, dq_t, dkv_near, dkv_back, bq, bk, bv, qg, kg, cos, sin,
    grad, low_out, down_pack, q_lift, kv_lift, b_all, down_sum, lift_sum,
):
    q_width, kv_width = bq.shape[2], bk.shape[2]
    step = pl.program_id(0)

    @pl.when(step == 0)
    def _():
        b_all[...] = jnp.zeros_like(b_all)
        b_all[0:rank, 0:q_width] = bq[0]
        b_all[rank : 2 * rank, q_width : q_width + kv_width] = bk[0]
        b_all[2 * rank : 3 * rank, q_width + kv_width :] = bv[0]
        down_sum[...] = jnp.zeros_like(down_sum)
        lift_sum[...] = jnp.zeros_like(lift_sum)

    matrix = head_mean_matrix()
    dkv = dkv_near[...] + dkv_back[...].astype(f32)
    for start in range(0, q_width + kv_width, lanes):
        if start < q_width:
            upstream = dq_t[start : start + lanes, :].T * (half**-0.5)
        else:
            upstream = dkv[:, start - q_width : start - q_width + lanes]
        upstream = upstream * cos[...] - partner(upstream) * sin[...]
        value = pre[:, start : start + lanes]
        inverse = lax.rsqrt(head_mean(value * value, matrix) + epsilon)
        weighted = upstream * (qg if start < q_width else kg)[...]
        mean = head_mean(weighted * value, matrix)
        grad[:, start : start + lanes] = (
            inverse * weighted - value * (inverse * inverse * inverse * mean)
        ).astype(bf16)
    grad[:, q_width + kv_width :] = dkv[:, kv_width:].astype(bf16)
    own = grad[...]
    low = nt(own, b_all[...])
    low_out[...] = low.astype(bf16)
    down_sum[...] += nn(low.T[0 : 3 * rank].astype(bf16), normed[...])
    lift_sum[...] += nn(narrow[...].astype(f32).T[0 : 3 * rank].astype(bf16), own)

    @pl.when(step == pl.num_programs(0) - 1)
    def _():
        down_pack[...] = down_sum[...].astype(bf16)
        q_lift[...] = lift_sum[0:rank, 0:q_width].astype(bf16)
        kv_lift[:, 0:kv_width] = lift_sum[rank : 2 * rank, q_width : q_width + kv_width].astype(bf16)
        kv_lift[:, kv_width:] = lift_sum[2 * rank :, q_width + kv_width :].astype(bf16)


def qkv_grads(
    meta, normed, narrow, pre, dq_t, dkv_near, dkv_back, lifts, q_gain, k_gain, cos, sin
):
    length, width = normed.shape
    q_width, kv_width = lifts[0].shape[2], lifts[1].shape[2]
    every = q_width + 2 * kv_width
    block = 256
    tile = lambda w: pl.BlockSpec((block, w), lambda i, m: (i, 0))
    return pl.pallas_call(
        qkv_grad_kernel,
        name="qkv_grads",
        grid_spec=pltpu.PrefetchScalarGridSpec(
            num_scalar_prefetch=1,
            grid=(length // block,),
            in_specs=[
                tile(width), tile(lanes), tile(q_width + kv_width),
                pl.BlockSpec((q_width, block), lambda i, m: (0, i)), tile(2 * kv_width),
                tile(2 * kv_width),
            ]
            + [picked(a) for a in lifts]
            + [fixed(q_gain.shape), fixed(k_gain.shape), tile(lanes), tile(lanes)],
            out_specs=[
                tile(every), tile(lanes), fixed((3 * rank, width)), fixed((rank, q_width)),
                fixed((rank, 2 * kv_width)),
            ],
            scratch_shapes=[
                pltpu.VMEM((lanes, every), bf16),
                pltpu.VMEM((3 * rank, width), f32),
                pltpu.VMEM((3 * rank, every), f32),
            ],
        ),
        out_shape=[
            result((length, every), bf16),
            result((length, lanes), bf16),
            result((3 * rank, width), bf16),
            result((rank, q_width), bf16),
            result((rank, 2 * kv_width), bf16),
        ],
        cost_estimate=pl.CostEstimate(
            flops=2 * length * width * every // 8, transcendentals=0, bytes_accessed=8 * 1024 * 1024
        ),
        compiler_params=params(),
    )(
        meta, normed, narrow, pre, dq_t, dkv_near, dkv_back, *lifts, q_gain, k_gain, cos, sin
    )


def qkv_back_kernel(
    meta, hid, gain, grad, low, q0, q1, q2, q3, kv0, kv1, kv2, kv3, aq, ak, av, back, a_all, total,
):
    @pl.when(pl.program_id(0) == 0)
    def _():
        a_all[...] = jnp.zeros_like(a_all)
        a_all[0:rank, :] = aq[0]
        a_all[rank : 2 * rank, :] = ak[0]
        a_all[2 * rank : 3 * rank, :] = av[0]

    q_width = q0.shape[1]
    q_own, kv_own = grad[:, :q_width], grad[:, q_width:]
    for index, (q_weight, kv_weight) in enumerate(((q0, kv0), (q1, kv1), (q2, kv2), (q3, kv3))):
        columns = pl.ds(at(meta, index), q_weight.shape[0])
        total[:, columns] = (
            nt(q_own, q_weight[...]) + nt(kv_own, kv_weight[...]) + nn(low[...], a_all[:, columns])
        )
    wide = hid[...].astype(f32)
    inverse = lax.rsqrt(jnp.mean(wide * wide, axis=-1, keepdims=True) + epsilon)
    weighted = total[...] * gain[...].astype(f32)
    mean = jnp.mean(weighted * wide, axis=-1, keepdims=True)
    back[...] = (inverse * weighted - wide * (inverse * inverse * inverse * mean)).astype(bf16)


def qkv_backward(meta, hid, gain, grad, low, weights, downs):
    length, width = hid.shape
    every = grad.shape[1]
    block = 256
    tile = lambda w: pl.BlockSpec((block, w), lambda i, m: (i, 0))
    return pl.pallas_call(
        qkv_back_kernel,
        name="qkv_backward",
        grid_spec=pltpu.PrefetchScalarGridSpec(
            num_scalar_prefetch=1,
            grid=(length // block,),
            in_specs=[tile(width), fixed(gain.shape), tile(every), tile(lanes)]
            + [fixed(w.shape) for w in weights]
            + [picked(a) for a in downs],
            out_specs=tile(width),
            scratch_shapes=[pltpu.VMEM((lanes, width), bf16), pltpu.VMEM((block, width), f32)],
        ),
        out_shape=result((length, width), bf16),
        cost_estimate=pl.CostEstimate(
            flops=2 * length * width * every, transcendentals=0, bytes_accessed=8 * 1024 * 1024
        ),
        compiler_params=params(),
    )(meta, hid, gain, grad, low, *weights, *downs)


def place_kernel(sets, *refs, pieces):
    inputs = refs[: len(refs) - len(pieces)]
    outputs = refs[len(inputs) :]
    slot = pl.program_id(0)
    for (source, row, column), out in zip(pieces, outputs):
        width = out.shape[2]
        total = jnp.zeros((rank, width), f32)
        for sequence in range(inputs[source].shape[0]):
            share = jnp.where(sets[sequence] == slot, 1.0, 0.0)
            piece = inputs[source][sequence, row : row + rank, column : column + width]
            total = total + piece.astype(f32) * share
        out[0] = total


def place_sets(sets, gathered, pieces, slots):
    shapes = [result((slots, rank, width), f32) for _, _, _, width in pieces]
    return pl.pallas_call(
        partial(place_kernel, pieces=[p[:3] for p in pieces]),
        name="place_sets",
        grid_spec=pltpu.PrefetchScalarGridSpec(
            num_scalar_prefetch=1,
            grid=(slots,),
            in_specs=[fixed(g.shape) for g in gathered],
            out_specs=[pl.BlockSpec((1,) + s.shape[1:], lambda i, m: (i, 0, 0)) for s in shapes],
        ),
        out_shape=shapes,
        cost_estimate=pl.CostEstimate(flops=0, transcendentals=0, bytes_accessed=8 * 1024 * 1024),
        compiler_params=params(),
    )(sets, *gathered)


def close_kernel(meta, first, second, reduced, out):
    out[...] = (
        first[...].astype(f32) + second[...].astype(f32) + reduced[...].astype(f32)
    ).astype(out.dtype)


def close(meta, first, second, reduced, dtype):
    length, width = reduced.shape
    columns = pl.BlockSpec((length, width), lambda i, m: (0, m[4]))
    return pl.pallas_call(
        close_kernel,
        name="close",
        grid_spec=pltpu.PrefetchScalarGridSpec(
            num_scalar_prefetch=1,
            grid=(1,),
            in_specs=[columns, columns, fixed(reduced.shape)],
            out_specs=fixed(reduced.shape),
        ),
        out_shape=result(reduced.shape, dtype),
        cost_estimate=pl.CostEstimate(flops=0, transcendentals=0, bytes_accessed=4 * 1024 * 1024),
        compiler_params=params(),
    )(meta, first, second, reduced)


def flip(array, axis, bit):
    count = lax.axis_size(axis)
    return lax.ppermute(array, axis, [(i, i ^ bit) for i in range(count)])


def quarters(weight, axis):
    full = lax.all_gather(weight, "fsdp", axis=axis, tiled=True)
    return jnp.split(full, 4, axis=axis)


def after(array, *others):
    return lax.optimization_barrier((array, *others))[0]


def own_half(weight, axis):
    size = weight.shape[axis] // 2
    return lax.dynamic_slice_in_dim(weight, lax.axis_index("ctx") * size, size, axis)


def six_parts(weight, axis):
    shards = quarters(weight, axis)
    return shards[:2] + jnp.split(shards[2], 2, axis=axis) + jnp.split(shards[3], 2, axis=axis)


def shard_places(width, direct):
    unit = width // 4
    part = unit // 2
    if direct:
        four = [(lax.axis_index("fsdp") ^ bit) * unit for bit in range(4)]
        near = lax.axis_index("ctx") * part
    else:
        four, near = [0, unit, 2 * unit, 3 * unit], 0
    away = part - near
    return four, [four[0], four[1], four[2] + near, four[2] + away, four[3] + near, four[3] + away]


def pick_side(low, high, bit, axis):
    return jnp.where(
        bit == 0, jnp.concatenate([low, high], axis=axis), jnp.concatenate([high, low], axis=axis)
    )


def halve(array, axis, bit, stride):
    size = array.shape[-1] // 2
    keep = lax.dynamic_slice_in_dim(array, bit * size, size, array.ndim - 1)
    give = lax.dynamic_slice_in_dim(array, (1 - bit) * size, size, array.ndim - 1)
    taken = flip(give, axis, stride)
    return (keep.astype(f32) + taken.astype(f32)).astype(bf16)


def double(array, axis, bit, stride):
    taken = flip(array, axis, stride)
    return pick_side(array, taken, bit, array.ndim - 1)


def gather_sequences(full, part):
    fsdp = lax.axis_size("fsdp")
    if fsdp != 4 or lax.axis_size("ctx") != 2 or lax.axis_size("tp") != 4:
        full = lax.psum(full, ("ctx", "tp"))
        part = [lax.psum(p, "ctx") for p in part]
        return (
            lax.all_gather(full, "fsdp", axis=0),
            [lax.all_gather(p, "fsdp", axis=0) for p in part],
        )
    own, side, place = lax.axis_index("fsdp"), lax.axis_index("ctx"), lax.axis_index("tp")
    full = halve(full, "ctx", side, 1)
    part = [halve(p, "ctx", side, 1) for p in part]
    full = halve(full, "tp", place % 2, 1)
    full = halve(full, "tp", place // 2, 2)

    def both(array, bit, stride):
        taken = flip(array, "fsdp", stride)
        return pick_side(array, taken, bit, 0)

    full = both(full[None], own // 2, 2)
    part = [both(p[None], own // 2, 2) for p in part]
    full = double(full, "tp", place // 2, 2)
    full = double(full, "tp", place % 2, 1)
    full = double(full, "ctx", side, 1)
    part = [double(p, "ctx", side, 1) for p in part]

    def cores(array):
        taken = flip(array, "fsdp", 1)
        even = own % 2 == 0
        pairs = [jnp.where(even, array[i], taken[i]) for i in range(2)]
        others = [jnp.where(even, taken[i], array[i]) for i in range(2)]
        return jnp.stack([pairs[0], others[0], pairs[1], others[1]])

    return cores(full), [cores(p) for p in part]


def gather_ids(ids):
    if lax.axis_size("fsdp") != 4:
        return lax.all_gather(ids, "fsdp", tiled=True)
    own = lax.axis_index("fsdp")
    two = pick_side(ids, flip(ids, "fsdp", 1), own % 2, 0)
    return pick_side(two, flip(two, "fsdp", 2), own // 2, 0)


def on_device(
    hidden_in, segment_ids, adapter_ids, attention_gain, query_gain, key_gain, feedforward_gain,
    query_weight, key_weight, value_weight, output_weight, gate_weight, linear_weight, reduce_weight,
    query_down, query_lift, key_down, key_lift, value_down, value_lift, output_down, output_lift,
    gate_down, gate_lift, linear_down, linear_lift, reduce_down, reduce_lift, output_cotangent,
):
    _, length, model = hidden_in.shape
    head_dim = query_gain.shape[0]
    log_scale = head_dim**-0.5 * 1.4426950408889634
    context_index = lax.axis_index("ctx")
    tensor_index = lax.axis_index("tp")
    hid = hidden_in[0]
    cot = output_cotangent[0]
    direct = lax.axis_size("fsdp") == 4 and lax.axis_size("ctx") == 2
    four, six = shard_places(model, direct)
    values = (*four, tensor_index, context_index, 0, adapter_ids[0], *six, 0, 0)
    meta = jnp.stack([jnp.asarray(value, jnp.int32) for value in values])

    positions = (context_index * length + jnp.arange(length)).astype(f32)
    frequency = rope_base ** (-2.0 * jnp.arange(head_dim // 2).astype(f32) / head_dim)
    angles = positions[:, None] * frequency[None, :]
    cosine, sine = jnp.cos(angles), jnp.sin(angles)
    cos = jnp.concatenate([cosine] * 4, axis=1)
    sin = jnp.concatenate([-sine, sine] * 2, axis=1)
    q_gain = jnp.tile(query_gain.astype(f32), 2)[None]
    k_gain = jnp.tile(key_gain.astype(f32), 2)[None]
    a_gain = attention_gain[None]
    f_gain = feedforward_gain[None]
    seg_own = segment_ids.reshape(length, 1)
    count = lax.axis_size("ctx")
    onward = [(i, i + 1) for i in range(count - 1)]
    backward = [(i + 1, i) for i in range(count - 1)]
    turn = lambda table: jnp.swapaxes(table, 1, 2)
    qkv_downs = [turn(query_down), turn(key_down), turn(value_down)]
    qkv_lifts = [query_lift, key_lift, value_lift]
    output_first = turn(output_down)
    reduce_first = turn(reduce_down)

    kv_own = jnp.concatenate([key_weight, value_weight], axis=1)
    if direct:
        q_across = flip(query_weight, "fsdp", 2)
        kv_across = flip(kv_own, "fsdp", 2)
        gate_half = own_half(gate_weight, 0)
        cores = [flip(w, "fsdp", 1) for w in (gate_weight, linear_weight, reduce_weight)]
        q_side = flip(after(query_weight, q_across), "fsdp", 1)
        kv_side = flip(after(kv_own, kv_across), "fsdp", 1)
        tables = (*cores, cos, sin, meta, q_gain, k_gain, a_gain, f_gain, seg_own, gate_half)
        qkv_weights = [
            query_weight, q_side, q_across,
            flip(after(q_across, *tables), "fsdp", 1),
            kv_own, kv_side, kv_across, flip(after(kv_across, *tables), "fsdp", 1),
        ]
        output_across = flip(after(output_weight, q_across, kv_across), "fsdp", 2)
        gate_across = flip(after(gate_half, q_across, kv_across), "fsdp", 2)
    else:
        qkv_weights = quarters(query_weight, 0) + quarters(kv_own, 0)
        output_weights = quarters(output_weight, 1)
        gates = six_parts(gate_weight, 0)
        linears = quarters(linear_weight, 0)
        reduces = quarters(reduce_weight, 1)

    normed, qkv_narrow, pre, qrot, kv = qkv_forward(
        meta, hid, a_gain, qkv_weights, qkv_downs, qkv_lifts, q_gain, k_gain, cos, sin, seg_own
    )
    kv_far = lax.ppermute(kv, "ctx", onward)
    ready = after(qrot, gate_across, output_across) if direct else qrot
    att, wide, inv = attention_forward(meta, ready, kv_far, kv, log_scale)
    if direct:
        gate_other = flip(after(gate_across, att), "ctx", 1)
        linear_across = flip(after(linear_weight, att), "fsdp", 2)
        reduce_across = flip(after(reduce_weight, att), "fsdp", 2)
        output_weights = [
            output_weight, flip(after(output_weight, kv_far), "fsdp", 1), output_across,
            flip(after(output_across, kv_far), "fsdp", 1),
        ]
    branch, output_narrow = output_forward(meta, att, output_weights, output_first, output_lift)
    if direct:
        gates = [
            gate_weight, cores[0], gate_across, gate_other, flip(after(gate_across, gate_other), "fsdp", 1),
            flip(gate_other, "fsdp", 1),
        ]
        linears = [linear_weight, cores[1], linear_across, flip(linear_across, "fsdp", 1)]
        reduces = [reduce_weight, cores[2], reduce_across, flip(reduce_across, "fsdp", 1)]
    branch = lax.psum(branch, "tp")

    back, inner, gate_grad, linear_grad, n_gl_t, m_gl_t, m_r_t = ffn(
        meta, hid, branch, cot, f_gain, gates, linears, reduces,
        [turn(gate_down), turn(linear_down), reduce_first], [gate_lift, linear_lift, reduce_lift],
    )
    summed = lax.psum(back, "tp")
    ffn_part, ffn_full, n_r = ffn_adapters(
        meta, hid, branch, cot, f_gain, inner, gate_grad, linear_grad, n_gl_t, m_gl_t, m_r_t,
        reduce_first,
    )
    sets = gather_ids(after(adapter_ids, inner))
    slots = query_down.shape[0]
    ffn_full, (ffn_part,) = gather_sequences(ffn_full, [ffn_part])
    hidden = gate_lift.shape[2]
    ffn_pieces = [(0, rank * i, 0, model) for i in range(3)] + [(1, rank * i, 0, hidden) for i in range(3)]
    ffn_grads = place_sets(sets, [ffn_full, ffn_part], ffn_pieces, slots)
    out = reduce_forward(meta, inner, n_r, reduces, reduce_lift)
    out_columns = lax.psum_scatter(out, "tp", scatter_dimension=1, tiled=True)
    block_out = close(meta, hid, branch, out_columns, bf16)

    dop, mixed, dq_far, dkv_far, output_part, output_full = attention_backward_far(
        meta, cot, summed, att, wide, inv, output_narrow, qrot, kv_far, segment_ids,
        output_weights, output_first, output_lift, log_scale,
    )
    dkv_back = lax.ppermute(dkv_far, "ctx", backward)
    dq_t, dkv_near = attention_backward_near(
        meta, dop, mixed, qrot, kv, segment_ids, dq_far, log_scale
    )
    grad, low, qkv_full, q_part, kv_part = qkv_grads(
        meta, normed, qkv_narrow, pre, dq_t, dkv_near, dkv_back, qkv_lifts, q_gain, k_gain, cos, sin
    )
    last = qkv_backward(meta, hid, a_gain, grad, low, qkv_weights, qkv_downs)
    last_columns = lax.psum_scatter(last, "tp", scatter_dimension=1, tiled=True)
    input_grad = close(meta, cot, summed, last_columns, f32)

    q_width, kv_width = query_lift.shape[2], key_lift.shape[2]
    att_full, (att_part,) = gather_sequences(
        jnp.concatenate([qkv_full, output_full], axis=0),
        [jnp.concatenate([q_part, kv_part, output_part], axis=1)],
    )

    att_pieces = [(0, rank * i, 0, model) for i in range(4)] + [
        (1, 0, 0, q_width),
        (1, 0, q_width, kv_width),
        (1, 0, q_width + kv_width, kv_width),
        (1, 0, q_width + 2 * kv_width, q_width),
    ]
    att_grads = place_sets(sets, [att_full, att_part], att_pieces, slots)
    return (
        block_out[None],
        input_grad[None],
        turn(att_grads[0]),
        att_grads[4],
        turn(att_grads[1]),
        att_grads[5],
        turn(att_grads[2]),
        att_grads[6],
        turn(att_grads[7]),
        att_grads[3],
        turn(ffn_grads[0]),
        ffn_grads[3],
        turn(ffn_grads[1]),
        ffn_grads[4],
        turn(ffn_grads[5]),
        ffn_grads[2],
    )


def solution(mesh):
    tokens = P("fsdp", "ctx", None)
    rows_split = P("fsdp", "tp")
    lift_split = P(None, None, "tp")
    down_split = P(None, "tp", None)
    in_specs = (
        tokens, P("fsdp", "ctx"), P("fsdp"), P(), P(), P(), P(),
        rows_split, rows_split, rows_split, P("tp", "fsdp"), rows_split, rows_split, P("tp", "fsdp"),
        P(), lift_split, P(), lift_split, P(), lift_split, down_split, P(),
        P(), lift_split, P(), lift_split, down_split, P(), tokens,
    )
    cut = P("fsdp", "ctx", "tp")
    out_specs = (
        cut, cut, P(), lift_split, P(), lift_split, P(), lift_split, down_split, P(),
        P(), lift_split, P(), lift_split, down_split, P(),
    )
    return jax.shard_map(
        on_device, mesh=mesh, in_specs=in_specs, out_specs=out_specs, check_vma=False
    )
```

time: 1070 us -> 427 us (0.40)
  waiting for transfers between devices: 743 us -> 197 us
  matrix products: 176 us -> 0 us
  Pallas kernels: 0 us -> 145 us
  other arithmetic: 69.3 us -> 8.25 us
  starting transfers between devices: 11.2 us -> 37.6 us
  blocking collectives: 18.8 us -> 0 us
    psum x6 -> x2, waiting for transfers between devices: 550 us -> 27.2 us  [the longest x1 27.2 us: on_device(): summed = lax.psum(back, 'tp')]
    dot_general x76 -> x0, matrix products: 176 us -> none  [the longest x7 29.2 us: project_back(): jnp.einsum('sln,kn->slk', grad_low, weight, preferred_element_type=jnp.fl...]
    ppermute x5 -> x48, waiting for transfers between devices: 3.28 us -> 170 us  [the longest x46 170 us: flip(): return lax.ppermute(array, axis, [(i, i ^ bit) for i in range(count)])]
    all_gather x5 -> x0, waiting for transfers between devices: 149 us -> none  [the longest x1 52 us: on_device(): lax.all_gather(linear_weight, 'fsdp', axis=0, tiled=True)]
    pallas_call x0 -> x14, Pallas kernels: none -> 145 us  [the longest x1 39 us: ffn(): pl.pallas_call(partial(ffn_kernel, shards=shards, chunk=chunk), name='fee...]
    reduce_scatter x1 -> x2, waiting for transfers between devices: 37.4 us -> 0.02 us  [the longest x1 0.02 us: on_device(): out_columns = lax.psum_scatter(out, 'tp', scatter_dimension=1, tiled=True)]
    convert_element_type x25 -> x5, other arithmetic: 36.8 us -> 0.1 us  [the longest x4 0.1 us: halve(): return (keep.astype(f32) + taken.astype(f32)).astype(bf16)]
    ppermute x5 -> x48, starting transfers between devices: 10.1 us -> 37.4 us  [the longest x46 32.4 us: flip(): return lax.ppermute(array, axis, [(i, i ^ bit) for i in range(count)])]
  transfers between devices with their start and end apart: 17 -> 52, of which waited for: 12 -> 26; matrix products, arithmetic and copies ran while one was open for 16% -> 4% of each run, Pallas kernels for 0% -> 22%
where the time goes in v1:
time: 427 us; the launch traced here: 420 us
  waiting for transfers between devices  197 us (46%)
  Pallas kernels  145 us (34%)
  starting transfers between devices  37.6 us (9%)
  local copies, waits for them, and re-layouts  16.3 us (4%)
  between operations  15.5 us (4%)
  other arithmetic  8.25 us (2%)
    ppermute x46, waiting for transfers between devices, flip(): return lax.ppermute(array, axis, [(i, i ^ bit) for i in range(count)])  170 us
    pallas_call x1, Pallas kernels, ffn(): pl.pallas_call(partial(ffn_kernel, shards=shards, chunk=chunk), name='fee...  39 us
    ppermute x46, starting transfers between devices, flip(): return lax.ppermute(array, axis, [(i, i ^ bit) for i in range(count)])  32.4 us
    psum x1, waiting for transfers between devices, on_device(): summed = lax.psum(back, 'tp')  27.2 us
    pallas_call x1, Pallas kernels, attention_backward_far(): pl.pallas_call(partial(far_kernel, log_scale=log_scale, block=256), name=...  16.2 us
    pallas_call x2, Pallas kernels, place_sets(): pl.pallas_call(partial(place_kernel, pieces=[p[:3] for p in pieces]), nam...  12.6 us
    pallas_call x1, Pallas kernels, reduce_forward(): pl.pallas_call(reduce_kernel, name='reduce_forward', grid_spec=pltpu.Pref...  11.2 us
    pallas_call x1, Pallas kernels, attention_backward_near(): pl.pallas_call(partial(near_kernel, log_scale=log_scale, block=256), name...  10.1 us
  transfers between devices with their start and end apart: 52, of which 26 were waited for; matrix products, arithmetic and copies ran while one was open for 4% of the time, Pallas kernels for 22%

profile of v1, /device:TPU:0, one launch (start us, length us, event | category | flops | bytes accessed | tf_op | source)
XLA Modules:
  0.0 419.7 jit_solution(17564618330643143737)
XLA Ops:
  8.3 2.6 collective-permute-start
  12.9 2.4 constant_dynamic-slice_fusion.8
  15.3 14.0 %collective-permute-done.6.kv2 = bf16[512,256]{1,0:T(8,128)(2,1)} collective-permute-done((bf16[512,256]{1,0:T(8,128)(2,1)S(1)}, bf16[512,256]{1,0:T(8,128)(2,1)}, u32[]{:S(2)}, u32[]{:S(2)}) %collective-permute-start.6) | collective-permute-done | bytes 262176 | tf_op jit(solution)/shard_map/ppermute | solution.py:949
  29.3 1.8 collective-permute-start.9
  38.3 2.1 collective-permute-done.7.kv1
  42.4 9.9 %qkv_forward.1 = (bf16[512,2048]{1,0:T(8,128)(2,1)}, bf16[512,128]{1,0:T(8,128)(2,1)}, f32[512,640]{1,0:T(8,128)}, bf16[512,512]{1,0:T(8,128)(2,1)}, bf16[512,384]{1,0:T(8,128)(2,1)}) custom-call(s32[16]{0:T(128)} %stack.73.meta, bf16[512,2048]{1,0:T(8,128)(2,1)} %bitcast.37, bf16[1,2048]{1,0:T(2,128)(2,1)} %broadcast_in_dim.26.gain, bf16[512,512]{1,0:T(8,128)(2,1)} %q0.3, ...), custom_call_target="tpu_custom_call" | custom-call | flops 1024 | bytes 1024 | tf_op jit(solution)/shard_map/qkv_forward/pallas_call | solution.py:122
  52.4 3.7 collective-permute-start.11
  56.1 9.6 %collective-permute-done.10.w2 = bf16[512,512]{1,0:T(8,128)(2,1)S(1)} collective-permute-done((bf16[512,512]{1,0:T(8,128)(2,1)S(1)}, bf16[512,512]{1,0:T(8,128)(2,1)S(1)}, u32[]{:S(2)}, u32[]{:S(2)}) %collective-permute-start.10) | collective-permute-done | bytes 524320 | tf_op jit(solution)/shard_map/ppermute | solution.py:949
  66.5 9.7 %attention_forward.1 = (bf16[512,512]{1,0:T(8,128)(2,1)}, f32[512,512]{1,0:T(8,128)}, f32[512,512]{1,0:T(8,128)}) custom-call(s32[16]{0:T(128)} %stack.73.meta, bf16[512,512]{1,0:T(8,128)(2,1)} %get-tuple-element.84.qrot, bf16[512,384]{1,0:T(8,128)(2,1)} %copy-done.9, bf16[512,384]{1,0:T(8,128)(2,1)} %get-tuple-element.85.kvn.kvq.kv, ...), custom_call_target="tpu_custom_call" | custom-call | flops 1024 | bytes 1024 | tf_op jit(solution)/shard_map/attention_forward/pallas_call | solution.py:222
  76.2 1.5 collective-permute-start.17
  78.7 1.6 collective-permute-start.14
  81.6 5.7 %output_forward.1 = (bf16[512,2048]{1,0:T(8,128)(2,1)}, bf16[512,128]{1,0:T(8,128)(2,1)}) custom-call(s32[16]{0:T(128)} %stack.73.meta, bf16[512,512]{1,0:T(8,128)(2,1)} %get-tuple-element.86.att, bf16[512,512]{1,0:T(8,128)(2,1)} %w0.3, bf16[512,512]{1,0:T(8,128)(2,1)} %copy-done.7, bf16[512,512]{1,0:T(8,128)(2,1)} %copy-done.5, bf16[512,512]{1,0:T(8,128)(2,1)} %copy-done.6, ...), custom_call_target="tpu_custom_call" | custom-call | flops 1024 | bytes 1024 | tf_op jit(solution)/shard_map/output_forward/pallas_call | solution.py:272
  87.4 37.6 %collective-permute-done.17.refs_8_ = bf16[512,2048]{1,0:T(8,128)(2,1)} collective-permute-done((bf16[512,2048]{1,0:T(8,128)(2,1)}, bf16[512,2048]{1,0:T(8,128)(2,1)}, u32[]{:S(2)}, u32[]{:S(2)}) %collective-permute-start.17) | collective-permute-done | bytes 2097184 | tf_op jit(solution)/shard_map/ppermute | solution.py:949
  125.0 42.9 %collective-permute-done.19.refs_12_.refs_2_ = bf16[2048,512]{1,0:T(8,128)(2,1)} collective-permute-done((bf16[2048,512]{1,0:T(8,128)(2,1)}, bf16[2048,512]{1,0:T(8,128)(2,1)}, u32[]{:S(2)}, u32[]{:S(2)}) %collective-permute-start.19) | collective-permute-done | bytes 2097184 | tf_op jit(solution)/shard_map/ppermute | solution.py:949
  168.4 5.1 %collective-permute-done.15.refs_4_ = bf16[256,2048]{1,0:T(8,128)(2,1)} collective-permute-done((bf16[256,2048]{1,0:T(8,128)(2,1)}, bf16[256,2048]{1,0:T(8,128)(2,1)}, u32[]{:S(2)}, u32[]{:S(2)}) %collective-permute-start.15) | collective-permute-done | bytes 1048608 | tf_op jit(solution)/shard_map/ppermute | solution.py:949
  173.5 1.9 collective-permute-done.16.refs_5_
  176.7 39.0 %feed_forward.1 = (bf16[512,2048]{1,0:T(8,128)(2,1)}, bf16[512,2048]{1,0:T(8,128)(2,1)}, bf16[512,2048]{1,0:T(8,128)(2,1)}, bf16[512,2048]{1,0:T(8,128)(2,1)}, b...) custom-call(s32[16]{0:T(128)} %stack.73.meta, bf16[512,2048]{1,0:T(8,128)(2,1)} %bitcast.38, ...), custom_call_target="tpu_custom_call" | custom-call | flops 17179869184 | bytes 31457280 | tf_op jit(solution)/shard_map/feed_forward/pallas_call | solution.py:410
  215.9 9.9 %feed_forward_adapters.1 = (bf16[48,2048]{1,0:T(8,128)(2,1)}, bf16[48,2048]{1,0:T(8,128)(2,1)}, bf16[512,128]{1,0:T(8,128)(2,1)}) custom-call(s32[16]{0:T(128)} %stack.73.meta, bf16[512,2048]{1,0:T(8,128)(2,1)} %bitcast.39, bf16[512,2048]{1,0:T(8,128)(2,1)} %all-reduce.3.cloned.1.call-done.branch.second, bf16[512,2048]{1,0:T(8,128)(2,1)} %bitcast.43, ...), custom_call_target="tpu_custom_call" | custom-call | flops 536870912 | bytes 12582912 | tf_op jit(solution)/shard_map/feed_forward_adapters/pallas_call | solution.py:483
  227.9 11.2 %reduce_forward.1 = bf16[512,2048]{1,0:T(8,128)(2,1)} custom-call(s32[16]{0:T(128)} %stack.73.meta, bf16[512,2048]{1,0:T(8,128)(2,1)} %get-tuple-element.94.inner, bf16[512,128]{1,0:T(8,128)(2,1)} %get-tuple-element.100.n_r, bf16[2048,512]{1,0:T(8,128)(2,1)} %refs_0_.3, bf16[2048,512]{1,0:T(8,128)(2,1)} %collective-permute-done.4.refs_11_.refs_1_, ...), custom_call_target="tpu_custom_call" | custom-call | flops 4294967296 | bytes 12582912 | tf_op jit(solution)/shard_map/reduce_forward/pallas_call | solution.py:523
  240.1 1.7 collective-permute-start.37
  241.8 6.5 %collective-permute-done.37 = bf16[48,512]{1,0:T(8,128)(2,1)S(1)} collective-permute-done((bf16[48,512]{1,0:T(8,128)(2,1)S(1)}, bf16[48,512]{1,0:T(8,128)(2,1)S(1)}, u32[]{:S(2)}, u32[]{:S(2)}) %collective-permute-start.37) | collective-permute-done | bytes 49184 | tf_op jit(solution)/shard_map/ppermute | solution.py:949
  248.3 1.5 collective-permute-start.38
  249.7 5.8 %collective-permute-done.38 = bf16[48,256]{1,0:T(8,128)(2,1)S(1)} collective-permute-done((bf16[48,256]{1,0:T(8,128)(2,1)S(1)}, bf16[48,256]{1,0:T(8,128)(2,1)S(1)}, u32[]{:S(2)}, u32[]{:S(2)}) %collective-permute-start.38) | collective-permute-done | bytes 24608 | tf_op jit(solution)/shard_map/ppermute | solution.py:949
  255.5 1.5 collective-permute-start.39
  257.1 1.5 collective-permute-start.44
  259.5 2.2 collective-permute-done.44
  262.4 2.6 collective-permute-done.40
  266.5 1.5 collective-permute-start.46
  268.0 1.7 collective-permute-done.41
  270.9 2.3 collective-permute-done.46
  274.8 2.8 collective-permute-done.23
  278.5 27.2 %all-reduce.5.cloned.1.call-done.summed.second = bf16[512,2048]{1,0:T(8,128)(2,1)} async-done(((bf16[512,2048]{1,0:T(8,128)(2,1)}), bf16[512,2048]{1,0:T(8,128)(2,1)}) %all-reduce.5.cloned.1.call-update) | async-done | bytes 2097168 | tf_op jit(solution)/shard_map/psum | solution.py:1135
  305.6 16.2 %attention_backward_far.1 = (bf16[512,512]{1,0:T(8,128)(2,1)}, bf16[512,512]{1,0:T(8,128)(2,1)}, f32[512,512]{1,0:T(8,128)}, bf16[512,256]{1,0:T(8,128)(2,1)}, b...) custom-call(s32[16]{0:T(128)} %stack.73.meta, bf16[512,2048]{1,0:T(8,128)(2,1)} %bitcast.44, ...), custom_call_target="tpu_custom_call" | custom-call | flops 2684354560 | bytes 16777216 | tf_op jit(solution)/shard_map/attention_backward_far/pallas_call | solution.py:703
  324.1 10.1 %attention_backward_near.1 = (f32[512,512]{1,0:T(8,128)}, f32[512,256]{1,0:T(8,128)}) custom-call(s32[16]{0:T(128)} %stack.73.meta, bf16[512,512]{1,0:T(8,128)(2,1)} %get-tuple-element.108.dop, bf16[512,512]{1,0:T(8,128)(2,1)} %get-tuple-element.109.mixed, bf16[512,512]{1,0:T(8,128)(2,1)} %get-tuple-element.84.qrot, ...), custom_call_target="tpu_custom_call" | custom-call | flops 2684354560 | bytes 6291456 | tf_op jit(solution)/shard_map/attention_backward_near/pallas_call | solution.py:731
  334.9 6.5 %qkv_grads.1 = (bf16[512,768]{1,0:T(8,128)(2,1)}, bf16[512,128]{1,0:T(8,128)(2,1)}, bf16[48,2048]{1,0:T(8,128)(2,1)}, bf16[16,512]{1,0:T(8,128)(2,1)}, bf16[16,256]{1,0:T(8,128)(2,1)}) custom-call(s32[16]{0:T(128)} %stack.73.meta, bf16[512,2048]{1,0:T(8,128)(2,1)} %get-tuple-element.102.normed, bf16[512,128]{1,0:T(8,128)(2,1)} %get-tuple-element.103.narrow, ...), custom_call_target="tpu_custom_call" | custom-call | flops 201326592 | bytes 8388608 | tf_op jit(solution)/shard_map/qkv_grads/pallas_call | solution.py:804
  342.5 2.6 collective-permute-start.24
  345.1 7.9 %qkv_backward.1 = bf16[512,2048]{1,0:T(8,128)(2,1)} custom-call(s32[16]{0:T(128)} %stack.73.meta, bf16[512,2048]{1,0:T(8,128)(2,1)} %bitcast.40, bf16[1,2048]{1,0:T(2,128)(2,1)} %broadcast_in_dim.26.gain, bf16[512,768]{1,0:T(8,128)(2,1)} %get-tuple-element.114.grad, bf16[512,128]{1,0:T(8,128)(2,1)} %get-tuple-element.115.low, bf16[512,512]{1,0:T(8,128)(2,1)} %q0.3, ...), custom_call_target="tpu_custom_call" | custom-call | flops 1610612736 | bytes 8388608 | tf_op jit(solution)/shard_map/qkv_backward/pallas_call | solution.py:872
  353.9 4.1 collective-permute-done.25
  358.1 1.3 collective-permute-start.26
  359.5 5.4 %collective-permute-done.26 = bf16[64,256]{1,0:T(8,128)(2,1)S(1)} collective-permute-done((bf16[64,256]{1,0:T(8,128)(2,1)S(1)}, bf16[64,256]{1,0:T(8,128)(2,1)S(1)}, u32[]{:S(2)}, u32[]{:S(2)}) %collective-permute-start.26) | collective-permute-done | bytes 32800 | tf_op jit(solution)/shard_map/ppermute | solution.py:949
  364.9 1.5 collective-permute-start.27
  366.4 2.4 collective-permute-done.27
  370.9 5.2 %collective-permute-done.28 = bf16[2,64,256]{2,1,0:T(8,128)(2,1)S(1)} collective-permute-done((bf16[2,64,256]{2,1,0:T(8,128)(2,1)S(1)}, bf16[2,64,256]{2,1,0:T(8,128)(2,1)S(1)}, u32[]{:S(2)}, u32[]{:S(2)}) %collective-permute-start.28) | collective-permute-done | bytes 65568 | tf_op jit(solution)/shard_map/ppermute | solution.py:949
  377.1 11.3 %collective-permute-done.29 = bf16[2,64,512]{2,1,0:T(8,128)(2,1)S(1)} collective-permute-done((bf16[2,64,512]{2,1,0:T(8,128)(2,1)S(1)}, bf16[2,64,512]{2,1,0:T(8,128)(2,1)S(1)}, u32[]{:S(2)}, u32[]{:S(2)}) %collective-permute-start.29) | collective-permute-done | bytes 131104 | tf_op jit(solution)/shard_map/ppermute | solution.py:949
  390.4 6.6 %place_sets.3 = (f32[8,16,2048]{2,1,0:T(8,128)}, f32[8,16,2048]{2,1,0:T(8,128)}, f32[8,16,2048]{2,1,0:T(8,128)}, f32[8,16,2048]{2,1,0:T(8,128)}, f32[8,16,2048]{2,1,0:T(8,128)}, /*index=5*/f32[8,16,2048]{2,1,0:T(8,128)}) custom-call(s32[4]{0:T(128)} %broadcast_select_fusion.17.sets, bf16[4,48,2048]{2,1,0:T(8,128)(2,1)} %pad_maximum_fusion.1.refs_0_, ...), custom_call_target="tpu_custom_call" | custom-call | bytes 8388608 | tf_op jit(solution)/shard_map/place_sets/pallas_call | solution.py:908
  400.5 6.0 %place_sets.2 = (f32[8,16,2048]{2,1,0:T(8,128)}, f32[8,16,2048]{2,1,0:T(8,128)}, f32[8,16,2048]{2,1,0:T(8,128)}, f32[8,16,2048]{2,1,0:T(8,128)}, f32[8,16,512]{2...) custom-call(s32[4]{0:T(128)} %broadcast_select_fusion.17.sets, ...), custom_call_target="tpu_custom_call" | custom-call | bytes 8388608 | tf_op jit(solution)/shard_map/place_sets/pallas_call | solution.py:908
  406.5 3.0 close.2
  409.5 3.2 close.3
  (179 shorter events, 39.8 us)
Async XLA Ops:
  7.2 168.2 %all-reduce.3.cloned.1.call-start = ((), (), s32[]{:S(2)}) async-start(), calls=%async_computation.2 | async-start | bytes 4194304 | tf_op jit(solution)/shard_map/psum | solution.py:1129
  7.3 29.9 %collective-permute-start.4 = (bf16[2048,512]{1,0:T(8,128)(2,1)}, bf16[2048,512]{1,0:T(8,128)(2,1)}, u32[]{:S(2)}, u32[]{:S(2)}) collective-permute-start(bf16[2048,512]{1,0:T(8,128)(2,1)} %refs_0_.3), channel_id=1, source_target_pairs={{0,8},{8,0},{16,24},{24,16},{1,9},{9,1},{17,25},{25,17},{2,10},{10... | collective-permute-start | bytes 6291464 | tf_op jit(solution)/shard_map/ppermute | solution.py:949
  7.8 29.4 %collective-permute-start.2 = (bf16[512,2048]{1,0:T(8,128)(2,1)}, bf16[512,2048]{1,0:T(8,128)(2,1)}, u32[]{:S(2)}, u32[]{:S(2)}) collective-permute-start(bf16[512,2048]{1,0:T(8,128)(2,1)} %refs_0_.2), channel_id=1, source_target_pairs={{0,8},{8,0},{16,24},{24,16},{1,9},{9,1},{17,25},{25,17},{2,10},{10... | collective-permute-start | bytes 6291464 | tf_op jit(solution)/shard_map/ppermute | solution.py:949
  7.9 29.3 %collective-permute-start.3 = (bf16[512,2048]{1,0:T(8,128)(2,1)}, bf16[512,2048]{1,0:T(8,128)(2,1)}, u32[]{:S(2)}, u32[]{:S(2)}) collective-permute-start(bf16[512,2048]{1,0:T(8,128)(2,1)} %refs_6_.1), channel_id=1, source_target_pairs={{0,8},{8,0},{16,24},{24,16},{1,9},{9,1},{17,25},{25,17},{2,10},{10... | collective-permute-start | bytes 6291464 | tf_op jit(solution)/shard_map/ppermute | solution.py:949
  8.3 21.0 %collective-permute-start = (bf16[512,512]{1,0:T(8,128)(2,1)}, bf16[512,512]{1,0:T(8,128)(2,1)S(1)}, u32[]{:S(2)}, u32[]{:S(2)}) collective-permute-start(bf16[512,512]{1,0:T(8,128)(2,1)} %q0.3), channel_id=1, source_target_pairs={{0,16},{8,24},{16,0},{24,8},{1,17},{9,25},{17,1},{25,9},{2,18},{10... | collective-permute-start | bytes 1572872 | tf_op jit(solution)/shard_map/ppermute | solution.py:949
  12.7 16.6 %collective-permute-start.6 = (bf16[512,256]{1,0:T(8,128)(2,1)S(1)}, bf16[512,256]{1,0:T(8,128)(2,1)}, u32[]{:S(2)}, u32[]{:S(2)}) collective-permute-start(bf16[512,256]{1,0:T(8,128)(2,1)S(1)} %constant_dynamic-update-slice_fusion.kv0), channel_id=1, source_target_pairs={{0,16},{8,24},{16,0},{24,8},{1,17},{9,25},{17,1},{25,9},{2,18},{10... | collective-permute-start | bytes 786440 | tf_op jit(solution)/shard_map/ppermute | solution.py:949
  29.3 36.4 %collective-permute-start.9 = (bf16[256,2048]{1,0:T(8,128)(2,1)}, bf16[256,2048]{1,0:T(8,128)(2,1)}, u32[]{:S(2)}, u32[]{:S(2)}) collective-permute-start(bf16[256,2048]{1,0:T(8,128)(2,1)} %constant_dynamic-slice_fusion.8), channel_id=1, source_target_pairs={{0,16},{8,24},{16,0},{24,8},{1,17},{9,25},{17,1},{25,9},{2,18},{10... | collective-permute-start | bytes 3145736 | tf_op jit(solution)/shard_map/ppermute | solution.py:949
  37.2 4.3 %collective-permute-start.1 = (bf16[512,512]{1,0:T(8,128)(2,1)S(1)}, bf16[512,512]{1,0:T(8,128)(2,1)S(1)}, u32[]{:S(2)}, u32[]{:S(2)}) collective-permute-start(bf16[512,512]{1,0:T(8,128)(2,1)S(1)} %copy-done), channel_id=1, source_target_pairs={{0,8},{8,0},{16,24},{24,16},{1,9},{9,1},{17,25},{25,17},{2,10},{10... | collective-permute-start | bytes 1572872 | tf_op jit(solution)/shard_map/ppermute | solution.py:949
  37.2 4.3 %collective-permute-start.5 = (bf16[512,512]{1,0:T(8,128)(2,1)S(1)}, bf16[512,512]{1,0:T(8,128)(2,1)S(1)}, u32[]{:S(2)}, u32[]{:S(2)}) collective-permute-start(bf16[512,512]{1,0:T(8,128)(2,1)S(1)} %collective-permute-done.q2), channel_id=1, source_target_pairs={{0,8},{8,0},{16,24},{24,16},{1,9},{9,1},{17,25},{25,17},{2,10},{10... | collective-permute-start | bytes 1572872 | tf_op jit(solution)/shard_map/ppermute | solution.py:949
  37.8 3.6 collective-permute-start.8
  40.3 25.4 %collective-permute-start.10 = (bf16[512,512]{1,0:T(8,128)(2,1)S(1)}, bf16[512,512]{1,0:T(8,128)(2,1)S(1)}, u32[]{:S(2)}, u32[]{:S(2)}) collective-permute-start(bf16[512,512]{1,0:T(8,128)(2,1)S(1)} %copy-done.4), channel_id=1, source_target_pairs={{0,16},{8,24},{16,0},{24,8},{1,17},{9,25},{17,1},{25,9},{2,18},{10... | collective-permute-start | bytes 1572872 | tf_op jit(solution)/shard_map/ppermute | solution.py:949
  52.4 13.3 %collective-permute-start.11 = (bf16[512,384]{1,0:T(8,128)(2,1)}, bf16[512,384]{1,0:T(8,128)(2,1)S(1)}, u32[]{:S(2)}, u32[]{:S(2)}) collective-permute-start(bf16[512,384]{1,0:T(8,128)(2,1)} %get-tuple-element.85.kvn.kvq.kv), channel_id=1, source_target_pairs={{0,4},{1,5},{2,6},{3,7},{8,12},{9,13},{10,14},{11,15},{16,20},{17,... | collective-permute-start | bytes 1179656 | tf_op jit(solution)/shard_map/ppermute | solution.py:1110
  76.2 48.9 %collective-permute-start.17 = (bf16[512,2048]{1,0:T(8,128)(2,1)}, bf16[512,2048]{1,0:T(8,128)(2,1)}, u32[]{:S(2)}, u32[]{:S(2)}) collective-permute-start(bf16[512,2048]{1,0:T(8,128)(2,1)} %refs_6_.1), channel_id=1, source_target_pairs={{0,16},{8,24},{16,0},{24,8},{1,17},{9,25},{17,1},{25,9},{2,18},{10... | collective-permute-start | bytes 6291464 | tf_op jit(solution)/shard_map/ppermute | solution.py:949
  77.7 90.2 %collective-permute-start.19 = (bf16[2048,512]{1,0:T(8,128)(2,1)}, bf16[2048,512]{1,0:T(8,128)(2,1)}, u32[]{:S(2)}, u32[]{:S(2)}) collective-permute-start(bf16[2048,512]{1,0:T(8,128)(2,1)} %refs_0_.3), channel_id=1, source_target_pairs={{0,16},{8,24},{16,0},{24,8},{1,17},{9,25},{17,1},{25,9},{2,18},{10... | collective-permute-start | bytes 6291464 | tf_op jit(solution)/shard_map/ppermute | solution.py:949
  78.2 2.7 collective-permute-start.12
  78.7 89.2 %collective-permute-start.14 = (bf16[256,2048]{1,0:T(8,128)(2,1)}, bf16[256,2048]{1,0:T(8,128)(2,1)}, u32[]{:S(2)}, u32[]{:S(2)}) collective-permute-start(bf16[256,2048]{1,0:T(8,128)(2,1)} %collective-permute-done.9.refs_2_), channel_id=1, source_target_pairs={{0,4},{4,0},{1,5},{5,1},{2,6},{6,2},{3,7},{7,3},{8,12},{12,8},{9,1... | collective-permute-start | bytes 3145736 | tf_op jit(solution)/shard_map/ppermute | solution.py:949
  87.4 218.3 %all-reduce.5.cloned.1.call-start = ((), (), s32[]{:S(2)}) async-start(), calls=%async_computation.4 | async-start | bytes 4194304 | tf_op jit(solution)/shard_map/psum | solution.py:1135
  125.0 50.4 %collective-permute-start.18 = (bf16[512,2048]{1,0:T(8,128)(2,1)}, bf16[512,2048]{1,0:T(8,128)(2,1)}, u32[]{:S(2)}, u32[]{:S(2)}) collective-permute-start(bf16[512,2048]{1,0:T(8,128)(2,1)} %collective-permute-done.17.refs_8_), channel_id=1, source_target_pairs={{0,8},{8,0},{16,24},{24,16},{1,9},{9,1},{17,25},{25,17},{2,10},{10... | collective-permute-start | bytes 6291464 | tf_op jit(solution)/shard_map/ppermute | solution.py:949
  167.9 7.5 %collective-permute-start.20 = (bf16[2048,512]{1,0:T(8,128)(2,1)}, bf16[2048,512]{1,0:T(8,128)(2,1)S(1)}, u32[]{:S(2)}, u32[]{:S(2)}) collective-permute-start(bf16[2048,512]{1,0:T(8,128)(2,1)} %collective-permute-done.19.refs_12_.refs_2_), channel_id=1, source_target_pairs={{0,8},{8,0},{16,24},{24,16},{1,9},{9,1},{17,25},{25,17},{2,10},{10... | collective-permute-start | bytes 6291464 | tf_op jit(solution)/shard_map/ppermute | solution.py:949
  167.9 5.6 %collective-permute-start.15 = (bf16[256,2048]{1,0:T(8,128)(2,1)}, bf16[256,2048]{1,0:T(8,128)(2,1)}, u32[]{:S(2)}, u32[]{:S(2)}) collective-permute-start(bf16[256,2048]{1,0:T(8,128)(2,1)} %collective-permute-done.9.refs_2_), channel_id=1, source_target_pairs={{0,8},{8,0},{16,24},{24,16},{1,9},{9,1},{17,25},{25,17},{2,10},{10... | collective-permute-start | bytes 3145736 | tf_op jit(solution)/shard_map/ppermute | solution.py:949
  168.4 7.0 %collective-permute-start.16 = (bf16[256,2048]{1,0:T(8,128)(2,1)}, bf16[256,2048]{1,0:T(8,128)(2,1)}, u32[]{:S(2)}, u32[]{:S(2)}) collective-permute-start(bf16[256,2048]{1,0:T(8,128)(2,1)} %collective-permute-done.14.refs_3_), channel_id=1, source_target_pairs={{0,8},{8,0},{16,24},{24,16},{1,9},{9,1},{17,25},{25,17},{2,10},{10... | collective-permute-start | bytes 3145736 | tf_op jit(solution)/shard_map/ppermute | solution.py:949
  215.8 190.7 %reduce-scatter.3.cloned.1.call-start = ((), (), s32[]{:S(2)}) async-start(), calls=%async_computation.3 | async-start | bytes 2621440 | tf_op jit(solution)/shard_map/reduce_scatter | solution.py:1147
  226.7 12.6 %collective-permute-start.36 = (bf16[48,1024]{1,0:T(8,128)(2,1)S(1)}, bf16[48,1024]{1,0:T(8,128)(2,1)S(1)}, u32[]{:S(2)}, u32[]{:S(2)}) collective-permute-start(bf16[48,1024]{1,0:T(8,128)(2,1)S(1)} %constant_dynamic-slice_fusion.3), channel_id=1, source_target_pairs={{0,4},{4,0},{1,5},{5,1},{2,6},{6,2},{3,7},{7,3},{8,12},{12,8},{9,1... | collective-permute-start | bytes 294920 | tf_op jit(solution)/shard_map/ppermute | solution.py:949
  239.2 170.3 %reduce-scatter.5.cloned.1.call-start = ((), (), s32[]{:S(2)}) async-start(), calls=%async_computation.5 | async-start | bytes 2621440 | tf_op jit(solution)/shard_map/reduce_scatter | solution.py:1162
  240.1 8.1 %collective-permute-start.37 = (bf16[48,512]{1,0:T(8,128)(2,1)S(1)}, bf16[48,512]{1,0:T(8,128)(2,1)S(1)}, u32[]{:S(2)}, u32[]{:S(2)}) collective-permute-start(bf16[48,512]{1,0:T(8,128)(2,1)S(1)} %constant_dynamic-slice_fusion.2), channel_id=1, source_target_pairs={{0,1},{1,0},{2,3},{3,2},{4,5},{5,4},{6,7},{7,6},{8,9},{9,8},{10,11... | collective-permute-start | bytes 147464 | tf_op jit(solution)/shard_map/ppermute | solution.py:949
  248.3 7.2 %collective-permute-start.38 = (bf16[48,256]{1,0:T(8,128)(2,1)S(1)}, bf16[48,256]{1,0:T(8,128)(2,1)S(1)}, u32[]{:S(2)}, u32[]{:S(2)}) collective-permute-start(bf16[48,256]{1,0:T(8,128)(2,1)S(1)} %constant_dynamic-slice_fusion.1), channel_id=1, source_target_pairs={{0,2},{1,3},{2,0},{3,1},{4,6},{5,7},{6,4},{7,5},{8,10},{9,11},{10,... | collective-permute-start | bytes 73736 | tf_op jit(solution)/shard_map/ppermute | solution.py:949
  255.5 3.9 collective-permute-start.39
  257.1 4.7 %collective-permute-start.44 = (bf16[48,1024]{1,0:T(8,128)(2,1)S(1)}, bf16[48,1024]{1,0:T(8,128)(2,1)S(1)}, u32[]{:S(2)}, u32[]{:S(2)}) collective-permute-start(bf16[48,1024]{1,0:T(8,128)(2,1)S(1)} %constant_dynamic-slice_fusion), channel_id=1, source_target_pairs={{0,4},{4,0},{1,5},{5,1},{2,6},{6,2},{3,7},{7,3},{8,12},{12,8},{9,1... | collective-permute-start | bytes 294920 | tf_op jit(solution)/shard_map/ppermute | solution.py:949
  259.4 5.6 %collective-permute-start.40 = (bf16[2,48,256]{2,1,0:T(8,128)(2,1)S(1)}, bf16[2,48,256]{2,1,0:T(8,128)(2,1)S(1)}, u32[]{:S(2)}, u32[]{:S(2)}) collective-permute-start(bf16[2,48,256]{2,1,0:T(8,128)(2,1)S(1)} %maximum_select_fusion.10), channel_id=1, source_target_pairs={{0,2},{1,3},{2,0},{3,1},{4,6},{5,7},{6,4},{7,5},{8,10},{9,11},{10,... | collective-permute-start | bytes 147464 | tf_op jit(solution)/shard_map/ppermute | solution.py:949
  261.8 4.7 %collective-permute-start.45 = (bf16[1,48,1024]{2,1,0:T(8,128)(2,1)S(1)}, bf16[1,48,1024]{2,1,0:T(8,128)(2,1)S(1)}, u32[]{:S(2)}, u32[]{:S(2)}) collective-permute-start(bf16[1,48,1024]{2,1,0:T(8,128)(2,1)S(1)} %fusion), channel_id=1, source_target_pairs={{0,16},{8,24},{16,0},{24,8},{1,17},{9,25},{17,1},{25,9},{2,18},{10... | collective-permute-start | bytes 294920 | tf_op jit(solution)/shard_map/ppermute | solution.py:949
  265.0 4.7 %collective-permute-start.41 = (bf16[2,48,512]{2,1,0:T(8,128)(2,1)S(1)}, bf16[2,48,512]{2,1,0:T(8,128)(2,1)S(1)}, u32[]{:S(2)}, u32[]{:S(2)}) collective-permute-start(bf16[2,48,512]{2,1,0:T(8,128)(2,1)S(1)} %maximum_select_fusion.7), channel_id=1, source_target_pairs={{0,1},{1,0},{2,3},{3,2},{4,5},{5,4},{6,7},{7,6},{8,9},{9,8},{10,11... | collective-permute-start | bytes 294920 | tf_op jit(solution)/shard_map/ppermute | solution.py:949
  266.5 6.7 %collective-permute-start.46 = (bf16[2,48,1024]{2,1,0:T(8,128)(2,1)S(1)}, bf16[2,48,1024]{2,1,0:T(8,128)(2,1)S(1)}, u32[]{:S(2)}, u32[]{:S(2)}) collective-permute-start(bf16[2,48,1024]{2,1,0:T(8,128)(2,1)S(1)} %maximum_select_fusion.5), channel_id=1, source_target_pairs={{0,4},{4,0},{1,5},{5,1},{2,6},{6,2},{3,7},{7,3},{8,12},{12,8},{9,1... | collective-permute-start | bytes 589832 | tf_op jit(solution)/shard_map/ppermute | solution.py:949
  268.0 5.4 %collective-permute-start.22 = (s32[1]{0:T(128)}, s32[1]{0:T(128)}, u32[]{:S(2)}, u32[]{:S(2)}) collective-permute-start(s32[1]{0:T(128)} %param.31), channel_id=1, source_target_pairs={{0,8},{8,0},{16,24},{24,16},{1,9},{9,1},{17,25},{25,17},{2,10},{10... | collective-permute-start | bytes 20 | tf_op jit(solution)/shard_map/ppermute | solution.py:949
  269.8 8.4 %collective-permute-start.42 = (bf16[2,48,1024]{2,1,0:T(8,128)(2,1)S(1)}, bf16[2,48,1024]{2,1,0:T(8,128)(2,1)S(1)}, u32[]{:S(2)}, u32[]{:S(2)}) collective-permute-start(bf16[2,48,1024]{2,1,0:T(8,128)(2,1)S(1)} %maximum_select_fusion.4), channel_id=1, source_target_pairs={{0,4},{4,0},{1,5},{5,1},{2,6},{6,2},{3,7},{7,3},{8,12},{12,8},{9,1... | collective-permute-start | bytes 589832 | tf_op jit(solution)/shard_map/ppermute | solution.py:949
  273.3 5.1 %collective-permute-start.47 = (bf16[2,48,2048]{2,1,0:T(8,128)(2,1)S(1)}, bf16[2,48,2048]{2,1,0:T(8,128)(2,1)S(1)}, u32[]{:S(2)}, u32[]{:S(2)}) collective-permute-start(bf16[2,48,2048]{2,1,0:T(8,128)(2,1)S(1)} %maximum_select_fusion.2), channel_id=1, source_target_pairs={{0,8},{8,0},{16,24},{24,16},{1,9},{9,1},{17,25},{25,17},{2,10},{10... | collective-permute-start | bytes 1179656 | tf_op jit(solution)/shard_map/ppermute | solution.py:949
  274.1 3.5 collective-permute-start.23
  278.3 97.8 %collective-permute-start.43 = (bf16[2,48,2048]{2,1,0:T(8,128)(2,1)S(1)}, bf16[2,48,2048]{2,1,0:T(8,128)(2,1)S(1)}, u32[]{:S(2)}, u32[]{:S(2)}) collective-permute-start(bf16[2,48,2048]{2,1,0:T(8,128)(2,1)S(1)} %maximum_select_fusion.1), channel_id=1, source_target_pairs={{0,8},{8,0},{16,24},{24,16},{1,9},{9,1},{17,25},{25,17},{2,10},{10... | collective-permute-start | bytes 1179656 | tf_op jit(solution)/shard_map/ppermute | solution.py:949
  321.8 12.4 %collective-permute-start.21 = (bf16[512,256]{1,0:T(8,128)(2,1)}, bf16[512,256]{1,0:T(8,128)(2,1)S(1)}, u32[]{:S(2)}, u32[]{:S(2)}) collective-permute-start(bf16[512,256]{1,0:T(8,128)(2,1)} %get-tuple-element.113), channel_id=1, source_target_pairs={{4,0},{5,1},{6,2},{7,3},{12,8},{13,9},{14,10},{15,11},{20,16},{21,... | collective-permute-start | bytes 786440 | tf_op jit(solution)/shard_map/ppermute | solution.py:1154
  342.5 11.2 %collective-permute-start.24 = (bf16[64,1024]{1,0:T(8,128)(2,1)S(1)}, bf16[64,1024]{1,0:T(8,128)(2,1)S(1)}, u32[]{:S(2)}, u32[]{:S(2)}) collective-permute-start(bf16[64,1024]{1,0:T(8,128)(2,1)S(1)} %constant_dynamic-slice_fusion.7), channel_id=1, source_target_pairs={{0,4},{4,0},{1,5},{5,1},{2,6},{6,2},{3,7},{7,3},{8,12},{12,8},{9,1... | collective-permute-start | bytes 393224 | tf_op jit(solution)/shard_map/ppermute | solution.py:949
  353.8 4.3 %collective-permute-start.25 = (bf16[64,512]{1,0:T(8,128)(2,1)S(1)}, bf16[64,512]{1,0:T(8,128)(2,1)S(1)}, u32[]{:S(2)}, u32[]{:S(2)}) collective-permute-start(bf16[64,512]{1,0:T(8,128)(2,1)S(1)} %constant_dynamic-slice_fusion.6), channel_id=1, source_target_pairs={{0,1},{1,0},{2,3},{3,2},{4,5},{5,4},{6,7},{7,6},{8,9},{9,8},{10,11... | collective-permute-start | bytes 196616 | tf_op jit(solution)/shard_map/ppermute | solution.py:949
  358.1 6.8 %collective-permute-start.26 = (bf16[64,256]{1,0:T(8,128)(2,1)S(1)}, bf16[64,256]{1,0:T(8,128)(2,1)S(1)}, u32[]{:S(2)}, u32[]{:S(2)}) collective-permute-start(bf16[64,256]{1,0:T(8,128)(2,1)S(1)} %constant_dynamic-slice_fusion.5), channel_id=1, source_target_pairs={{0,2},{1,3},{2,0},{3,1},{4,6},{5,7},{6,4},{7,5},{8,10},{9,11},{10,... | collective-permute-start | bytes 98312 | tf_op jit(solution)/shard_map/ppermute | solution.py:949
  364.9 4.0 collective-permute-start.27
  366.4 3.8 collective-permute-start.32
  368.9 7.2 %collective-permute-start.28 = (bf16[2,64,256]{2,1,0:T(8,128)(2,1)S(1)}, bf16[2,64,256]{2,1,0:T(8,128)(2,1)S(1)}, u32[]{:S(2)}, u32[]{:S(2)}) collective-permute-start(bf16[2,64,256]{2,1,0:T(8,128)(2,1)S(1)} %maximum_select_fusion.9), channel_id=1, source_target_pairs={{0,2},{1,3},{2,0},{3,1},{4,6},{5,7},{6,4},{7,5},{8,10},{9,11},{10,... | collective-permute-start | bytes 196616 | tf_op jit(solution)/shard_map/ppermute | solution.py:949
  370.2 6.0 %collective-permute-start.33 = (bf16[1,16,640]{2,1,0:T(8,128)(2,1)S(1)}, bf16[1,16,640]{2,1,0:T(8,128)(2,1)S(1)}, u32[]{:S(2)}, u32[]{:S(2)}) collective-permute-start(bf16[1,16,640]{2,1,0:T(8,128)(2,1)S(1)} %fusion.4), channel_id=1, source_target_pairs={{0,16},{8,24},{16,0},{24,8},{1,17},{9,25},{17,1},{25,9},{2,18},{10... | collective-permute-start | bytes 61448 | tf_op jit(solution)/shard_map/ppermute | solution.py:949
  376.1 12.3 %collective-permute-start.29 = (bf16[2,64,512]{2,1,0:T(8,128)(2,1)S(1)}, bf16[2,64,512]{2,1,0:T(8,128)(2,1)S(1)}, u32[]{:S(2)}, u32[]{:S(2)}) collective-permute-start(bf16[2,64,512]{2,1,0:T(8,128)(2,1)S(1)} %maximum_select_fusion.6), channel_id=1, source_target_pairs={{0,1},{1,0},{2,3},{3,2},{4,5},{5,4},{6,7},{7,6},{8,9},{9,8},{10,11... | collective-permute-start | bytes 393224 | tf_op jit(solution)/shard_map/ppermute | solution.py:949
  376.3 20.7 %collective-permute-start.34 = (bf16[2,16,640]{2,1,0:T(8,128)(2,1)S(1)}, bf16[2,16,640]{2,1,0:T(8,128)(2,1)S(1)}, u32[]{:S(2)}, u32[]{:S(2)}) collective-permute-start(bf16[2,16,640]{2,1,0:T(8,128)(2,1)S(1)} %maximum_select_fusion.11), channel_id=1, source_target_pairs={{0,4},{4,0},{1,5},{5,1},{2,6},{6,2},{3,7},{7,3},{8,12},{12,8},{9,1... | collective-permute-start | bytes 122888 | tf_op jit(solution)/shard_map/ppermute | solution.py:949
  388.5 8.6 %collective-permute-start.30 = (bf16[2,64,1024]{2,1,0:T(8,128)(2,1)S(1)}, bf16[2,64,1024]{2,1,0:T(8,128)(2,1)S(1)}, u32[]{:S(2)}, u32[]{:S(2)}) collective-permute-start(bf16[2,64,1024]{2,1,0:T(8,128)(2,1)S(1)} %maximum_select_fusion.3), channel_id=1, source_target_pairs={{0,4},{4,0},{1,5},{5,1},{2,6},{6,2},{3,7},{7,3},{8,12},{12,8},{9,1... | collective-permute-start | bytes 786440 | tf_op jit(solution)/shard_map/ppermute | solution.py:949
  (27 other events, 286.3 us)
Sparse Core Ops, SparseCore 0:
  87.5 87.8 all-reduce.2
  215.9 89.6 all-reduce.4
  307.9 42.8 reduce-scatter.2
  353.1 47.3 reduce-scatter.4

commit v2 on v1

--- a/solution.py
+++ b/solution.py
@@ -34,6 +34,16 @@
     return pl.BlockSpec(shape, lambda *_: (0,) * len(shape), pipeline_mode=pl.Buffered(1))
 
 
+def picked(array):
+    return pl.BlockSpec(
+        (1,) + array.shape[1:], lambda i, m: (m[7], 0, 0), pipeline_mode=pl.Buffered(1)
+    )
+
+
+def params():
+    return pltpu.CompilerParams(vmem_limit_bytes=vmem_bytes)
+
+
 def result(shape, dtype):
     return jax.ShapeDtypeStruct(shape, dtype)
 
@@ -67,29 +77,54 @@
     return pltpu.roll(values, half, values.ndim - 1)
 
 
-def qkv_kernel(
-    meta, hid, gain, q0, q1, q2, q3, kv0, kv1, kv2, kv3, aq, ak, av, bq, bk, bv, qg, kg, cos, sin,
-    seg, normed, narrow, pre, qrot, kv, a_all, b_all,
-):
-    q_width, kv_width = bq.shape[2], bk.shape[2]
-
+def norm_kernel(meta, hid, gain, aq, ak, av, normed, narrow, a_all):
     @pl.when(pl.program_id(0) == 0)
     def _():
         a_all[...] = jnp.zeros_like(a_all)
-        b_all[...] = jnp.zeros_like(b_all)
         a_all[0:rank, :] = aq[0]
         a_all[rank : 2 * rank, :] = ak[0]
         a_all[2 * rank : 3 * rank, :] = av[0]
+
+    wide = hid[...].astype(f32)
+    inverse = lax.rsqrt(jnp.mean(wide * wide, axis=-1, keepdims=True) + epsilon)
+    normed[...] = (wide * inverse * gain[...].astype(f32)).astype(bf16)
+    narrow[...] = nt(normed[...], a_all[...]).astype(bf16)
+
+
+def attention_norm(meta, hid, gain, downs):
+    length, width = hid.shape
+    block = 128
+    tile = lambda w: pl.BlockSpec((block, w), lambda i, m: (i, 0))
+    return pl.pallas_call(
+        norm_kernel,
+        name="attention_norm",
+        grid_spec=pltpu.PrefetchScalarGridSpec(
+            num_scalar_prefetch=1,
+            grid=(length // block,),
+            in_specs=[tile(width), fixed(gain.shape)] + [picked(a) for a in downs],
+            out_specs=[tile(width), tile(lanes)],
+            scratch_shapes=[pltpu.VMEM((lanes, width), bf16)],
+        ),
+        out_shape=[result((length, width), bf16), result((length, lanes), bf16)],
+        cost_estimate=pl.CostEstimate(flops=1024, transcendentals=0, bytes_accessed=1024),
+        compiler_params=params(),
+    )(meta, hid, gain, *downs)
+
+
+def qkv_kernel(
+    meta, normed, narrow, q0, q1, q2, q3, kv0, kv1, kv2, kv3, bq, bk, bv, qg, kg, cos, sin,
+    seg, pre, qrot, kv, b_all,
+):
+    q_width, kv_width = bq.shape[2], bk.shape[2]
+
+    @pl.when(pl.program_id(0) == 0)
+    def _():
+        b_all[...] = jnp.zeros_like(b_all)
         b_all[0:rank, 0:q_width] = bq[0]
         b_all[rank : 2 * rank, q_width : q_width + kv_width] = bk[0]
         b_all[2 * rank : 3 * rank, q_width + kv_width :] = bv[0]
 
-    wide = hid[...].astype(f32)
-    inverse = lax.rsqrt(jnp.mean(wide * wide, axis=-1, keepdims=True) + epsilon)
-    normed[...] = (wide * inverse * gain[...].astype(f32)).astype(bf16)
-    low = nt(normed[...], a_all[...]).astype(bf16)
-    narrow[...] = low
-    total = nn(low, b_all[...])
+    total = nn(narrow[...], b_all[...])
     q_total, kv_total = total[:, :q_width], total[:, q_width:]
     for index, (q_weight, kv_weight) in enumerate(((q0, kv0), (q1, kv1), (q2, kv2), (q3, kv3))):
         part = normed[:, pl.ds(at(meta, index), q_weight.shape[0])]
@@ -111,44 +146,32 @@
     kv[:, 2 * kv_width :] = jnp.broadcast_to(seg[...].astype(f32), (seg.shape[0], lanes)).astype(bf16)
 
 
-def qkv_forward(meta, hid, gain, weights, downs, lifts, q_gain, k_gain, cos, sin, seg):
-    length, width = hid.shape
+def qkv_forward(meta, normed, narrow, weights, lifts, q_gain, k_gain, cos, sin, seg):
+    length, width = normed.shape
     q_width, kv_width = lifts[0].shape[2], lifts[1].shape[2]
     block = 256
     tile = lambda w: pl.BlockSpec((block, w), lambda i, m: (i, 0))
-    pick = lambda a: pl.BlockSpec(
-        (1,) + a.shape[1:], lambda i, m: (m[7], 0, 0), pipeline_mode=pl.Buffered(1)
-    )
     return pl.pallas_call(
         qkv_kernel,
         name="qkv_forward",
         grid_spec=pltpu.PrefetchScalarGridSpec(
             num_scalar_prefetch=1,
             grid=(length // block,),
-            in_specs=[tile(width), fixed(gain.shape)]
+            in_specs=[tile(width), tile(lanes)]
             + [fixed(w.shape) for w in weights]
-            + [pick(a) for a in downs]
-            + [pick(a) for a in lifts]
+            + [picked(a) for a in lifts]
             + [fixed(q_gain.shape), fixed(k_gain.shape), tile(lanes), tile(lanes), tile(1)],
-            out_specs=[
-                tile(width), tile(lanes), tile(q_width + kv_width), tile(q_width),
-                tile(2 * kv_width + lanes),
-            ],
-            scratch_shapes=[
-                pltpu.VMEM((lanes, width), bf16),
-                pltpu.VMEM((lanes, q_width + 2 * kv_width), bf16),
-            ],
+            out_specs=[tile(q_width + kv_width), tile(q_width), tile(2 * kv_width + lanes)],
+            scratch_shapes=[pltpu.VMEM((lanes, q_width + 2 * kv_width), bf16)],
         ),
         out_shape=[
-            result((length, width), bf16),
-            result((length, lanes), bf16),
             result((length, q_width + kv_width), f32),
             result((length, q_width), bf16),
             result((length, 2 * kv_width + lanes), bf16),
         ],
         cost_estimate=pl.CostEstimate(flops=1024, transcendentals=0, bytes_accessed=1024),
-        compiler_params=pltpu.CompilerParams(vmem_limit_bytes=vmem_bytes),
-    )(meta, hid, gain, *weights, *downs, *lifts, q_gain, k_gain, cos, sin, seg)
+        compiler_params=params(),
+    )(meta, normed, narrow, *weights, *lifts, q_gain, k_gain, cos, sin, seg)
 
 
 def spread_keys(kv, kd, v0, v1, rows, size):
@@ -240,7 +263,10 @@
             result((length, q_width), f32),
             result((length, q_width), f32),
         ],
-        cost_estimate=pl.CostEstimate(flops=1024, transcendentals=0, bytes_accessed=1024),
+        cost_estimate=pl.CostEstimate(
+            flops=64 * length * keys * q_width, transcendentals=length * keys * 8,
+            bytes_accessed=64 * 1024 * 1024,
+        ),
         compiler_params=pltpu.CompilerParams(vmem_limit_bytes=vmem_bytes),
     )(meta, qrot, kvf, kvn, kvn)
 
@@ -285,18 +311,8 @@
     )(meta, att, *weights, down, lift)
 
 
-def picked(array):
-    return pl.BlockSpec(
-        (1,) + array.shape[1:], lambda i, m: (m[7], 0, 0), pipeline_mode=pl.Buffered(1)
-    )
-
-
 def strip(array, width):
     return pl.BlockSpec((1, rank, width), lambda j, m: (m[7], 0, j))
-
-
-def params():
-    return pltpu.CompilerParams(vmem_limit_bytes=vmem_bytes)
 
 
 def ffn_kernel(meta, hid, branch, cot, gain, *refs, shards, chunk):
@@ -893,17 +909,18 @@
     inputs = refs[: len(refs) - len(pieces)]
     outputs = refs[len(inputs) :]
     slot = pl.program_id(0)
-    for (source, row, column), out in zip(pieces, outputs):
-        width = out.shape[2]
-        total = jnp.zeros((rank, width), f32)
-        for sequence in range(inputs[source].shape[0]):
-            share = jnp.where(sets[sequence] == slot, 1.0, 0.0)
-            piece = inputs[source][sequence, row : row + rank, column : column + width]
-            total = total + piece.astype(f32) * share
-        out[0] = total
-
-
-def place_sets(sets, gathered, pieces, slots):
+    for out in outputs:
+        out[...] = jnp.zeros_like(out)
+    for sequence in range(inputs[0].shape[0]):
+
+        @pl.when(sets[sequence] == slot)
+        def _():
+            for (source, row, column), out in zip(pieces, outputs):
+                piece = inputs[source][sequence, row : row + rank, column : column + out.shape[2]]
+                out[0] += piece.astype(f32)
+
+
+def place_sets(sets, gathered, pieces, slots, weight):
     shapes = [result((slots, rank, width), f32) for _, _, _, width in pieces]
     return pl.pallas_call(
         partial(place_kernel, pieces=[p[:3] for p in pieces]),
@@ -915,7 +932,7 @@
             out_specs=[pl.BlockSpec((1,) + s.shape[1:], lambda i, m: (i, 0, 0)) for s in shapes],
         ),
         out_shape=shapes,
-        cost_estimate=pl.CostEstimate(flops=0, transcendentals=0, bytes_accessed=8 * 1024 * 1024),
+        cost_estimate=pl.CostEstimate(flops=weight, transcendentals=0, bytes_accessed=8 * 1024 * 1024),
         compiler_params=params(),
     )(sets, *gathered)
 
@@ -928,15 +945,17 @@
 
 def close(meta, first, second, reduced, dtype):
     length, width = reduced.shape
-    columns = pl.BlockSpec((length, width), lambda i, m: (0, m[4]))
+    block = 256
+    columns = pl.BlockSpec((block, width), lambda i, m: (i, m[4]))
+    tile = pl.BlockSpec((block, width), lambda i, m: (i, 0))
     return pl.pallas_call(
         close_kernel,
         name="close",
         grid_spec=pltpu.PrefetchScalarGridSpec(
             num_scalar_prefetch=1,
-            grid=(1,),
-            in_specs=[columns, columns, fixed(reduced.shape)],
-            out_specs=fixed(reduced.shape),
+            grid=(length // block,),
+            in_specs=[columns, columns, tile],
+            out_specs=tile,
         ),
         out_shape=result(reduced.shape, dtype),
         cost_estimate=pl.CostEstimate(flops=0, transcendentals=0, bytes_accessed=4 * 1024 * 1024),
@@ -999,7 +1018,7 @@
     return pick_side(array, taken, bit, array.ndim - 1)
 
 
-def gather_sequences(full, part):
+def gather_sequences(full, part, *others):
     fsdp = lax.axis_size("fsdp")
     if fsdp != 4 or lax.axis_size("ctx") != 2 or lax.axis_size("tp") != 4:
         full = lax.psum(full, ("ctx", "tp"))
@@ -1018,6 +1037,7 @@
         taken = flip(array, "fsdp", stride)
         return pick_side(array, taken, bit, 0)
 
+    full = after(full, *others) if others else full
     full = both(full[None], own // 2, 2)
     part = [both(p[None], own // 2, 2) for p in part]
     full = double(full, "tp", place // 2, 2)
@@ -1082,18 +1102,19 @@
     reduce_first = turn(reduce_down)
 
     kv_own = jnp.concatenate([key_weight, value_weight], axis=1)
+    normed, qkv_narrow = attention_norm(meta, hid, a_gain, qkv_downs)
     if direct:
         q_across = flip(query_weight, "fsdp", 2)
-        kv_across = flip(kv_own, "fsdp", 2)
         gate_half = own_half(gate_weight, 0)
+        tables = (cos, sin, q_gain, k_gain, f_gain, seg_own, normed)
+        kv_across = flip(after(kv_own, *tables), "fsdp", 2)
         cores = [flip(w, "fsdp", 1) for w in (gate_weight, linear_weight, reduce_weight)]
         q_side = flip(after(query_weight, q_across), "fsdp", 1)
         kv_side = flip(after(kv_own, kv_across), "fsdp", 1)
-        tables = (*cores, cos, sin, meta, q_gain, k_gain, a_gain, f_gain, seg_own, gate_half)
         qkv_weights = [
             query_weight, q_side, q_across,
-            flip(after(q_across, *tables), "fsdp", 1),
-            kv_own, kv_side, kv_across, flip(after(kv_across, *tables), "fsdp", 1),
+            flip(after(q_across, *cores), "fsdp", 1),
+            kv_own, kv_side, kv_across, flip(after(kv_across, *cores), "fsdp", 1),
         ]
         output_across = flip(after(output_weight, q_across, kv_across), "fsdp", 2)
         gate_across = flip(after(gate_half, q_across, kv_across), "fsdp", 2)
@@ -1104,16 +1125,16 @@
         linears = quarters(linear_weight, 0)
         reduces = quarters(reduce_weight, 1)
 
-    normed, qkv_narrow, pre, qrot, kv = qkv_forward(
-        meta, hid, a_gain, qkv_weights, qkv_downs, qkv_lifts, q_gain, k_gain, cos, sin, seg_own
+    pre, qrot, kv = qkv_forward(
+        meta, normed, qkv_narrow, qkv_weights, qkv_lifts, q_gain, k_gain, cos, sin, seg_own
     )
     kv_far = lax.ppermute(kv, "ctx", onward)
-    ready = after(qrot, gate_across, output_across) if direct else qrot
+    ready = after(qrot, gate_across) if direct else qrot
     att, wide, inv = attention_forward(meta, ready, kv_far, kv, log_scale)
     if direct:
         gate_other = flip(after(gate_across, att), "ctx", 1)
-        linear_across = flip(after(linear_weight, att), "fsdp", 2)
-        reduce_across = flip(after(reduce_weight, att), "fsdp", 2)
+        linear_across = flip(after(linear_weight, att, output_across), "fsdp", 2)
+        reduce_across = flip(after(reduce_weight, att, output_across), "fsdp", 2)
         output_weights = [
             output_weight, flip(after(output_weight, kv_far), "fsdp", 1), output_across,
             flip(after(output_across, kv_far), "fsdp", 1),
@@ -1142,13 +1163,14 @@
     ffn_full, (ffn_part,) = gather_sequences(ffn_full, [ffn_part])
     hidden = gate_lift.shape[2]
     ffn_pieces = [(0, rank * i, 0, model) for i in range(3)] + [(1, rank * i, 0, hidden) for i in range(3)]
-    ffn_grads = place_sets(sets, [ffn_full, ffn_part], ffn_pieces, slots)
+    ffn_grads = place_sets(sets, [ffn_full, ffn_part], ffn_pieces, slots, 1024)
     out = reduce_forward(meta, inner, n_r, reduces, reduce_lift)
     out_columns = lax.psum_scatter(out, "tp", scatter_dimension=1, tiled=True)
     block_out = close(meta, hid, branch, out_columns, bf16)
+    settled = after(summed, *ffn_grads)
 
     dop, mixed, dq_far, dkv_far, output_part, output_full = attention_backward_far(
-        meta, cot, summed, att, wide, inv, output_narrow, qrot, kv_far, segment_ids,
+        meta, cot, settled, att, wide, inv, output_narrow, qrot, kv_far, segment_ids,
         output_weights, output_first, output_lift, log_scale,
     )
     dkv_back = lax.ppermute(dkv_far, "ctx", backward)
@@ -1166,6 +1188,7 @@
     att_full, (att_part,) = gather_sequences(
         jnp.concatenate([qkv_full, output_full], axis=0),
         [jnp.concatenate([q_part, kv_part, output_part], axis=1)],
+        block_out,
     )
 
     att_pieces = [(0, rank * i, 0, model) for i in range(4)] + [
@@ -1174,7 +1197,7 @@
         (1, 0, q_width + kv_width, kv_width),
         (1, 0, q_width + 2 * kv_width, q_width),
     ]
-    att_grads = place_sets(sets, [att_full, att_part], att_pieces, slots)
+    att_grads = place_sets(sets, [att_full, att_part], att_pieces, slots, 1 << 33)
     return (
         block_out[None],
         input_grad[None],

time: 427 us -> 417 us (0.977)
  waiting for transfers between devices: 197 us -> 180 us
  starting transfers between devices: 37.6 us -> 42.2 us
    ppermute x46, waiting for transfers between devices: 170 us -> 160 us  [flip(): return lax.ppermute(array, axis, [(i, i ^ bit) for i in range(count)])]
    psum x1, waiting for transfers between devices: 27.2 us -> 19.7 us  [on_device(): summed = lax.psum(back, 'tp')]
    pallas_call x0 -> x1, Pallas kernels: none -> 5.01 us  [attention_norm(): pl.pallas_call(norm_kernel, name='attention_norm', grid_spec=pltpu.Prefet...]
    ppermute x46, starting transfers between devices: 32.4 us -> 37.1 us  [flip(): return lax.ppermute(array, axis, [(i, i ^ bit) for i in range(count)])]
  transfers between devices with their start and end apart: 52 -> 52, of which waited for: 26 -> 28; matrix products, arithmetic and copies ran while one was open for 4% -> 5% of each run, Pallas kernels for 22% -> 26%
where the time goes in v2:
time: 417 us; the launch traced here: 409 us
  waiting for transfers between devices  180 us (43%)
  Pallas kernels  147 us (35%)
  starting transfers between devices  42.2 us (10%)
  local copies, waits for them, and re-layouts  15.5 us (4%)
  between operations  15.5 us (4%)
  other arithmetic  9.2 us (2%)
    ppermute x46, waiting for transfers between devices, flip(): return lax.ppermute(array, axis, [(i, i ^ bit) for i in range(count)])  160 us
    pallas_call x1, Pallas kernels, ffn(): pl.pallas_call(partial(ffn_kernel, shards=shards, chunk=chunk), name='fee...  39 us
    ppermute x46, starting transfers between devices, flip(): return lax.ppermute(array, axis, [(i, i ^ bit) for i in range(count)])  37.1 us
    psum x1, waiting for transfers between devices, on_device(): summed = lax.psum(back, 'tp')  19.7 us
    pallas_call x1, Pallas kernels, attention_backward_far(): pl.pallas_call(partial(far_kernel, log_scale=log_scale, block=256), name=...  16.2 us
    pallas_call x2, Pallas kernels, place_sets(): pl.pallas_call(partial(place_kernel, pieces=[p[:3] for p in pieces]), nam...  12 us
    pallas_call x1, Pallas kernels, reduce_forward(): pl.pallas_call(reduce_kernel, name='reduce_forward', grid_spec=pltpu.Pref...  11.2 us
    pallas_call x1, Pallas kernels, attention_backward_near(): pl.pallas_call(partial(near_kernel, log_scale=log_scale, block=256), name...  10.2 us
  transfers between devices with their start and end apart: 52, of which 28 were waited for; matrix products, arithmetic and copies ran while one was open for 5% of the time, Pallas kernels for 26%

profile of v2, /device:TPU:0, one launch (start us, length us, event | category | flops | bytes accessed | tf_op | source)
XLA Modules:
  0.0 409.2 jit_solution(15750154012243528182)
XLA Ops:
  8.3 2.6 collective-permute-start
  15.4 5.0 %attention_norm.1 = (bf16[512,2048]{1,0:T(8,128)(2,1)}, bf16[512,128]{1,0:T(8,128)(2,1)}) custom-call(s32[16]{0:T(128)} %stack.73.meta, bf16[512,2048]{1,0:T(8,128)(2,1)} %bitcast.36, bf16[1,2048]{1,0:T(2,128)(2,1)} %broadcast_in_dim.26.gain, bf16[8,16,2048]{2,1,0:T(8,128)(2,1)} %bitcast.45, bf16[8,16,2048]{2,1,0:T(8,128)(2,1)} %bitcast.47, ...), custom_call_target="tpu_custom_call" | custom-call | flops 1024 | bytes 1024 | tf_op jit(solution)/shard_map/attention_norm/pallas_call | solution.py:98
  23.6 2.3 constant_dynamic-slice_fusion.8
  25.9 6.1 %collective-permute-done.6.kv2 = bf16[512,256]{1,0:T(8,128)(2,1)S(1)} collective-permute-done((bf16[512,256]{1,0:T(8,128)(2,1)S(1)}, bf16[512,256]{1,0:T(8,128)(2,1)S(1)}, u32[]{:S(2)}, u32[]{:S(2)}) %collective-permute-start.6) | collective-permute-done | bytes 262176 | tf_op jit(solution)/shard_map/ppermute | solution.py:968
  37.2 7.6 %qkv_forward.1 = (f32[512,640]{1,0:T(8,128)}, bf16[512,512]{1,0:T(8,128)(2,1)}, bf16[512,384]{1,0:T(8,128)(2,1)}) custom-call(s32[16]{0:T(128)} %stack.73.meta, bf16[512,2048]{1,0:T(8,128)(2,1)} %get-tuple-element.80.normed, bf16[512,128]{1,0:T(8,128)(2,1)} %get-tuple-element.81.narrow, bf16[512,512]{1,0:T(8,128)(2,1)} %q0.3, bf16[512,512]{1,0:T(8,128)(2,1)} %copy-done.6, ...), custom_call_target="tpu_custom_call" | custom-call | flops 1024 | bytes 1024 | tf_op jit(solution)/shard_map/qkv_forward/pallas_call | solution.py:154
  44.8 3.7 collective-permute-start.10
  48.6 1.6 collective-permute-start.12
  50.1 8.3 %collective-permute-done.9.refs_2_ = bf16[256,2048]{1,0:T(8,128)(2,1)} collective-permute-done((bf16[256,2048]{1,0:T(8,128)(2,1)}, bf16[256,2048]{1,0:T(8,128)(2,1)}, u32[]{:S(2)}, u32[]{:S(2)}) %collective-permute-start.9) | collective-permute-done | bytes 1048608 | tf_op jit(solution)/shard_map/ppermute | solution.py:968
  59.2 9.8 %attention_forward.1 = (bf16[512,512]{1,0:T(8,128)(2,1)}, f32[512,512]{1,0:T(8,128)}, f32[512,512]{1,0:T(8,128)}) custom-call(s32[16]{0:T(128)} %stack.73.meta, bf16[512,512]{1,0:T(8,128)(2,1)} %get-tuple-element.89.qrot, bf16[512,384]{1,0:T(8,128)(2,1)} %copy-done.12, bf16[512,384]{1,0:T(8,128)(2,1)} %get-tuple-element.90.kvn.kvq.kv, ...), custom_call_target="tpu_custom_call" | custom-call | flops 17179869184 | bytes 67108864 | tf_op jit(solution)/shard_map/attention_forward/pallas_call | solution.py:245
  69.5 1.6 collective-permute-start.17
  71.6 1.5 collective-permute-start.14
  74.5 5.7 %output_forward.1 = (bf16[512,2048]{1,0:T(8,128)(2,1)}, bf16[512,128]{1,0:T(8,128)(2,1)}) custom-call(s32[16]{0:T(128)} %stack.73.meta, bf16[512,512]{1,0:T(8,128)(2,1)} %get-tuple-element.91.att, bf16[512,512]{1,0:T(8,128)(2,1)} %w0.3, bf16[512,512]{1,0:T(8,128)(2,1)} %copy-done.3, bf16[512,512]{1,0:T(8,128)(2,1)} %copy-done.1, bf16[512,512]{1,0:T(8,128)(2,1)} %copy-done.2, ...), custom_call_target="tpu_custom_call" | custom-call | flops 1024 | bytes 1024 | tf_op jit(solution)/shard_map/output_forward/pallas_call | solution.py:298
  80.3 37.6 %collective-permute-done.19.refs_12_.refs_2_ = bf16[2048,512]{1,0:T(8,128)(2,1)} collective-permute-done((bf16[2048,512]{1,0:T(8,128)(2,1)}, bf16[2048,512]{1,0:T(8,128)(2,1)}, u32[]{:S(2)}, u32[]{:S(2)}) %collective-permute-start.19) | collective-permute-done | bytes 2097184 | tf_op jit(solution)/shard_map/ppermute | solution.py:968
  117.9 42.1 %collective-permute-done.17.refs_8_ = bf16[512,2048]{1,0:T(8,128)(2,1)} collective-permute-done((bf16[512,2048]{1,0:T(8,128)(2,1)S(1)}, bf16[512,2048]{1,0:T(8,128)(2,1)}, u32[]{:S(2)}, u32[]{:S(2)}) %collective-permute-start.17) | collective-permute-done | bytes 2097184 | tf_op jit(solution)/shard_map/ppermute | solution.py:968
  160.6 6.5 %collective-permute-done.15.refs_4_ = bf16[256,2048]{1,0:T(8,128)(2,1)} collective-permute-done((bf16[256,2048]{1,0:T(8,128)(2,1)}, bf16[256,2048]{1,0:T(8,128)(2,1)}, u32[]{:S(2)}, u32[]{:S(2)}) %collective-permute-start.15) | collective-permute-done | bytes 1048608 | tf_op jit(solution)/shard_map/ppermute | solution.py:968
  169.3 39.0 %feed_forward.1 = (bf16[512,2048]{1,0:T(8,128)(2,1)}, bf16[512,2048]{1,0:T(8,128)(2,1)}, bf16[512,2048]{1,0:T(8,128)(2,1)}, bf16[512,2048]{1,0:T(8,128)(2,1)}, b...) custom-call(s32[16]{0:T(128)} %stack.73.meta, bf16[512,2048]{1,0:T(8,128)(2,1)} %bitcast.37, ...), custom_call_target="tpu_custom_call" | custom-call | flops 17179869184 | bytes 31457280 | tf_op jit(solution)/shard_map/feed_forward/pallas_call | solution.py:426
  208.4 9.7 %feed_forward_adapters.1 = (bf16[48,2048]{1,0:T(8,128)(2,1)}, bf16[48,2048]{1,0:T(8,128)(2,1)}, bf16[512,128]{1,0:T(8,128)(2,1)}) custom-call(s32[16]{0:T(128)} %stack.73.meta, bf16[512,2048]{1,0:T(8,128)(2,1)} %bitcast.38, bf16[512,2048]{1,0:T(8,128)(2,1)} %all-reduce.3.cloned.1.call-done.branch.second, bf16[512,2048]{1,0:T(8,128)(2,1)} %bitcast.42, ...), custom_call_target="tpu_custom_call" | custom-call | flops 536870912 | bytes 12582912 | tf_op jit(solution)/shard_map/feed_forward_adapters/pallas_call | solution.py:499
  219.0 1.9 collective-permute-start.23
  220.9 3.1 collective-permute-done.23
  224.9 1.7 collective-permute-start.24
  226.6 6.2 %collective-permute-done.24 = bf16[48,512]{1,0:T(8,128)(2,1)S(1)} collective-permute-done((bf16[48,512]{1,0:T(8,128)(2,1)S(1)}, bf16[48,512]{1,0:T(8,128)(2,1)S(1)}, u32[]{:S(2)}, u32[]{:S(2)}) %collective-permute-start.24) | collective-permute-done | bytes 49184 | tf_op jit(solution)/shard_map/ppermute | solution.py:968
  232.9 1.4 collective-permute-start.25
  234.3 11.2 %reduce_forward.1 = bf16[512,2048]{1,0:T(8,128)(2,1)} custom-call(s32[16]{0:T(128)} %stack.73.meta, bf16[512,2048]{1,0:T(8,128)(2,1)} %get-tuple-element.100.inner, bf16[512,128]{1,0:T(8,128)(2,1)} %get-tuple-element.106.n_r, bf16[2048,512]{1,0:T(8,128)(2,1)} %refs_0_.3, bf16[2048,512]{1,0:T(8,128)(2,1)} %collective-permute-done.4.refs_11_.refs_1_, ...), custom_call_target="tpu_custom_call" | custom-call | flops 4294967296 | bytes 12582912 | tf_op jit(solution)/shard_map/reduce_forward/pallas_call | solution.py:539
  246.8 2.2 collective-permute-start.31
  249.6 1.7 collective-permute-start.27
  252.6 2.3 collective-permute-done.27
  254.9 2.2 collective-permute-start.28
  257.2 2.2 collective-permute-start.33
  259.8 2.2 collective-permute-start.29
  262.0 2.6 collective-permute-done.33
  266.6 2.5 collective-permute-done.22
  272.6 6.3 %place_sets.2 = (f32[8,16,2048]{2,1,0:T(8,128)}, f32[8,16,2048]{2,1,0:T(8,128)}, f32[8,16,2048]{2,1,0:T(8,128)}, f32[8,16,2048]{2,1,0:T(8,128)}, f32[8,16,2048]{2,1,0:T(8,128)}, /*index=5*/f32[8,16,2048]{2,1,0:T(8,128)}) custom-call(s32[4]{0:T(128)} %broadcast_select_fusion.17.sets, bf16[4,48,2048]{2,1,0:T(8,128)(2,1)} %pad_maximum_fusion.1.refs_0_, ...), custom_call_target="tpu_custom_call" | custom-call | flops 1024 | bytes 8388608 | tf_op jit(solution)/shard_map/place_sets/pallas_call | solution.py:925
  278.9 19.7 %all-reduce.5.cloned.1.call-done.summed.second = bf16[512,2048]{1,0:T(8,128)(2,1)} async-done(((bf16[512,2048]{1,0:T(8,128)(2,1)}), bf16[512,2048]{1,0:T(8,128)(2,1)}) %all-reduce.5.cloned.1.call-update) | async-done | bytes 2097168 | tf_op jit(solution)/shard_map/psum | solution.py:1156
  298.5 16.2 %attention_backward_far.1 = (bf16[512,512]{1,0:T(8,128)(2,1)}, bf16[512,512]{1,0:T(8,128)(2,1)}, f32[512,512]{1,0:T(8,128)}, bf16[512,256]{1,0:T(8,128)(2,1)}, b...) custom-call(s32[16]{0:T(128)} %stack.73.meta, bf16[512,2048]{1,0:T(8,128)(2,1)} %bitcast.43, ...), custom_call_target="tpu_custom_call" | custom-call | flops 2684354560 | bytes 16777216 | tf_op jit(solution)/shard_map/attention_backward_far/pallas_call | solution.py:719
  316.0 10.2 %attention_backward_near.1 = (f32[512,512]{1,0:T(8,128)}, f32[512,256]{1,0:T(8,128)}) custom-call(s32[16]{0:T(128)} %stack.73.meta, bf16[512,512]{1,0:T(8,128)(2,1)} %get-tuple-element.122.dop, bf16[512,512]{1,0:T(8,128)(2,1)} %get-tuple-element.123.mixed, bf16[512,512]{1,0:T(8,128)(2,1)} %get-tuple-element.89.qrot, ...), custom_call_target="tpu_custom_call" | custom-call | flops 2684354560 | bytes 6291456 | tf_op jit(solution)/shard_map/attention_backward_near/pallas_call | solution.py:747
  326.9 6.5 %qkv_grads.1 = (bf16[512,768]{1,0:T(8,128)(2,1)}, bf16[512,128]{1,0:T(8,128)(2,1)}, bf16[48,2048]{1,0:T(8,128)(2,1)}, bf16[16,512]{1,0:T(8,128)(2,1)}, bf16[16,256]{1,0:T(8,128)(2,1)}) custom-call(s32[16]{0:T(128)} %stack.73.meta, bf16[512,2048]{1,0:T(8,128)(2,1)} %get-tuple-element.80.normed, bf16[512,128]{1,0:T(8,128)(2,1)} %get-tuple-element.81.narrow, ...), custom_call_target="tpu_custom_call" | custom-call | flops 201326592 | bytes 8388608 | tf_op jit(solution)/shard_map/qkv_grads/pallas_call | solution.py:820
  334.4 2.8 collective-permute-start.36
  337.1 7.9 %qkv_backward.1 = bf16[512,2048]{1,0:T(8,128)(2,1)} custom-call(s32[16]{0:T(128)} %stack.73.meta, bf16[512,2048]{1,0:T(8,128)(2,1)} %bitcast.39, bf16[1,2048]{1,0:T(2,128)(2,1)} %broadcast_in_dim.26.gain, bf16[512,768]{1,0:T(8,128)(2,1)} %get-tuple-element.128.grad, bf16[512,128]{1,0:T(8,128)(2,1)} %get-tuple-element.129.low, bf16[512,512]{1,0:T(8,128)(2,1)} %q0.3, ...), custom_call_target="tpu_custom_call" | custom-call | flops 1610612736 | bytes 8388608 | tf_op jit(solution)/shard_map/qkv_backward/pallas_call | solution.py:888
  346.0 4.2 %collective-permute-done.37 = bf16[64,512]{1,0:T(8,128)(2,1)S(1)} collective-permute-done((bf16[64,512]{1,0:T(8,128)(2,1)S(1)}, bf16[64,512]{1,0:T(8,128)(2,1)S(1)}, u32[]{:S(2)}, u32[]{:S(2)}) %collective-permute-start.37) | collective-permute-done | bytes 65568 | tf_op jit(solution)/shard_map/ppermute | solution.py:968
  351.5 5.4 %collective-permute-done.38 = bf16[64,256]{1,0:T(8,128)(2,1)S(1)} collective-permute-done((bf16[64,256]{1,0:T(8,128)(2,1)S(1)}, bf16[64,256]{1,0:T(8,128)(2,1)S(1)}, u32[]{:S(2)}, u32[]{:S(2)}) %collective-permute-start.38) | collective-permute-done | bytes 32800 | tf_op jit(solution)/shard_map/ppermute | solution.py:968
  357.0 2.9 close.2
  359.9 1.5 collective-permute-start.39
  361.4 2.4 collective-permute-done.39
  365.8 5.8 %collective-permute-done.40 = bf16[2,64,256]{2,1,0:T(8,128)(2,1)S(1)} collective-permute-done((bf16[2,64,256]{2,1,0:T(8,128)(2,1)S(1)}, bf16[2,64,256]{2,1,0:T(8,128)(2,1)S(1)}, u32[]{:S(2)}, u32[]{:S(2)}) %collective-permute-start.40) | collective-permute-done | bytes 65568 | tf_op jit(solution)/shard_map/ppermute | solution.py:968
  371.8 12.0 %collective-permute-done.41 = bf16[2,64,512]{2,1,0:T(8,128)(2,1)S(1)} collective-permute-done((bf16[2,64,512]{2,1,0:T(8,128)(2,1)S(1)}, bf16[2,64,512]{2,1,0:T(8,128)(2,1)S(1)}, u32[]{:S(2)}, u32[]{:S(2)}) %collective-permute-start.41) | collective-permute-done | bytes 131104 | tf_op jit(solution)/shard_map/ppermute | solution.py:968
  384.1 6.2 %collective-permute-done.42 = bf16[2,64,1024]{2,1,0:T(8,128)(2,1)S(1)} collective-permute-done((bf16[2,64,1024]{2,1,0:T(8,128)(2,1)S(1)}, bf16[2,64,1024]{2,1,0:T(8,128)(2,1)S(1)}, u32[]{:S(2)}, u32[]{:S(2)}) %collective-permute-start.42) | collective-permute-done | bytes 262176 | tf_op jit(solution)/shard_map/ppermute | solution.py:968
  393.6 5.7 %place_sets.3 = (f32[8,16,2048]{2,1,0:T(8,128)}, f32[8,16,2048]{2,1,0:T(8,128)}, f32[8,16,2048]{2,1,0:T(8,128)}, f32[8,16,2048]{2,1,0:T(8,128)}, f32[8,16,512]{2...) custom-call(s32[4]{0:T(128)} %broadcast_select_fusion.17.sets, ...), custom_call_target="tpu_custom_call" | custom-call | flops 8589934592 | bytes 8388608 | tf_op jit(solution)/shard_map/place_sets/pallas_call | solution.py:925
  399.3 2.9 close.3
  (188 shorter events, 41.3 us)
Async XLA Ops:
  7.2 160.8 %all-reduce.3.cloned.1.call-start = ((), (), s32[]{:S(2)}) async-start(), calls=%async_computation.2 | async-start | bytes 4194304 | tf_op jit(solution)/shard_map/psum | solution.py:1150
  7.2 25.1 %collective-permute-start.4 = (bf16[2048,512]{1,0:T(8,128)(2,1)}, bf16[2048,512]{1,0:T(8,128)(2,1)}, u32[]{:S(2)}, u32[]{:S(2)}) collective-permute-start(bf16[2048,512]{1,0:T(8,128)(2,1)} %refs_0_.3), channel_id=1, source_target_pairs={{0,8},{8,0},{16,24},{24,16},{1,9},{9,1},{17,25},{25,17},{2,10},{10... | collective-permute-start | bytes 6291464 | tf_op jit(solution)/shard_map/ppermute | solution.py:968
  7.7 24.6 %collective-permute-start.2 = (bf16[512,2048]{1,0:T(8,128)(2,1)}, bf16[512,2048]{1,0:T(8,128)(2,1)}, u32[]{:S(2)}, u32[]{:S(2)}) collective-permute-start(bf16[512,2048]{1,0:T(8,128)(2,1)} %refs_0_.2), channel_id=1, source_target_pairs={{0,8},{8,0},{16,24},{24,16},{1,9},{9,1},{17,25},{25,17},{2,10},{10... | collective-permute-start | bytes 6291464 | tf_op jit(solution)/shard_map/ppermute | solution.py:968
  7.8 24.5 %collective-permute-start.3 = (bf16[512,2048]{1,0:T(8,128)(2,1)}, bf16[512,2048]{1,0:T(8,128)(2,1)}, u32[]{:S(2)}, u32[]{:S(2)}) collective-permute-start(bf16[512,2048]{1,0:T(8,128)(2,1)} %refs_6_.1), channel_id=1, source_target_pairs={{0,8},{8,0},{16,24},{24,16},{1,9},{9,1},{17,25},{25,17},{2,10},{10... | collective-permute-start | bytes 6291464 | tf_op jit(solution)/shard_map/ppermute | solution.py:968
  8.3 23.7 %collective-permute-start = (bf16[512,512]{1,0:T(8,128)(2,1)}, bf16[512,512]{1,0:T(8,128)(2,1)S(1)}, u32[]{:S(2)}, u32[]{:S(2)}) collective-permute-start(bf16[512,512]{1,0:T(8,128)(2,1)} %q0.3), channel_id=1, source_target_pairs={{0,16},{8,24},{16,0},{24,8},{1,17},{9,25},{17,1},{25,9},{2,18},{10... | collective-permute-start | bytes 1572872 | tf_op jit(solution)/shard_map/ppermute | solution.py:968
  23.6 8.4 %collective-permute-start.6 = (bf16[512,256]{1,0:T(8,128)(2,1)S(1)}, bf16[512,256]{1,0:T(8,128)(2,1)S(1)}, u32[]{:S(2)}, u32[]{:S(2)}) collective-permute-start(bf16[512,256]{1,0:T(8,128)(2,1)S(1)} %constant_dynamic-update-slice_fusion.kv0), channel_id=1, source_target_pairs={{0,16},{8,24},{16,0},{24,8},{1,17},{9,25},{17,1},{25,9},{2,18},{10... | collective-permute-start | bytes 786440 | tf_op jit(solution)/shard_map/ppermute | solution.py:968
  32.0 26.5 %collective-permute-start.9 = (bf16[256,2048]{1,0:T(8,128)(2,1)}, bf16[256,2048]{1,0:T(8,128)(2,1)}, u32[]{:S(2)}, u32[]{:S(2)}) collective-permute-start(bf16[256,2048]{1,0:T(8,128)(2,1)} %constant_dynamic-slice_fusion.8), channel_id=1, source_target_pairs={{0,16},{8,24},{16,0},{24,8},{1,17},{9,25},{17,1},{25,9},{2,18},{10... | collective-permute-start | bytes 3145736 | tf_op jit(solution)/shard_map/ppermute | solution.py:968
  32.3 3.0 collective-permute-start.1
  32.3 3.4 collective-permute-start.5
  33.0 2.7 collective-permute-start.8
  44.8 13.6 %collective-permute-start.10 = (bf16[512,384]{1,0:T(8,128)(2,1)}, bf16[512,384]{1,0:T(8,128)(2,1)S(1)}, u32[]{:S(2)}, u32[]{:S(2)}) collective-permute-start(bf16[512,384]{1,0:T(8,128)(2,1)} %get-tuple-element.90.kvn.kvq.kv), channel_id=1, source_target_pairs={{0,4},{1,5},{2,6},{3,7},{8,12},{9,13},{10,14},{11,15},{16,20},{17,... | collective-permute-start | bytes 1179656 | tf_op jit(solution)/shard_map/ppermute | solution.py:1131
  48.6 20.4 %collective-permute-start.12 = (bf16[512,512]{1,0:T(8,128)(2,1)S(1)}, bf16[512,512]{1,0:T(8,128)(2,1)S(1)}, u32[]{:S(2)}, u32[]{:S(2)}) collective-permute-start(bf16[512,512]{1,0:T(8,128)(2,1)S(1)} %copy-done), channel_id=1, source_target_pairs={{0,16},{8,24},{16,0},{24,8},{1,17},{9,25},{17,1},{25,9},{2,18},{10... | collective-permute-start | bytes 1572872 | tf_op jit(solution)/shard_map/ppermute | solution.py:968
  69.0 49.0 %collective-permute-start.19 = (bf16[2048,512]{1,0:T(8,128)(2,1)}, bf16[2048,512]{1,0:T(8,128)(2,1)}, u32[]{:S(2)}, u32[]{:S(2)}) collective-permute-start(bf16[2048,512]{1,0:T(8,128)(2,1)} %refs_0_.3), channel_id=1, source_target_pairs={{0,16},{8,24},{16,0},{24,8},{1,17},{9,25},{17,1},{25,9},{2,18},{10... | collective-permute-start | bytes 6291464 | tf_op jit(solution)/shard_map/ppermute | solution.py:968
  69.5 90.6 %collective-permute-start.17 = (bf16[512,2048]{1,0:T(8,128)(2,1)S(1)}, bf16[512,2048]{1,0:T(8,128)(2,1)}, u32[]{:S(2)}, u32[]{:S(2)}) collective-permute-start(bf16[512,2048]{1,0:T(8,128)(2,1)S(1)} %copy-done.22), channel_id=1, source_target_pairs={{0,16},{8,24},{16,0},{24,8},{1,17},{9,25},{17,1},{25,9},{2,18},{10... | collective-permute-start | bytes 6291464 | tf_op jit(solution)/shard_map/ppermute | solution.py:968
  71.1 2.7 collective-permute-start.11
  71.6 88.5 %collective-permute-start.14 = (bf16[256,2048]{1,0:T(8,128)(2,1)}, bf16[256,2048]{1,0:T(8,128)(2,1)S(1)}, u32[]{:S(2)}, u32[]{:S(2)}) collective-permute-start(bf16[256,2048]{1,0:T(8,128)(2,1)} %collective-permute-done.9.refs_2_), channel_id=1, source_target_pairs={{0,4},{4,0},{1,5},{5,1},{2,6},{6,2},{3,7},{7,3},{8,12},{12,8},{9,1... | collective-permute-start | bytes 3145736 | tf_op jit(solution)/shard_map/ppermute | solution.py:968
  80.3 218.2 %all-reduce.5.cloned.1.call-start = ((), (), s32[]{:S(2)}) async-start(), calls=%async_computation.4 | async-start | bytes 4194304 | tf_op jit(solution)/shard_map/psum | solution.py:1156
  117.9 50.1 %collective-permute-start.20 = (bf16[2048,512]{1,0:T(8,128)(2,1)}, bf16[2048,512]{1,0:T(8,128)(2,1)}, u32[]{:S(2)}, u32[]{:S(2)}) collective-permute-start(bf16[2048,512]{1,0:T(8,128)(2,1)} %collective-permute-done.19.refs_12_.refs_2_), channel_id=1, source_target_pairs={{0,8},{8,0},{16,24},{24,16},{1,9},{9,1},{17,25},{25,17},{2,10},{10... | collective-permute-start | bytes 6291464 | tf_op jit(solution)/shard_map/ppermute | solution.py:968
  160.0 7.9 %collective-permute-start.18 = (bf16[512,2048]{1,0:T(8,128)(2,1)}, bf16[512,2048]{1,0:T(8,128)(2,1)S(1)}, u32[]{:S(2)}, u32[]{:S(2)}) collective-permute-start(bf16[512,2048]{1,0:T(8,128)(2,1)} %collective-permute-done.17.refs_8_), channel_id=1, source_target_pairs={{0,8},{8,0},{16,24},{24,16},{1,9},{9,1},{17,25},{25,17},{2,10},{10... | collective-permute-start | bytes 6291464 | tf_op jit(solution)/shard_map/ppermute | solution.py:968
  160.1 7.1 %collective-permute-start.15 = (bf16[256,2048]{1,0:T(8,128)(2,1)}, bf16[256,2048]{1,0:T(8,128)(2,1)}, u32[]{:S(2)}, u32[]{:S(2)}) collective-permute-start(bf16[256,2048]{1,0:T(8,128)(2,1)} %collective-permute-done.9.refs_2_), channel_id=1, source_target_pairs={{0,8},{8,0},{16,24},{24,16},{1,9},{9,1},{17,25},{25,17},{2,10},{10... | collective-permute-start | bytes 3145736 | tf_op jit(solution)/shard_map/ppermute | solution.py:968
  160.6 6.8 %collective-permute-start.16 = (bf16[256,2048]{1,0:T(8,128)(2,1)S(1)}, bf16[256,2048]{1,0:T(8,128)(2,1)}, u32[]{:S(2)}, u32[]{:S(2)}) collective-permute-start(bf16[256,2048]{1,0:T(8,128)(2,1)S(1)} %collective-permute-done.14.refs_3_), channel_id=1, source_target_pairs={{0,8},{8,0},{16,24},{24,16},{1,9},{9,1},{17,25},{25,17},{2,10},{10... | collective-permute-start | bytes 3145736 | tf_op jit(solution)/shard_map/ppermute | solution.py:968
  208.3 148.7 %reduce-scatter.3.cloned.1.call-start = ((), (), s32[]{:S(2)}) async-start(), calls=%async_computation.3 | async-start | bytes 2621440 | tf_op jit(solution)/shard_map/reduce_scatter | solution.py:1168
  219.0 5.0 %collective-permute-start.23 = (bf16[48,1024]{1,0:T(8,128)(2,1)S(1)}, bf16[48,1024]{1,0:T(8,128)(2,1)S(1)}, u32[]{:S(2)}, u32[]{:S(2)}) collective-permute-start(bf16[48,1024]{1,0:T(8,128)(2,1)S(1)} %constant_dynamic-slice_fusion.7), channel_id=1, source_target_pairs={{0,4},{4,0},{1,5},{5,1},{2,6},{6,2},{3,7},{7,3},{8,12},{12,8},{9,1... | collective-permute-start | bytes 294920 | tf_op jit(solution)/shard_map/ppermute | solution.py:968
  224.9 7.9 %collective-permute-start.24 = (bf16[48,512]{1,0:T(8,128)(2,1)S(1)}, bf16[48,512]{1,0:T(8,128)(2,1)S(1)}, u32[]{:S(2)}, u32[]{:S(2)}) collective-permute-start(bf16[48,512]{1,0:T(8,128)(2,1)S(1)} %constant_dynamic-slice_fusion.6), channel_id=1, source_target_pairs={{0,1},{1,0},{2,3},{3,2},{4,5},{5,4},{6,7},{7,6},{8,9},{9,8},{10,11... | collective-permute-start | bytes 147464 | tf_op jit(solution)/shard_map/ppermute | solution.py:968
  232.9 12.7 %collective-permute-start.25 = (bf16[48,256]{1,0:T(8,128)(2,1)S(1)}, bf16[48,256]{1,0:T(8,128)(2,1)S(1)}, u32[]{:S(2)}, u32[]{:S(2)}) collective-permute-start(bf16[48,256]{1,0:T(8,128)(2,1)S(1)} %constant_dynamic-slice_fusion.5), channel_id=1, source_target_pairs={{0,2},{1,3},{2,0},{3,1},{4,6},{5,7},{6,4},{7,5},{8,10},{9,11},{10,... | collective-permute-start | bytes 73736 | tf_op jit(solution)/shard_map/ppermute | solution.py:968
  245.6 153.8 %reduce-scatter.5.cloned.1.call-start = ((), (), s32[]{:S(2)}) async-start(), calls=%async_computation.5 | async-start | bytes 2621440 | tf_op jit(solution)/shard_map/reduce_scatter | solution.py:1184
  245.6 3.9 collective-permute-start.26
  246.8 4.8 %collective-permute-start.31 = (bf16[48,1024]{1,0:T(8,128)(2,1)S(1)}, bf16[48,1024]{1,0:T(8,128)(2,1)S(1)}, u32[]{:S(2)}, u32[]{:S(2)}) collective-permute-start(bf16[48,1024]{1,0:T(8,128)(2,1)S(1)} %constant_dynamic-slice_fusion.4), channel_id=1, source_target_pairs={{0,4},{4,0},{1,5},{5,1},{2,6},{6,2},{3,7},{7,3},{8,12},{12,8},{9,1... | collective-permute-start | bytes 294920 | tf_op jit(solution)/shard_map/ppermute | solution.py:968
  249.6 5.3 %collective-permute-start.27 = (bf16[2,48,256]{2,1,0:T(8,128)(2,1)S(1)}, bf16[2,48,256]{2,1,0:T(8,128)(2,1)S(1)}, u32[]{:S(2)}, u32[]{:S(2)}) collective-permute-start(bf16[2,48,256]{2,1,0:T(8,128)(2,1)S(1)} %maximum_select_fusion.10), channel_id=1, source_target_pairs={{0,2},{1,3},{2,0},{3,1},{4,6},{5,7},{6,4},{7,5},{8,10},{9,11},{10,... | collective-permute-start | bytes 147464 | tf_op jit(solution)/shard_map/ppermute | solution.py:968
  251.6 5.5 %collective-permute-start.32 = (bf16[1,48,1024]{2,1,0:T(8,128)(2,1)S(1)}, bf16[1,48,1024]{2,1,0:T(8,128)(2,1)S(1)}, u32[]{:S(2)}, u32[]{:S(2)}) collective-permute-start(bf16[1,48,1024]{2,1,0:T(8,128)(2,1)S(1)} %fusion), channel_id=1, source_target_pairs={{0,16},{8,24},{16,0},{24,8},{1,17},{9,25},{17,1},{25,9},{2,18},{10... | collective-permute-start | bytes 294920 | tf_op jit(solution)/shard_map/ppermute | solution.py:968
  254.9 4.8 %collective-permute-start.28 = (bf16[2,48,512]{2,1,0:T(8,128)(2,1)S(1)}, bf16[2,48,512]{2,1,0:T(8,128)(2,1)S(1)}, u32[]{:S(2)}, u32[]{:S(2)}) collective-permute-start(bf16[2,48,512]{2,1,0:T(8,128)(2,1)S(1)} %maximum_select_fusion.7), channel_id=1, source_target_pairs={{0,1},{1,0},{2,3},{3,2},{4,5},{5,4},{6,7},{7,6},{8,9},{9,8},{10,11... | collective-permute-start | bytes 294920 | tf_op jit(solution)/shard_map/ppermute | solution.py:968
  257.2 7.4 %collective-permute-start.33 = (bf16[2,48,1024]{2,1,0:T(8,128)(2,1)S(1)}, bf16[2,48,1024]{2,1,0:T(8,128)(2,1)S(1)}, u32[]{:S(2)}, u32[]{:S(2)}) collective-permute-start(bf16[2,48,1024]{2,1,0:T(8,128)(2,1)S(1)} %maximum_select_fusion.5), channel_id=1, source_target_pairs={{0,4},{4,0},{1,5},{5,1},{2,6},{6,2},{3,7},{7,3},{8,12},{12,8},{9,1... | collective-permute-start | bytes 589832 | tf_op jit(solution)/shard_map/ppermute | solution.py:968
  259.3 5.5 %collective-permute-start.21 = (s32[1]{0:T(128)}, s32[1]{0:T(128)}, u32[]{:S(2)}, u32[]{:S(2)}) collective-permute-start(s32[1]{0:T(128)} %param.31), channel_id=1, source_target_pairs={{0,8},{8,0},{16,24},{24,16},{1,9},{9,1},{17,25},{25,17},{2,10},{10... | collective-permute-start | bytes 20 | tf_op jit(solution)/shard_map/ppermute | solution.py:968
  259.8 9.9 %collective-permute-start.29 = (bf16[2,48,1024]{2,1,0:T(8,128)(2,1)S(1)}, bf16[2,48,1024]{2,1,0:T(8,128)(2,1)S(1)}, u32[]{:S(2)}, u32[]{:S(2)}) collective-permute-start(bf16[2,48,1024]{2,1,0:T(8,128)(2,1)S(1)} %maximum_select_fusion.4), channel_id=1, source_target_pairs={{0,4},{4,0},{1,5},{5,1},{2,6},{6,2},{3,7},{7,3},{8,12},{12,8},{9,1... | collective-permute-start | bytes 589832 | tf_op jit(solution)/shard_map/ppermute | solution.py:968
  264.7 5.1 %collective-permute-start.34 = (bf16[2,48,2048]{2,1,0:T(8,128)(2,1)S(1)}, bf16[2,48,2048]{2,1,0:T(8,128)(2,1)S(1)}, u32[]{:S(2)}, u32[]{:S(2)}) collective-permute-start(bf16[2,48,2048]{2,1,0:T(8,128)(2,1)S(1)} %maximum_select_fusion.2), channel_id=1, source_target_pairs={{0,8},{8,0},{16,24},{24,16},{1,9},{9,1},{17,25},{25,17},{2,10},{10... | collective-permute-start | bytes 1179656 | tf_op jit(solution)/shard_map/ppermute | solution.py:968
  265.5 3.5 collective-permute-start.22
  314.7 11.5 %collective-permute-start.35 = (bf16[512,256]{1,0:T(8,128)(2,1)}, bf16[512,256]{1,0:T(8,128)(2,1)S(1)}, u32[]{:S(2)}, u32[]{:S(2)}) collective-permute-start(bf16[512,256]{1,0:T(8,128)(2,1)} %get-tuple-element.127), channel_id=1, source_target_pairs={{4,0},{5,1},{6,2},{7,3},{12,8},{13,9},{14,10},{15,11},{20,16},{21,... | collective-permute-start | bytes 786440 | tf_op jit(solution)/shard_map/ppermute | solution.py:1176
  334.4 11.4 %collective-permute-start.36 = (bf16[64,1024]{1,0:T(8,128)(2,1)S(1)}, bf16[64,1024]{1,0:T(8,128)(2,1)S(1)}, u32[]{:S(2)}, u32[]{:S(2)}) collective-permute-start(bf16[64,1024]{1,0:T(8,128)(2,1)S(1)} %constant_dynamic-slice_fusion.3), channel_id=1, source_target_pairs={{0,4},{4,0},{1,5},{5,1},{2,6},{6,2},{3,7},{7,3},{8,12},{12,8},{9,1... | collective-permute-start | bytes 393224 | tf_op jit(solution)/shard_map/ppermute | solution.py:968
  345.8 4.3 %collective-permute-start.37 = (bf16[64,512]{1,0:T(8,128)(2,1)S(1)}, bf16[64,512]{1,0:T(8,128)(2,1)S(1)}, u32[]{:S(2)}, u32[]{:S(2)}) collective-permute-start(bf16[64,512]{1,0:T(8,128)(2,1)S(1)} %constant_dynamic-slice_fusion.2), channel_id=1, source_target_pairs={{0,1},{1,0},{2,3},{3,2},{4,5},{5,4},{6,7},{7,6},{8,9},{9,8},{10,11... | collective-permute-start | bytes 196616 | tf_op jit(solution)/shard_map/ppermute | solution.py:968
  350.2 6.8 %collective-permute-start.38 = (bf16[64,256]{1,0:T(8,128)(2,1)S(1)}, bf16[64,256]{1,0:T(8,128)(2,1)S(1)}, u32[]{:S(2)}, u32[]{:S(2)}) collective-permute-start(bf16[64,256]{1,0:T(8,128)(2,1)S(1)} %constant_dynamic-slice_fusion.1), channel_id=1, source_target_pairs={{0,2},{1,3},{2,0},{3,1},{4,6},{5,7},{6,4},{7,5},{8,10},{9,11},{10,... | collective-permute-start | bytes 98312 | tf_op jit(solution)/shard_map/ppermute | solution.py:968
  359.9 3.9 collective-permute-start.39
  361.4 3.8 collective-permute-start.44
  363.8 7.8 %collective-permute-start.40 = (bf16[2,64,256]{2,1,0:T(8,128)(2,1)S(1)}, bf16[2,64,256]{2,1,0:T(8,128)(2,1)S(1)}, u32[]{:S(2)}, u32[]{:S(2)}) collective-permute-start(bf16[2,64,256]{2,1,0:T(8,128)(2,1)S(1)} %maximum_select_fusion.9), channel_id=1, source_target_pairs={{0,2},{1,3},{2,0},{3,1},{4,6},{5,7},{6,4},{7,5},{8,10},{9,11},{10,... | collective-permute-start | bytes 196616 | tf_op jit(solution)/shard_map/ppermute | solution.py:968
  365.2 6.5 %collective-permute-start.45 = (bf16[1,16,640]{2,1,0:T(8,128)(2,1)S(1)}, bf16[1,16,640]{2,1,0:T(8,128)(2,1)S(1)}, u32[]{:S(2)}, u32[]{:S(2)}) collective-permute-start(bf16[1,16,640]{2,1,0:T(8,128)(2,1)S(1)} %fusion.3), channel_id=1, source_target_pairs={{0,16},{8,24},{16,0},{24,8},{1,17},{9,25},{17,1},{25,9},{2,18},{10... | collective-permute-start | bytes 61448 | tf_op jit(solution)/shard_map/ppermute | solution.py:968
  371.6 12.1 %collective-permute-start.41 = (bf16[2,64,512]{2,1,0:T(8,128)(2,1)S(1)}, bf16[2,64,512]{2,1,0:T(8,128)(2,1)S(1)}, u32[]{:S(2)}, u32[]{:S(2)}) collective-permute-start(bf16[2,64,512]{2,1,0:T(8,128)(2,1)S(1)} %maximum_select_fusion.6), channel_id=1, source_target_pairs={{0,1},{1,0},{2,3},{3,2},{4,5},{5,4},{6,7},{7,6},{8,9},{9,8},{10,11... | collective-permute-start | bytes 393224 | tf_op jit(solution)/shard_map/ppermute | solution.py:968
  371.7 12.2 %collective-permute-start.46 = (bf16[2,16,640]{2,1,0:T(8,128)(2,1)S(1)}, bf16[2,16,640]{2,1,0:T(8,128)(2,1)S(1)}, u32[]{:S(2)}, u32[]{:S(2)}) collective-permute-start(bf16[2,16,640]{2,1,0:T(8,128)(2,1)S(1)} %maximum_select_fusion.11), channel_id=1, source_target_pairs={{0,4},{4,0},{1,5},{5,1},{2,6},{6,2},{3,7},{7,3},{8,12},{12,8},{9,1... | collective-permute-start | bytes 122888 | tf_op jit(solution)/shard_map/ppermute | solution.py:968
  383.9 6.4 %collective-permute-start.42 = (bf16[2,64,1024]{2,1,0:T(8,128)(2,1)S(1)}, bf16[2,64,1024]{2,1,0:T(8,128)(2,1)S(1)}, u32[]{:S(2)}, u32[]{:S(2)}) collective-permute-start(bf16[2,64,1024]{2,1,0:T(8,128)(2,1)S(1)} %maximum_select_fusion.3), channel_id=1, source_target_pairs={{0,4},{4,0},{1,5},{5,1},{2,6},{6,2},{3,7},{7,3},{8,12},{12,8},{9,1... | collective-permute-start | bytes 786440 | tf_op jit(solution)/shard_map/ppermute | solution.py:968
  384.0 6.5 %collective-permute-start.47 = (bf16[2,16,1280]{2,1,0:T(8,128)(2,1)S(1)}, bf16[2,16,1280]{2,1,0:T(8,128)(2,1)S(1)}, u32[]{:S(2)}, u32[]{:S(2)}) collective-permute-start(bf16[2,16,1280]{2,1,0:T(8,128)(2,1)S(1)} %maximum_select_fusion.8), channel_id=1, source_target_pairs={{0,8},{8,0},{16,24},{24,16},{1,9},{9,1},{17,25},{25,17},{2,10},{10... | collective-permute-start | bytes 245768 | tf_op jit(solution)/shard_map/ppermute | solution.py:968
  (31 other events, 154.1 us)
Sparse Core Ops, SparseCore 0:
  80.4 87.5 all-reduce.2
  208.4 90.0 all-reduce.4
  300.8 42.8 reduce-scatter.2
  345.9 47.1 reduce-scatter.4

commit v3 on v2

--- a/solution.py
+++ b/solution.py
@@ -908,16 +908,17 @@
 def place_kernel(sets, *refs, pieces):
     inputs = refs[: len(refs) - len(pieces)]
     outputs = refs[len(inputs) :]
-    slot = pl.program_id(0)
+    slots = outputs[0].shape[0]
     for out in outputs:
         out[...] = jnp.zeros_like(out)
     for sequence in range(inputs[0].shape[0]):
-
-        @pl.when(sets[sequence] == slot)
+        slot = sets[sequence] - pl.program_id(0) * slots
+
+        @pl.when((slot >= 0) & (slot < slots))
         def _():
             for (source, row, column), out in zip(pieces, outputs):
                 piece = inputs[source][sequence, row : row + rank, column : column + out.shape[2]]
-                out[0] += piece.astype(f32)
+                out[slot] += piece.astype(f32)
 
 
 def place_sets(sets, gathered, pieces, slots, weight):
@@ -927,9 +928,11 @@
         name="place_sets",
         grid_spec=pltpu.PrefetchScalarGridSpec(
             num_scalar_prefetch=1,
-            grid=(slots,),
+            grid=(2,),
             in_specs=[fixed(g.shape) for g in gathered],
-            out_specs=[pl.BlockSpec((1,) + s.shape[1:], lambda i, m: (i, 0, 0)) for s in shapes],
+            out_specs=[
+                pl.BlockSpec((slots // 2,) + s.shape[1:], lambda i, m: (i, 0, 0)) for s in shapes
+            ],
         ),
         out_shape=shapes,
         cost_estimate=pl.CostEstimate(flops=weight, transcendentals=0, bytes_accessed=8 * 1024 * 1024),

time: 417 us -> 415 us (level)
  transfers between devices with their start and end apart: 52 -> 52, of which waited for: 28 -> 28; matrix products, arithmetic and copies ran while one was open for 5% -> 5% of each run, Pallas kernels for 26% -> 25%
where the time goes in v3:
time: 415 us; the launch traced here: 408 us
  waiting for transfers between devices  181 us (44%)
  Pallas kernels  144 us (35%)
  starting transfers between devices  42.2 us (10%)
  local copies, waits for them, and re-layouts  15.5 us (4%)
  between operations  15.4 us (4%)
  other arithmetic  9.2 us (2%)
    ppermute x46, waiting for transfers between devices, flip(): return lax.ppermute(array, axis, [(i, i ^ bit) for i in range(count)])  160 us
    pallas_call x1, Pallas kernels, ffn(): pl.pallas_call(partial(ffn_kernel, shards=shards, chunk=chunk), name='fee...  39 us
    ppermute x46, starting transfers between devices, flip(): return lax.ppermute(array, axis, [(i, i ^ bit) for i in range(count)])  37.1 us
    psum x1, waiting for transfers between devices, on_device(): summed = lax.psum(back, 'tp')  20.9 us
    pallas_call x1, Pallas kernels, attention_backward_far(): pl.pallas_call(partial(far_kernel, log_scale=log_scale, block=256), name=...  16.2 us
    pallas_call x1, Pallas kernels, reduce_forward(): pl.pallas_call(reduce_kernel, name='reduce_forward', grid_spec=pltpu.Pref...  11.2 us
    pallas_call x1, Pallas kernels, attention_backward_near(): pl.pallas_call(partial(near_kernel, log_scale=log_scale, block=256), name...  10.2 us
    pallas_call x1, Pallas kernels, attention_forward(): pl.pallas_call(partial(attention_kernel, log_scale=log_scale, block=block...  9.78 us
  transfers between devices with their start and end apart: 52, of which 28 were waited for; matrix products, arithmetic and copies ran while one was open for 5% of the time, Pallas kernels for 25%

profile of v3, /device:TPU:0, one launch (start us, length us, event | category | flops | bytes accessed | tf_op | source)
XLA Modules:
  0.0 407.9 jit_solution(830234049652967388)
XLA Ops:
  8.3 2.6 collective-permute-start
  15.4 5.0 %attention_norm.1 = (bf16[512,2048]{1,0:T(8,128)(2,1)}, bf16[512,128]{1,0:T(8,128)(2,1)}) custom-call(s32[16]{0:T(128)} %stack.73.meta, bf16[512,2048]{1,0:T(8,128)(2,1)} %bitcast.36, bf16[1,2048]{1,0:T(2,128)(2,1)} %broadcast_in_dim.26.gain, bf16[8,16,2048]{2,1,0:T(8,128)(2,1)} %bitcast.45, bf16[8,16,2048]{2,1,0:T(8,128)(2,1)} %bitcast.47, ...), custom_call_target="tpu_custom_call" | custom-call | flops 1024 | bytes 1024 | tf_op jit(solution)/shard_map/attention_norm/pallas_call | solution.py:98
  23.6 2.3 constant_dynamic-slice_fusion.8
  25.9 6.1 %collective-permute-done.6.kv2 = bf16[512,256]{1,0:T(8,128)(2,1)S(1)} collective-permute-done((bf16[512,256]{1,0:T(8,128)(2,1)S(1)}, bf16[512,256]{1,0:T(8,128)(2,1)S(1)}, u32[]{:S(2)}, u32[]{:S(2)}) %collective-permute-start.6) | collective-permute-done | bytes 262176 | tf_op jit(solution)/shard_map/ppermute | solution.py:971
  37.2 7.6 %qkv_forward.1 = (f32[512,640]{1,0:T(8,128)}, bf16[512,512]{1,0:T(8,128)(2,1)}, bf16[512,384]{1,0:T(8,128)(2,1)}) custom-call(s32[16]{0:T(128)} %stack.73.meta, bf16[512,2048]{1,0:T(8,128)(2,1)} %get-tuple-element.80.normed, bf16[512,128]{1,0:T(8,128)(2,1)} %get-tuple-element.81.narrow, bf16[512,512]{1,0:T(8,128)(2,1)} %q0.3, bf16[512,512]{1,0:T(8,128)(2,1)} %copy-done.6, ...), custom_call_target="tpu_custom_call" | custom-call | flops 1024 | bytes 1024 | tf_op jit(solution)/shard_map/qkv_forward/pallas_call | solution.py:154
  44.8 3.7 collective-permute-start.10
  48.6 1.6 collective-permute-start.12
  50.1 8.3 %collective-permute-done.9.refs_2_ = bf16[256,2048]{1,0:T(8,128)(2,1)} collective-permute-done((bf16[256,2048]{1,0:T(8,128)(2,1)}, bf16[256,2048]{1,0:T(8,128)(2,1)}, u32[]{:S(2)}, u32[]{:S(2)}) %collective-permute-start.9) | collective-permute-done | bytes 1048608 | tf_op jit(solution)/shard_map/ppermute | solution.py:971
  59.2 9.8 %attention_forward.1 = (bf16[512,512]{1,0:T(8,128)(2,1)}, f32[512,512]{1,0:T(8,128)}, f32[512,512]{1,0:T(8,128)}) custom-call(s32[16]{0:T(128)} %stack.73.meta, bf16[512,512]{1,0:T(8,128)(2,1)} %get-tuple-element.89.qrot, bf16[512,384]{1,0:T(8,128)(2,1)} %copy-done.12, bf16[512,384]{1,0:T(8,128)(2,1)} %get-tuple-element.90.kvn.kvq.kv, ...), custom_call_target="tpu_custom_call" | custom-call | flops 17179869184 | bytes 67108864 | tf_op jit(solution)/shard_map/attention_forward/pallas_call | solution.py:245
  69.5 1.6 collective-permute-start.17
  71.6 1.5 collective-permute-start.14
  74.5 5.7 %output_forward.1 = (bf16[512,2048]{1,0:T(8,128)(2,1)}, bf16[512,128]{1,0:T(8,128)(2,1)}) custom-call(s32[16]{0:T(128)} %stack.73.meta, bf16[512,512]{1,0:T(8,128)(2,1)} %get-tuple-element.91.att, bf16[512,512]{1,0:T(8,128)(2,1)} %w0.3, bf16[512,512]{1,0:T(8,128)(2,1)} %copy-done.3, bf16[512,512]{1,0:T(8,128)(2,1)} %copy-done.1, bf16[512,512]{1,0:T(8,128)(2,1)} %copy-done.2, ...), custom_call_target="tpu_custom_call" | custom-call | flops 1024 | bytes 1024 | tf_op jit(solution)/shard_map/output_forward/pallas_call | solution.py:298
  80.3 37.6 %collective-permute-done.19.refs_12_.refs_2_ = bf16[2048,512]{1,0:T(8,128)(2,1)} collective-permute-done((bf16[2048,512]{1,0:T(8,128)(2,1)}, bf16[2048,512]{1,0:T(8,128)(2,1)}, u32[]{:S(2)}, u32[]{:S(2)}) %collective-permute-start.19) | collective-permute-done | bytes 2097184 | tf_op jit(solution)/shard_map/ppermute | solution.py:971
  117.9 42.1 %collective-permute-done.17.refs_8_ = bf16[512,2048]{1,0:T(8,128)(2,1)} collective-permute-done((bf16[512,2048]{1,0:T(8,128)(2,1)S(1)}, bf16[512,2048]{1,0:T(8,128)(2,1)}, u32[]{:S(2)}, u32[]{:S(2)}) %collective-permute-start.17) | collective-permute-done | bytes 2097184 | tf_op jit(solution)/shard_map/ppermute | solution.py:971
  160.6 6.5 %collective-permute-done.15.refs_4_ = bf16[256,2048]{1,0:T(8,128)(2,1)} collective-permute-done((bf16[256,2048]{1,0:T(8,128)(2,1)}, bf16[256,2048]{1,0:T(8,128)(2,1)}, u32[]{:S(2)}, u32[]{:S(2)}) %collective-permute-start.15) | collective-permute-done | bytes 1048608 | tf_op jit(solution)/shard_map/ppermute | solution.py:971
  169.3 39.0 %feed_forward.1 = (bf16[512,2048]{1,0:T(8,128)(2,1)}, bf16[512,2048]{1,0:T(8,128)(2,1)}, bf16[512,2048]{1,0:T(8,128)(2,1)}, bf16[512,2048]{1,0:T(8,128)(2,1)}, b...) custom-call(s32[16]{0:T(128)} %stack.73.meta, bf16[512,2048]{1,0:T(8,128)(2,1)} %bitcast.37, ...), custom_call_target="tpu_custom_call" | custom-call | flops 17179869184 | bytes 31457280 | tf_op jit(solution)/shard_map/feed_forward/pallas_call | solution.py:426
  208.4 9.7 %feed_forward_adapters.1 = (bf16[48,2048]{1,0:T(8,128)(2,1)}, bf16[48,2048]{1,0:T(8,128)(2,1)}, bf16[512,128]{1,0:T(8,128)(2,1)}) custom-call(s32[16]{0:T(128)} %stack.73.meta, bf16[512,2048]{1,0:T(8,128)(2,1)} %bitcast.38, bf16[512,2048]{1,0:T(8,128)(2,1)} %all-reduce.3.cloned.1.call-done.branch.second, bf16[512,2048]{1,0:T(8,128)(2,1)} %bitcast.42, ...), custom_call_target="tpu_custom_call" | custom-call | flops 536870912 | bytes 12582912 | tf_op jit(solution)/shard_map/feed_forward_adapters/pallas_call | solution.py:499
  219.0 1.9 collective-permute-start.23
  220.9 3.1 collective-permute-done.23
  224.9 1.7 collective-permute-start.24
  226.6 6.2 %collective-permute-done.24 = bf16[48,512]{1,0:T(8,128)(2,1)S(1)} collective-permute-done((bf16[48,512]{1,0:T(8,128)(2,1)S(1)}, bf16[48,512]{1,0:T(8,128)(2,1)S(1)}, u32[]{:S(2)}, u32[]{:S(2)}) %collective-permute-start.24) | collective-permute-done | bytes 49184 | tf_op jit(solution)/shard_map/ppermute | solution.py:971
  232.9 1.4 collective-permute-start.25
  234.3 11.2 %reduce_forward.1 = bf16[512,2048]{1,0:T(8,128)(2,1)} custom-call(s32[16]{0:T(128)} %stack.73.meta, bf16[512,2048]{1,0:T(8,128)(2,1)} %get-tuple-element.100.inner, bf16[512,128]{1,0:T(8,128)(2,1)} %get-tuple-element.106.n_r, bf16[2048,512]{1,0:T(8,128)(2,1)} %refs_0_.3, bf16[2048,512]{1,0:T(8,128)(2,1)} %collective-permute-done.4.refs_11_.refs_1_, ...), custom_call_target="tpu_custom_call" | custom-call | flops 4294967296 | bytes 12582912 | tf_op jit(solution)/shard_map/reduce_forward/pallas_call | solution.py:539
  246.8 2.2 collective-permute-start.31
  249.6 1.7 collective-permute-start.27
  252.6 2.3 collective-permute-done.27
  254.9 2.2 collective-permute-start.28
  257.2 2.2 collective-permute-start.33
  259.8 2.2 collective-permute-start.29
  262.0 2.6 collective-permute-done.33
  266.6 2.5 collective-permute-done.22
  272.6 5.0 %place_sets.2 = (f32[8,16,2048]{2,1,0:T(8,128)}, f32[8,16,2048]{2,1,0:T(8,128)}, f32[8,16,2048]{2,1,0:T(8,128)}, f32[8,16,2048]{2,1,0:T(8,128)}, f32[8,16,2048]{2,1,0:T(8,128)}, /*index=5*/f32[8,16,2048]{2,1,0:T(8,128)}) custom-call(s32[4]{0:T(128)} %broadcast_select_fusion.17.sets, bf16[4,48,2048]{2,1,0:T(8,128)(2,1)} %pad_maximum_fusion.1.refs_0_, ...), custom_call_target="tpu_custom_call" | custom-call | flops 1024 | bytes 8388608 | tf_op jit(solution)/shard_map/place_sets/pallas_call | solution.py:926
  277.6 20.9 %all-reduce.5.cloned.1.call-done.summed.second = bf16[512,2048]{1,0:T(8,128)(2,1)} async-done(((bf16[512,2048]{1,0:T(8,128)(2,1)}), bf16[512,2048]{1,0:T(8,128)(2,1)}) %all-reduce.5.cloned.1.call-update) | async-done | bytes 2097168 | tf_op jit(solution)/shard_map/psum | solution.py:1159
  298.5 16.2 %attention_backward_far.1 = (bf16[512,512]{1,0:T(8,128)(2,1)}, bf16[512,512]{1,0:T(8,128)(2,1)}, f32[512,512]{1,0:T(8,128)}, bf16[512,256]{1,0:T(8,128)(2,1)}, b...) custom-call(s32[16]{0:T(128)} %stack.73.meta, bf16[512,2048]{1,0:T(8,128)(2,1)} %bitcast.43, ...), custom_call_target="tpu_custom_call" | custom-call | flops 2684354560 | bytes 16777216 | tf_op jit(solution)/shard_map/attention_backward_far/pallas_call | solution.py:719
  316.0 10.2 %attention_backward_near.1 = (f32[512,512]{1,0:T(8,128)}, f32[512,256]{1,0:T(8,128)}) custom-call(s32[16]{0:T(128)} %stack.73.meta, bf16[512,512]{1,0:T(8,128)(2,1)} %get-tuple-element.122.dop, bf16[512,512]{1,0:T(8,128)(2,1)} %get-tuple-element.123.mixed, bf16[512,512]{1,0:T(8,128)(2,1)} %get-tuple-element.89.qrot, ...), custom_call_target="tpu_custom_call" | custom-call | flops 2684354560 | bytes 6291456 | tf_op jit(solution)/shard_map/attention_backward_near/pallas_call | solution.py:747
  326.9 6.5 %qkv_grads.1 = (bf16[512,768]{1,0:T(8,128)(2,1)}, bf16[512,128]{1,0:T(8,128)(2,1)}, bf16[48,2048]{1,0:T(8,128)(2,1)}, bf16[16,512]{1,0:T(8,128)(2,1)}, bf16[16,256]{1,0:T(8,128)(2,1)}) custom-call(s32[16]{0:T(128)} %stack.73.meta, bf16[512,2048]{1,0:T(8,128)(2,1)} %get-tuple-element.80.normed, bf16[512,128]{1,0:T(8,128)(2,1)} %get-tuple-element.81.narrow, ...), custom_call_target="tpu_custom_call" | custom-call | flops 201326592 | bytes 8388608 | tf_op jit(solution)/shard_map/qkv_grads/pallas_call | solution.py:820
  334.4 2.8 collective-permute-start.36
  337.1 7.9 %qkv_backward.1 = bf16[512,2048]{1,0:T(8,128)(2,1)} custom-call(s32[16]{0:T(128)} %stack.73.meta, bf16[512,2048]{1,0:T(8,128)(2,1)} %bitcast.39, bf16[1,2048]{1,0:T(2,128)(2,1)} %broadcast_in_dim.26.gain, bf16[512,768]{1,0:T(8,128)(2,1)} %get-tuple-element.128.grad, bf16[512,128]{1,0:T(8,128)(2,1)} %get-tuple-element.129.low, bf16[512,512]{1,0:T(8,128)(2,1)} %q0.3, ...), custom_call_target="tpu_custom_call" | custom-call | flops 1610612736 | bytes 8388608 | tf_op jit(solution)/shard_map/qkv_backward/pallas_call | solution.py:888
  346.0 4.2 %collective-permute-done.37 = bf16[64,512]{1,0:T(8,128)(2,1)S(1)} collective-permute-done((bf16[64,512]{1,0:T(8,128)(2,1)S(1)}, bf16[64,512]{1,0:T(8,128)(2,1)S(1)}, u32[]{:S(2)}, u32[]{:S(2)}) %collective-permute-start.37) | collective-permute-done | bytes 65568 | tf_op jit(solution)/shard_map/ppermute | solution.py:971
  351.5 5.4 %collective-permute-done.38 = bf16[64,256]{1,0:T(8,128)(2,1)S(1)} collective-permute-done((bf16[64,256]{1,0:T(8,128)(2,1)S(1)}, bf16[64,256]{1,0:T(8,128)(2,1)S(1)}, u32[]{:S(2)}, u32[]{:S(2)}) %collective-permute-start.38) | collective-permute-done | bytes 32800 | tf_op jit(solution)/shard_map/ppermute | solution.py:971
  357.0 2.9 close.2
  359.9 1.5 collective-permute-start.39
  361.4 2.4 collective-permute-done.39
  365.8 5.8 %collective-permute-done.40 = bf16[2,64,256]{2,1,0:T(8,128)(2,1)S(1)} collective-permute-done((bf16[2,64,256]{2,1,0:T(8,128)(2,1)S(1)}, bf16[2,64,256]{2,1,0:T(8,128)(2,1)S(1)}, u32[]{:S(2)}, u32[]{:S(2)}) %collective-permute-start.40) | collective-permute-done | bytes 65568 | tf_op jit(solution)/shard_map/ppermute | solution.py:971
  371.8 12.0 %collective-permute-done.41 = bf16[2,64,512]{2,1,0:T(8,128)(2,1)S(1)} collective-permute-done((bf16[2,64,512]{2,1,0:T(8,128)(2,1)S(1)}, bf16[2,64,512]{2,1,0:T(8,128)(2,1)S(1)}, u32[]{:S(2)}, u32[]{:S(2)}) %collective-permute-start.41) | collective-permute-done | bytes 131104 | tf_op jit(solution)/shard_map/ppermute | solution.py:971
  384.1 6.2 %collective-permute-done.42 = bf16[2,64,1024]{2,1,0:T(8,128)(2,1)S(1)} collective-permute-done((bf16[2,64,1024]{2,1,0:T(8,128)(2,1)S(1)}, bf16[2,64,1024]{2,1,0:T(8,128)(2,1)S(1)}, u32[]{:S(2)}, u32[]{:S(2)}) %collective-permute-start.42) | collective-permute-done | bytes 262176 | tf_op jit(solution)/shard_map/ppermute | solution.py:971
  393.6 4.4 %place_sets.3 = (f32[8,16,2048]{2,1,0:T(8,128)}, f32[8,16,2048]{2,1,0:T(8,128)}, f32[8,16,2048]{2,1,0:T(8,128)}, f32[8,16,2048]{2,1,0:T(8,128)}, f32[8,16,512]{2...) custom-call(s32[4]{0:T(128)} %broadcast_select_fusion.17.sets, ...), custom_call_target="tpu_custom_call" | custom-call | flops 8589934592 | bytes 8388608 | tf_op jit(solution)/shard_map/place_sets/pallas_call | solution.py:926
  398.0 2.9 close.3
  (188 shorter events, 41.3 us)
Async XLA Ops:
  7.2 160.8 %all-reduce.3.cloned.1.call-start = ((), (), s32[]{:S(2)}) async-start(), calls=%async_computation.2 | async-start | bytes 4194304 | tf_op jit(solution)/shard_map/psum | solution.py:1153
  7.2 25.1 %collective-permute-start.4 = (bf16[2048,512]{1,0:T(8,128)(2,1)}, bf16[2048,512]{1,0:T(8,128)(2,1)}, u32[]{:S(2)}, u32[]{:S(2)}) collective-permute-start(bf16[2048,512]{1,0:T(8,128)(2,1)} %refs_0_.3), channel_id=1, source_target_pairs={{0,8},{8,0},{16,24},{24,16},{1,9},{9,1},{17,25},{25,17},{2,10},{10... | collective-permute-start | bytes 6291464 | tf_op jit(solution)/shard_map/ppermute | solution.py:971
  7.7 24.6 %collective-permute-start.2 = (bf16[512,2048]{1,0:T(8,128)(2,1)}, bf16[512,2048]{1,0:T(8,128)(2,1)}, u32[]{:S(2)}, u32[]{:S(2)}) collective-permute-start(bf16[512,2048]{1,0:T(8,128)(2,1)} %refs_0_.2), channel_id=1, source_target_pairs={{0,8},{8,0},{16,24},{24,16},{1,9},{9,1},{17,25},{25,17},{2,10},{10... | collective-permute-start | bytes 6291464 | tf_op jit(solution)/shard_map/ppermute | solution.py:971
  7.8 24.5 %collective-permute-start.3 = (bf16[512,2048]{1,0:T(8,128)(2,1)}, bf16[512,2048]{1,0:T(8,128)(2,1)}, u32[]{:S(2)}, u32[]{:S(2)}) collective-permute-start(bf16[512,2048]{1,0:T(8,128)(2,1)} %refs_6_.1), channel_id=1, source_target_pairs={{0,8},{8,0},{16,24},{24,16},{1,9},{9,1},{17,25},{25,17},{2,10},{10... | collective-permute-start | bytes 6291464 | tf_op jit(solution)/shard_map/ppermute | solution.py:971
  8.3 23.7 %collective-permute-start = (bf16[512,512]{1,0:T(8,128)(2,1)}, bf16[512,512]{1,0:T(8,128)(2,1)S(1)}, u32[]{:S(2)}, u32[]{:S(2)}) collective-permute-start(bf16[512,512]{1,0:T(8,128)(2,1)} %q0.3), channel_id=1, source_target_pairs={{0,16},{8,24},{16,0},{24,8},{1,17},{9,25},{17,1},{25,9},{2,18},{10... | collective-permute-start | bytes 1572872 | tf_op jit(solution)/shard_map/ppermute | solution.py:971
  23.6 8.4 %collective-permute-start.6 = (bf16[512,256]{1,0:T(8,128)(2,1)S(1)}, bf16[512,256]{1,0:T(8,128)(2,1)S(1)}, u32[]{:S(2)}, u32[]{:S(2)}) collective-permute-start(bf16[512,256]{1,0:T(8,128)(2,1)S(1)} %constant_dynamic-update-slice_fusion.kv0), channel_id=1, source_target_pairs={{0,16},{8,24},{16,0},{24,8},{1,17},{9,25},{17,1},{25,9},{2,18},{10... | collective-permute-start | bytes 786440 | tf_op jit(solution)/shard_map/ppermute | solution.py:971
  32.0 26.5 %collective-permute-start.9 = (bf16[256,2048]{1,0:T(8,128)(2,1)}, bf16[256,2048]{1,0:T(8,128)(2,1)}, u32[]{:S(2)}, u32[]{:S(2)}) collective-permute-start(bf16[256,2048]{1,0:T(8,128)(2,1)} %constant_dynamic-slice_fusion.8), channel_id=1, source_target_pairs={{0,16},{8,24},{16,0},{24,8},{1,17},{9,25},{17,1},{25,9},{2,18},{10... | collective-permute-start | bytes 3145736 | tf_op jit(solution)/shard_map/ppermute | solution.py:971
  32.3 3.0 collective-permute-start.1
  32.3 3.4 collective-permute-start.5
  33.0 2.7 collective-permute-start.8
  44.8 13.6 %collective-permute-start.10 = (bf16[512,384]{1,0:T(8,128)(2,1)}, bf16[512,384]{1,0:T(8,128)(2,1)S(1)}, u32[]{:S(2)}, u32[]{:S(2)}) collective-permute-start(bf16[512,384]{1,0:T(8,128)(2,1)} %get-tuple-element.90.kvn.kvq.kv), channel_id=1, source_target_pairs={{0,4},{1,5},{2,6},{3,7},{8,12},{9,13},{10,14},{11,15},{16,20},{17,... | collective-permute-start | bytes 1179656 | tf_op jit(solution)/shard_map/ppermute | solution.py:1134
  48.6 20.4 %collective-permute-start.12 = (bf16[512,512]{1,0:T(8,128)(2,1)S(1)}, bf16[512,512]{1,0:T(8,128)(2,1)S(1)}, u32[]{:S(2)}, u32[]{:S(2)}) collective-permute-start(bf16[512,512]{1,0:T(8,128)(2,1)S(1)} %copy-done), channel_id=1, source_target_pairs={{0,16},{8,24},{16,0},{24,8},{1,17},{9,25},{17,1},{25,9},{2,18},{10... | collective-permute-start | bytes 1572872 | tf_op jit(solution)/shard_map/ppermute | solution.py:971
  69.0 49.0 %collective-permute-start.19 = (bf16[2048,512]{1,0:T(8,128)(2,1)}, bf16[2048,512]{1,0:T(8,128)(2,1)}, u32[]{:S(2)}, u32[]{:S(2)}) collective-permute-start(bf16[2048,512]{1,0:T(8,128)(2,1)} %refs_0_.3), channel_id=1, source_target_pairs={{0,16},{8,24},{16,0},{24,8},{1,17},{9,25},{17,1},{25,9},{2,18},{10... | collective-permute-start | bytes 6291464 | tf_op jit(solution)/shard_map/ppermute | solution.py:971
  69.5 90.6 %collective-permute-start.17 = (bf16[512,2048]{1,0:T(8,128)(2,1)S(1)}, bf16[512,2048]{1,0:T(8,128)(2,1)}, u32[]{:S(2)}, u32[]{:S(2)}) collective-permute-start(bf16[512,2048]{1,0:T(8,128)(2,1)S(1)} %copy-done.22), channel_id=1, source_target_pairs={{0,16},{8,24},{16,0},{24,8},{1,17},{9,25},{17,1},{25,9},{2,18},{10... | collective-permute-start | bytes 6291464 | tf_op jit(solution)/shard_map/ppermute | solution.py:971
  71.1 2.7 collective-permute-start.11
  71.6 88.5 %collective-permute-start.14 = (bf16[256,2048]{1,0:T(8,128)(2,1)}, bf16[256,2048]{1,0:T(8,128)(2,1)S(1)}, u32[]{:S(2)}, u32[]{:S(2)}) collective-permute-start(bf16[256,2048]{1,0:T(8,128)(2,1)} %collective-permute-done.9.refs_2_), channel_id=1, source_target_pairs={{0,4},{4,0},{1,5},{5,1},{2,6},{6,2},{3,7},{7,3},{8,12},{12,8},{9,1... | collective-permute-start | bytes 3145736 | tf_op jit(solution)/shard_map/ppermute | solution.py:971
  80.3 218.2 %all-reduce.5.cloned.1.call-start = ((), (), s32[]{:S(2)}) async-start(), calls=%async_computation.4 | async-start | bytes 4194304 | tf_op jit(solution)/shard_map/psum | solution.py:1159
  117.9 50.1 %collective-permute-start.20 = (bf16[2048,512]{1,0:T(8,128)(2,1)}, bf16[2048,512]{1,0:T(8,128)(2,1)}, u32[]{:S(2)}, u32[]{:S(2)}) collective-permute-start(bf16[2048,512]{1,0:T(8,128)(2,1)} %collective-permute-done.19.refs_12_.refs_2_), channel_id=1, source_target_pairs={{0,8},{8,0},{16,24},{24,16},{1,9},{9,1},{17,25},{25,17},{2,10},{10... | collective-permute-start | bytes 6291464 | tf_op jit(solution)/shard_map/ppermute | solution.py:971
  160.0 7.9 %collective-permute-start.18 = (bf16[512,2048]{1,0:T(8,128)(2,1)}, bf16[512,2048]{1,0:T(8,128)(2,1)S(1)}, u32[]{:S(2)}, u32[]{:S(2)}) collective-permute-start(bf16[512,2048]{1,0:T(8,128)(2,1)} %collective-permute-done.17.refs_8_), channel_id=1, source_target_pairs={{0,8},{8,0},{16,24},{24,16},{1,9},{9,1},{17,25},{25,17},{2,10},{10... | collective-permute-start | bytes 6291464 | tf_op jit(solution)/shard_map/ppermute | solution.py:971
  160.1 7.1 %collective-permute-start.15 = (bf16[256,2048]{1,0:T(8,128)(2,1)}, bf16[256,2048]{1,0:T(8,128)(2,1)}, u32[]{:S(2)}, u32[]{:S(2)}) collective-permute-start(bf16[256,2048]{1,0:T(8,128)(2,1)} %collective-permute-done.9.refs_2_), channel_id=1, source_target_pairs={{0,8},{8,0},{16,24},{24,16},{1,9},{9,1},{17,25},{25,17},{2,10},{10... | collective-permute-start | bytes 3145736 | tf_op jit(solution)/shard_map/ppermute | solution.py:971
  160.6 6.8 %collective-permute-start.16 = (bf16[256,2048]{1,0:T(8,128)(2,1)S(1)}, bf16[256,2048]{1,0:T(8,128)(2,1)}, u32[]{:S(2)}, u32[]{:S(2)}) collective-permute-start(bf16[256,2048]{1,0:T(8,128)(2,1)S(1)} %collective-permute-done.14.refs_3_), channel_id=1, source_target_pairs={{0,8},{8,0},{16,24},{24,16},{1,9},{9,1},{17,25},{25,17},{2,10},{10... | collective-permute-start | bytes 3145736 | tf_op jit(solution)/shard_map/ppermute | solution.py:971
  208.3 148.7 %reduce-scatter.3.cloned.1.call-start = ((), (), s32[]{:S(2)}) async-start(), calls=%async_computation.3 | async-start | bytes 2621440 | tf_op jit(solution)/shard_map/reduce_scatter | solution.py:1171
  219.0 5.0 %collective-permute-start.23 = (bf16[48,1024]{1,0:T(8,128)(2,1)S(1)}, bf16[48,1024]{1,0:T(8,128)(2,1)S(1)}, u32[]{:S(2)}, u32[]{:S(2)}) collective-permute-start(bf16[48,1024]{1,0:T(8,128)(2,1)S(1)} %constant_dynamic-slice_fusion.7), channel_id=1, source_target_pairs={{0,4},{4,0},{1,5},{5,1},{2,6},{6,2},{3,7},{7,3},{8,12},{12,8},{9,1... | collective-permute-start | bytes 294920 | tf_op jit(solution)/shard_map/ppermute | solution.py:971
  224.9 7.9 %collective-permute-start.24 = (bf16[48,512]{1,0:T(8,128)(2,1)S(1)}, bf16[48,512]{1,0:T(8,128)(2,1)S(1)}, u32[]{:S(2)}, u32[]{:S(2)}) collective-permute-start(bf16[48,512]{1,0:T(8,128)(2,1)S(1)} %constant_dynamic-slice_fusion.6), channel_id=1, source_target_pairs={{0,1},{1,0},{2,3},{3,2},{4,5},{5,4},{6,7},{7,6},{8,9},{9,8},{10,11... | collective-permute-start | bytes 147464 | tf_op jit(solution)/shard_map/ppermute | solution.py:971
  232.9 12.7 %collective-permute-start.25 = (bf16[48,256]{1,0:T(8,128)(2,1)S(1)}, bf16[48,256]{1,0:T(8,128)(2,1)S(1)}, u32[]{:S(2)}, u32[]{:S(2)}) collective-permute-start(bf16[48,256]{1,0:T(8,128)(2,1)S(1)} %constant_dynamic-slice_fusion.5), channel_id=1, source_target_pairs={{0,2},{1,3},{2,0},{3,1},{4,6},{5,7},{6,4},{7,5},{8,10},{9,11},{10,... | collective-permute-start | bytes 73736 | tf_op jit(solution)/shard_map/ppermute | solution.py:971
  245.6 152.4 %reduce-scatter.5.cloned.1.call-start = ((), (), s32[]{:S(2)}) async-start(), calls=%async_computation.5 | async-start | bytes 2621440 | tf_op jit(solution)/shard_map/reduce_scatter | solution.py:1187
  245.6 3.9 collective-permute-start.26
  246.8 4.8 %collective-permute-start.31 = (bf16[48,1024]{1,0:T(8,128)(2,1)S(1)}, bf16[48,1024]{1,0:T(8,128)(2,1)S(1)}, u32[]{:S(2)}, u32[]{:S(2)}) collective-permute-start(bf16[48,1024]{1,0:T(8,128)(2,1)S(1)} %constant_dynamic-slice_fusion.4), channel_id=1, source_target_pairs={{0,4},{4,0},{1,5},{5,1},{2,6},{6,2},{3,7},{7,3},{8,12},{12,8},{9,1... | collective-permute-start | bytes 294920 | tf_op jit(solution)/shard_map/ppermute | solution.py:971
  249.6 5.3 %collective-permute-start.27 = (bf16[2,48,256]{2,1,0:T(8,128)(2,1)S(1)}, bf16[2,48,256]{2,1,0:T(8,128)(2,1)S(1)}, u32[]{:S(2)}, u32[]{:S(2)}) collective-permute-start(bf16[2,48,256]{2,1,0:T(8,128)(2,1)S(1)} %maximum_select_fusion.10), channel_id=1, source_target_pairs={{0,2},{1,3},{2,0},{3,1},{4,6},{5,7},{6,4},{7,5},{8,10},{9,11},{10,... | collective-permute-start | bytes 147464 | tf_op jit(solution)/shard_map/ppermute | solution.py:971
  251.6 5.5 %collective-permute-start.32 = (bf16[1,48,1024]{2,1,0:T(8,128)(2,1)S(1)}, bf16[1,48,1024]{2,1,0:T(8,128)(2,1)S(1)}, u32[]{:S(2)}, u32[]{:S(2)}) collective-permute-start(bf16[1,48,1024]{2,1,0:T(8,128)(2,1)S(1)} %fusion), channel_id=1, source_target_pairs={{0,16},{8,24},{16,0},{24,8},{1,17},{9,25},{17,1},{25,9},{2,18},{10... | collective-permute-start | bytes 294920 | tf_op jit(solution)/shard_map/ppermute | solution.py:971
  254.9 4.8 %collective-permute-start.28 = (bf16[2,48,512]{2,1,0:T(8,128)(2,1)S(1)}, bf16[2,48,512]{2,1,0:T(8,128)(2,1)S(1)}, u32[]{:S(2)}, u32[]{:S(2)}) collective-permute-start(bf16[2,48,512]{2,1,0:T(8,128)(2,1)S(1)} %maximum_select_fusion.7), channel_id=1, source_target_pairs={{0,1},{1,0},{2,3},{3,2},{4,5},{5,4},{6,7},{7,6},{8,9},{9,8},{10,11... | collective-permute-start | bytes 294920 | tf_op jit(solution)/shard_map/ppermute | solution.py:971
  257.2 7.4 %collective-permute-start.33 = (bf16[2,48,1024]{2,1,0:T(8,128)(2,1)S(1)}, bf16[2,48,1024]{2,1,0:T(8,128)(2,1)S(1)}, u32[]{:S(2)}, u32[]{:S(2)}) collective-permute-start(bf16[2,48,1024]{2,1,0:T(8,128)(2,1)S(1)} %maximum_select_fusion.5), channel_id=1, source_target_pairs={{0,4},{4,0},{1,5},{5,1},{2,6},{6,2},{3,7},{7,3},{8,12},{12,8},{9,1... | collective-permute-start | bytes 589832 | tf_op jit(solution)/shard_map/ppermute | solution.py:971
  259.3 5.5 %collective-permute-start.21 = (s32[1]{0:T(128)}, s32[1]{0:T(128)}, u32[]{:S(2)}, u32[]{:S(2)}) collective-permute-start(s32[1]{0:T(128)} %param.31), channel_id=1, source_target_pairs={{0,8},{8,0},{16,24},{24,16},{1,9},{9,1},{17,25},{25,17},{2,10},{10... | collective-permute-start | bytes 20 | tf_op jit(solution)/shard_map/ppermute | solution.py:971
  259.8 9.9 %collective-permute-start.29 = (bf16[2,48,1024]{2,1,0:T(8,128)(2,1)S(1)}, bf16[2,48,1024]{2,1,0:T(8,128)(2,1)S(1)}, u32[]{:S(2)}, u32[]{:S(2)}) collective-permute-start(bf16[2,48,1024]{2,1,0:T(8,128)(2,1)S(1)} %maximum_select_fusion.4), channel_id=1, source_target_pairs={{0,4},{4,0},{1,5},{5,1},{2,6},{6,2},{3,7},{7,3},{8,12},{12,8},{9,1... | collective-permute-start | bytes 589832 | tf_op jit(solution)/shard_map/ppermute | solution.py:971
  264.7 5.1 %collective-permute-start.34 = (bf16[2,48,2048]{2,1,0:T(8,128)(2,1)S(1)}, bf16[2,48,2048]{2,1,0:T(8,128)(2,1)S(1)}, u32[]{:S(2)}, u32[]{:S(2)}) collective-permute-start(bf16[2,48,2048]{2,1,0:T(8,128)(2,1)S(1)} %maximum_select_fusion.2), channel_id=1, source_target_pairs={{0,8},{8,0},{16,24},{24,16},{1,9},{9,1},{17,25},{25,17},{2,10},{10... | collective-permute-start | bytes 1179656 | tf_op jit(solution)/shard_map/ppermute | solution.py:971
  265.5 3.5 collective-permute-start.22
  314.7 11.5 %collective-permute-start.35 = (bf16[512,256]{1,0:T(8,128)(2,1)}, bf16[512,256]{1,0:T(8,128)(2,1)S(1)}, u32[]{:S(2)}, u32[]{:S(2)}) collective-permute-start(bf16[512,256]{1,0:T(8,128)(2,1)} %get-tuple-element.127), channel_id=1, source_target_pairs={{4,0},{5,1},{6,2},{7,3},{12,8},{13,9},{14,10},{15,11},{20,16},{21,... | collective-permute-start | bytes 786440 | tf_op jit(solution)/shard_map/ppermute | solution.py:1179
  334.4 11.4 %collective-permute-start.36 = (bf16[64,1024]{1,0:T(8,128)(2,1)S(1)}, bf16[64,1024]{1,0:T(8,128)(2,1)S(1)}, u32[]{:S(2)}, u32[]{:S(2)}) collective-permute-start(bf16[64,1024]{1,0:T(8,128)(2,1)S(1)} %constant_dynamic-slice_fusion.3), channel_id=1, source_target_pairs={{0,4},{4,0},{1,5},{5,1},{2,6},{6,2},{3,7},{7,3},{8,12},{12,8},{9,1... | collective-permute-start | bytes 393224 | tf_op jit(solution)/shard_map/ppermute | solution.py:971
  345.8 4.3 %collective-permute-start.37 = (bf16[64,512]{1,0:T(8,128)(2,1)S(1)}, bf16[64,512]{1,0:T(8,128)(2,1)S(1)}, u32[]{:S(2)}, u32[]{:S(2)}) collective-permute-start(bf16[64,512]{1,0:T(8,128)(2,1)S(1)} %constant_dynamic-slice_fusion.2), channel_id=1, source_target_pairs={{0,1},{1,0},{2,3},{3,2},{4,5},{5,4},{6,7},{7,6},{8,9},{9,8},{10,11... | collective-permute-start | bytes 196616 | tf_op jit(solution)/shard_map/ppermute | solution.py:971
  350.2 6.8 %collective-permute-start.38 = (bf16[64,256]{1,0:T(8,128)(2,1)S(1)}, bf16[64,256]{1,0:T(8,128)(2,1)S(1)}, u32[]{:S(2)}, u32[]{:S(2)}) collective-permute-start(bf16[64,256]{1,0:T(8,128)(2,1)S(1)} %constant_dynamic-slice_fusion.1), channel_id=1, source_target_pairs={{0,2},{1,3},{2,0},{3,1},{4,6},{5,7},{6,4},{7,5},{8,10},{9,11},{10,... | collective-permute-start | bytes 98312 | tf_op jit(solution)/shard_map/ppermute | solution.py:971
  359.9 3.9 collective-permute-start.39
  361.4 3.8 collective-permute-start.44
  363.8 7.8 %collective-permute-start.40 = (bf16[2,64,256]{2,1,0:T(8,128)(2,1)S(1)}, bf16[2,64,256]{2,1,0:T(8,128)(2,1)S(1)}, u32[]{:S(2)}, u32[]{:S(2)}) collective-permute-start(bf16[2,64,256]{2,1,0:T(8,128)(2,1)S(1)} %maximum_select_fusion.9), channel_id=1, source_target_pairs={{0,2},{1,3},{2,0},{3,1},{4,6},{5,7},{6,4},{7,5},{8,10},{9,11},{10,... | collective-permute-start | bytes 196616 | tf_op jit(solution)/shard_map/ppermute | solution.py:971
  365.2 6.5 %collective-permute-start.45 = (bf16[1,16,640]{2,1,0:T(8,128)(2,1)S(1)}, bf16[1,16,640]{2,1,0:T(8,128)(2,1)S(1)}, u32[]{:S(2)}, u32[]{:S(2)}) collective-permute-start(bf16[1,16,640]{2,1,0:T(8,128)(2,1)S(1)} %fusion.3), channel_id=1, source_target_pairs={{0,16},{8,24},{16,0},{24,8},{1,17},{9,25},{17,1},{25,9},{2,18},{10... | collective-permute-start | bytes 61448 | tf_op jit(solution)/shard_map/ppermute | solution.py:971
  371.6 12.1 %collective-permute-start.41 = (bf16[2,64,512]{2,1,0:T(8,128)(2,1)S(1)}, bf16[2,64,512]{2,1,0:T(8,128)(2,1)S(1)}, u32[]{:S(2)}, u32[]{:S(2)}) collective-permute-start(bf16[2,64,512]{2,1,0:T(8,128)(2,1)S(1)} %maximum_select_fusion.6), channel_id=1, source_target_pairs={{0,1},{1,0},{2,3},{3,2},{4,5},{5,4},{6,7},{7,6},{8,9},{9,8},{10,11... | collective-permute-start | bytes 393224 | tf_op jit(solution)/shard_map/ppermute | solution.py:971
  371.7 12.2 %collective-permute-start.46 = (bf16[2,16,640]{2,1,0:T(8,128)(2,1)S(1)}, bf16[2,16,640]{2,1,0:T(8,128)(2,1)S(1)}, u32[]{:S(2)}, u32[]{:S(2)}) collective-permute-start(bf16[2,16,640]{2,1,0:T(8,128)(2,1)S(1)} %maximum_select_fusion.11), channel_id=1, source_target_pairs={{0,4},{4,0},{1,5},{5,1},{2,6},{6,2},{3,7},{7,3},{8,12},{12,8},{9,1... | collective-permute-start | bytes 122888 | tf_op jit(solution)/shard_map/ppermute | solution.py:971
  383.9 6.4 %collective-permute-start.42 = (bf16[2,64,1024]{2,1,0:T(8,128)(2,1)S(1)}, bf16[2,64,1024]{2,1,0:T(8,128)(2,1)S(1)}, u32[]{:S(2)}, u32[]{:S(2)}) collective-permute-start(bf16[2,64,1024]{2,1,0:T(8,128)(2,1)S(1)} %maximum_select_fusion.3), channel_id=1, source_target_pairs={{0,4},{4,0},{1,5},{5,1},{2,6},{6,2},{3,7},{7,3},{8,12},{12,8},{9,1... | collective-permute-start | bytes 786440 | tf_op jit(solution)/shard_map/ppermute | solution.py:971
  384.0 6.5 %collective-permute-start.47 = (bf16[2,16,1280]{2,1,0:T(8,128)(2,1)S(1)}, bf16[2,16,1280]{2,1,0:T(8,128)(2,1)S(1)}, u32[]{:S(2)}, u32[]{:S(2)}) collective-permute-start(bf16[2,16,1280]{2,1,0:T(8,128)(2,1)S(1)} %maximum_select_fusion.8), channel_id=1, source_target_pairs={{0,8},{8,0},{16,24},{24,16},{1,9},{9,1},{17,25},{25,17},{2,10},{10... | collective-permute-start | bytes 245768 | tf_op jit(solution)/shard_map/ppermute | solution.py:971
  (31 other events, 154.1 us)
Sparse Core Ops, SparseCore 0:
  80.4 87.5 all-reduce.2
  208.4 90.0 all-reduce.4
  300.8 42.8 reduce-scatter.2
  345.9 47.1 reduce-scatter.4

commit v4 on v3

--- a/solution.py
+++ b/solution.py
@@ -1132,12 +1132,12 @@
         meta, normed, qkv_narrow, qkv_weights, qkv_lifts, q_gain, k_gain, cos, sin, seg_own
     )
     kv_far = lax.ppermute(kv, "ctx", onward)
-    ready = after(qrot, gate_across) if direct else qrot
+    ready = after(qrot, output_across) if direct else qrot
     att, wide, inv = attention_forward(meta, ready, kv_far, kv, log_scale)
     if direct:
         gate_other = flip(after(gate_across, att), "ctx", 1)
-        linear_across = flip(after(linear_weight, att, output_across), "fsdp", 2)
-        reduce_across = flip(after(reduce_weight, att, output_across), "fsdp", 2)
+        linear_across = flip(after(linear_weight, att, output_across, gate_across), "fsdp", 2)
+        reduce_across = flip(after(reduce_weight, att, output_across, gate_across), "fsdp", 2)
         output_weights = [
             output_weight, flip(after(output_weight, kv_far), "fsdp", 1), output_across,
             flip(after(output_across, kv_far), "fsdp", 1),

time: 415 us -> 416 us (level)
  waiting for transfers between devices: 181 us -> 187 us
    ppermute x1, waiting for transfers between devices: 0.01 us -> 6.21 us  [on_device(): kv_far = lax.ppermute(kv, 'ctx', onward)]
  transfers between devices with their start and end apart: 52 -> 52, of which waited for: 28 -> 29; matrix products, arithmetic and copies ran while one was open for 5% -> 4% of each run, Pallas kernels for 25% -> 25%
where the time goes in v4:
time: 416 us; the launch traced here: 409 us
  waiting for transfers between devices  187 us (45%)
  Pallas kernels  144 us (35%)
  starting transfers between devices  38.8 us (9%)
  between operations  15.4 us (4%)
  local copies, waits for them, and re-layouts  14.8 us (4%)
  other arithmetic  9.15 us (2%)
    ppermute x46, waiting for transfers between devices, flip(): return lax.ppermute(array, axis, [(i, i ^ bit) for i in range(count)])  163 us
    pallas_call x1, Pallas kernels, ffn(): pl.pallas_call(partial(ffn_kernel, shards=shards, chunk=chunk), name='fee...  39 us
    ppermute x46, starting transfers between devices, flip(): return lax.ppermute(array, axis, [(i, i ^ bit) for i in range(count)])  33.9 us
    psum x1, waiting for transfers between devices, on_device(): summed = lax.psum(back, 'tp')  18 us
    pallas_call x1, Pallas kernels, attention_backward_far(): pl.pallas_call(partial(far_kernel, log_scale=log_scale, block=256), name=...  16.2 us
    pallas_call x1, Pallas kernels, reduce_forward(): pl.pallas_call(reduce_kernel, name='reduce_forward', grid_spec=pltpu.Pref...  11.2 us
    pallas_call x1, Pallas kernels, attention_backward_near(): pl.pallas_call(partial(near_kernel, log_scale=log_scale, block=256), name...  10.2 us
    pallas_call x1, Pallas kernels, ffn_adapters(): pl.pallas_call(ffn_adapter_kernel, name='feed_forward_adapters', grid_spe...  9.71 us
  transfers between devices with their start and end apart: 52, of which 29 were waited for; matrix products, arithmetic and copies ran while one was open for 4% of the time, Pallas kernels for 25%

profile of v4, /device:TPU:0, one launch (start us, length us, event | category | flops | bytes accessed | tf_op | source)
XLA Modules:
  0.0 409.2 jit_solution(14639448192952107711)
XLA Ops:
  8.3 2.6 collective-permute-start
  14.4 5.0 %attention_norm.1 = (bf16[512,2048]{1,0:T(8,128)(2,1)}, bf16[512,128]{1,0:T(8,128)(2,1)}) custom-call(s32[16]{0:T(128)} %stack.73.meta, bf16[512,2048]{1,0:T(8,128)(2,1)} %bitcast.36, bf16[1,2048]{1,0:T(2,128)(2,1)} %broadcast_in_dim.26.gain, bf16[8,16,2048]{2,1,0:T(8,128)(2,1)} %bitcast.45, bf16[8,16,2048]{2,1,0:T(8,128)(2,1)} %bitcast.47, ...), custom_call_target="tpu_custom_call" | custom-call | flops 1024 | bytes 1024 | tf_op jit(solution)/shard_map/attention_norm/pallas_call | solution.py:98
  24.2 7.8 %collective-permute-done.6.kv2 = bf16[512,256]{1,0:T(8,128)(2,1)} collective-permute-done((bf16[512,256]{1,0:T(8,128)(2,1)S(1)}, bf16[512,256]{1,0:T(8,128)(2,1)}, u32[]{:S(2)}, u32[]{:S(2)}) %collective-permute-start.6) | collective-permute-done | bytes 262176 | tf_op jit(solution)/shard_map/ppermute | solution.py:971
  35.0 7.5 %qkv_forward.1 = (f32[512,640]{1,0:T(8,128)}, bf16[512,512]{1,0:T(8,128)(2,1)}, bf16[512,384]{1,0:T(8,128)(2,1)}) custom-call(s32[16]{0:T(128)} %stack.73.meta, bf16[512,2048]{1,0:T(8,128)(2,1)} %get-tuple-element.80.normed, bf16[512,128]{1,0:T(8,128)(2,1)} %get-tuple-element.81.narrow, bf16[512,512]{1,0:T(8,128)(2,1)} %q0.3, bf16[512,512]{1,0:T(8,128)(2,1)} %copy-done.6, ...), custom_call_target="tpu_custom_call" | custom-call | flops 1024 | bytes 1024 | tf_op jit(solution)/shard_map/qkv_forward/pallas_call | solution.py:154
  42.5 3.4 collective-permute-start.10
  47.3 1.4 collective-permute-start.13
  48.7 6.2 %collective-permute-done.10.kvf.kv = bf16[512,384]{1,0:T(8,128)(2,1)S(1)} collective-permute-done((bf16[512,384]{1,0:T(8,128)(2,1)}, bf16[512,384]{1,0:T(8,128)(2,1)S(1)}, u32[]{:S(2)}, u32[]{:S(2)}) %collective-permute-start.10) | collective-permute-done | bytes 393248 | tf_op jit(solution)/shard_map/ppermute | solution.py:1134
  55.7 9.7 %attention_forward.1 = (bf16[512,512]{1,0:T(8,128)(2,1)}, f32[512,512]{1,0:T(8,128)}, f32[512,512]{1,0:T(8,128)}) custom-call(s32[16]{0:T(128)} %stack.73.meta, bf16[512,512]{1,0:T(8,128)(2,1)} %get-tuple-element.89.qrot, bf16[512,384]{1,0:T(8,128)(2,1)} %copy-done.9, bf16[512,384]{1,0:T(8,128)(2,1)} %get-tuple-element.90.kvn.kvq.kv, ...), custom_call_target="tpu_custom_call" | custom-call | flops 17179869184 | bytes 67108864 | tf_op jit(solution)/shard_map/attention_forward/pallas_call | solution.py:245
  65.3 7.0 %collective-permute-done.13.refs_2_ = bf16[256,2048]{1,0:T(8,128)(2,1)S(1)} collective-permute-done((bf16[256,2048]{1,0:T(8,128)(2,1)S(1)}, bf16[256,2048]{1,0:T(8,128)(2,1)S(1)}, u32[]{:S(2)}, u32[]{:S(2)}) %collective-permute-start.13) | collective-permute-done | bytes 1048608 | tf_op jit(solution)/shard_map/ppermute | solution.py:971
  74.8 1.4 collective-permute-done.12.w3
  77.8 5.7 %output_forward.1 = (bf16[512,2048]{1,0:T(8,128)(2,1)}, bf16[512,128]{1,0:T(8,128)(2,1)}) custom-call(s32[16]{0:T(128)} %stack.73.meta, bf16[512,512]{1,0:T(8,128)(2,1)} %get-tuple-element.91.att, bf16[512,512]{1,0:T(8,128)(2,1)} %w0.3, bf16[512,512]{1,0:T(8,128)(2,1)} %copy-done.3, bf16[512,512]{1,0:T(8,128)(2,1)} %copy-done.1, bf16[512,512]{1,0:T(8,128)(2,1)} %copy-done.2, ...), custom_call_target="tpu_custom_call" | custom-call | flops 1024 | bytes 1024 | tf_op jit(solution)/shard_map/output_forward/pallas_call | solution.py:298
  83.6 37.6 %collective-permute-done.19.refs_12_.refs_2_ = bf16[2048,512]{1,0:T(8,128)(2,1)} collective-permute-done((bf16[2048,512]{1,0:T(8,128)(2,1)}, bf16[2048,512]{1,0:T(8,128)(2,1)}, u32[]{:S(2)}, u32[]{:S(2)}) %collective-permute-start.19) | collective-permute-done | bytes 2097184 | tf_op jit(solution)/shard_map/ppermute | solution.py:971
  121.2 42.9 %collective-permute-done.17.refs_8_ = bf16[512,2048]{1,0:T(8,128)(2,1)} collective-permute-done((bf16[512,2048]{1,0:T(8,128)(2,1)}, bf16[512,2048]{1,0:T(8,128)(2,1)}, u32[]{:S(2)}, u32[]{:S(2)}) %collective-permute-start.17) | collective-permute-done | bytes 2097184 | tf_op jit(solution)/shard_map/ppermute | solution.py:971
  164.6 6.3 %collective-permute-done.15.refs_4_ = bf16[256,2048]{1,0:T(8,128)(2,1)S(1)} collective-permute-done((bf16[256,2048]{1,0:T(8,128)(2,1)S(1)}, bf16[256,2048]{1,0:T(8,128)(2,1)S(1)}, u32[]{:S(2)}, u32[]{:S(2)}) %collective-permute-start.15) | collective-permute-done | bytes 1048608 | tf_op jit(solution)/shard_map/ppermute | solution.py:971
  173.1 39.0 %feed_forward.1 = (bf16[512,2048]{1,0:T(8,128)(2,1)}, bf16[512,2048]{1,0:T(8,128)(2,1)}, bf16[512,2048]{1,0:T(8,128)(2,1)}, bf16[512,2048]{1,0:T(8,128)(2,1)}, b...) custom-call(s32[16]{0:T(128)} %stack.73.meta, bf16[512,2048]{1,0:T(8,128)(2,1)} %bitcast.37, ...), custom_call_target="tpu_custom_call" | custom-call | flops 17179869184 | bytes 31457280 | tf_op jit(solution)/shard_map/feed_forward/pallas_call | solution.py:426
  212.2 9.7 %feed_forward_adapters.1 = (bf16[48,2048]{1,0:T(8,128)(2,1)}, bf16[48,2048]{1,0:T(8,128)(2,1)}, bf16[512,128]{1,0:T(8,128)(2,1)}) custom-call(s32[16]{0:T(128)} %stack.73.meta, bf16[512,2048]{1,0:T(8,128)(2,1)} %bitcast.38, bf16[512,2048]{1,0:T(8,128)(2,1)} %all-reduce.3.cloned.1.call-done.branch.second, bf16[512,2048]{1,0:T(8,128)(2,1)} %bitcast.42, ...), custom_call_target="tpu_custom_call" | custom-call | flops 536870912 | bytes 12582912 | tf_op jit(solution)/shard_map/feed_forward_adapters/pallas_call | solution.py:499
  222.9 5.0 %collective-permute-done.23 = bf16[48,1024]{1,0:T(8,128)(2,1)S(1)} collective-permute-done((bf16[48,1024]{1,0:T(8,128)(2,1)S(1)}, bf16[48,1024]{1,0:T(8,128)(2,1)S(1)}, u32[]{:S(2)}, u32[]{:S(2)}) %collective-permute-start.23) | collective-permute-done | bytes 98336 | tf_op jit(solution)/shard_map/ppermute | solution.py:971
  228.8 1.7 collective-permute-start.24
  230.4 6.6 %collective-permute-done.24 = bf16[48,512]{1,0:T(8,128)(2,1)S(1)} collective-permute-done((bf16[48,512]{1,0:T(8,128)(2,1)S(1)}, bf16[48,512]{1,0:T(8,128)(2,1)S(1)}, u32[]{:S(2)}, u32[]{:S(2)}) %collective-permute-start.24) | collective-permute-done | bytes 49184 | tf_op jit(solution)/shard_map/ppermute | solution.py:971
  238.0 11.2 %reduce_forward.1 = bf16[512,2048]{1,0:T(8,128)(2,1)} custom-call(s32[16]{0:T(128)} %stack.73.meta, bf16[512,2048]{1,0:T(8,128)(2,1)} %get-tuple-element.100.inner, bf16[512,128]{1,0:T(8,128)(2,1)} %get-tuple-element.106.n_r, bf16[2048,512]{1,0:T(8,128)(2,1)} %refs_0_.3, bf16[2048,512]{1,0:T(8,128)(2,1)} %collective-permute-done.4.refs_11_.refs_1_, ...), custom_call_target="tpu_custom_call" | custom-call | flops 4294967296 | bytes 12582912 | tf_op jit(solution)/shard_map/reduce_forward/pallas_call | solution.py:539
  249.3 1.8 collective-permute-start.26
  251.5 1.7 collective-permute-done.26
  253.2 2.2 collective-permute-start.27
  256.7 1.6 collective-permute-done.27
  258.3 3.2 collective-permute-start.28
  261.5 1.5 collective-permute-start.33
  263.0 2.5 collective-permute-done.28
  265.5 1.7 collective-permute-start.29
  269.1 2.7 collective-permute-start.22
  271.7 1.5 collective-permute-done.22
  276.8 5.0 %place_sets.2 = (f32[8,16,2048]{2,1,0:T(8,128)}, f32[8,16,2048]{2,1,0:T(8,128)}, f32[8,16,2048]{2,1,0:T(8,128)}, f32[8,16,2048]{2,1,0:T(8,128)}, f32[8,16,2048]{2,1,0:T(8,128)}, /*index=5*/f32[8,16,2048]{2,1,0:T(8,128)}) custom-call(s32[4]{0:T(128)} %broadcast_select_fusion.17.sets, bf16[4,48,2048]{2,1,0:T(8,128)(2,1)} %pad_maximum_fusion.1.refs_0_, ...), custom_call_target="tpu_custom_call" | custom-call | flops 1024 | bytes 8388608 | tf_op jit(solution)/shard_map/place_sets/pallas_call | solution.py:926
  281.8 18.0 %all-reduce.5.cloned.1.call-done.summed.second = bf16[512,2048]{1,0:T(8,128)(2,1)} async-done(((bf16[512,2048]{1,0:T(8,128)(2,1)}), bf16[512,2048]{1,0:T(8,128)(2,1)}) %all-reduce.5.cloned.1.call-update) | async-done | bytes 2097168 | tf_op jit(solution)/shard_map/psum | solution.py:1159
  299.8 16.2 %attention_backward_far.1 = (bf16[512,512]{1,0:T(8,128)(2,1)}, bf16[512,512]{1,0:T(8,128)(2,1)}, f32[512,512]{1,0:T(8,128)}, bf16[512,256]{1,0:T(8,128)(2,1)}, b...) custom-call(s32[16]{0:T(128)} %stack.73.meta, bf16[512,2048]{1,0:T(8,128)(2,1)} %bitcast.43, ...), custom_call_target="tpu_custom_call" | custom-call | flops 2684354560 | bytes 16777216 | tf_op jit(solution)/shard_map/attention_backward_far/pallas_call | solution.py:719
  317.3 10.2 %attention_backward_near.1 = (f32[512,512]{1,0:T(8,128)}, f32[512,256]{1,0:T(8,128)}) custom-call(s32[16]{0:T(128)} %stack.73.meta, bf16[512,512]{1,0:T(8,128)(2,1)} %get-tuple-element.122.dop, bf16[512,512]{1,0:T(8,128)(2,1)} %get-tuple-element.123.mixed, bf16[512,512]{1,0:T(8,128)(2,1)} %get-tuple-element.89.qrot, ...), custom_call_target="tpu_custom_call" | custom-call | flops 2684354560 | bytes 6291456 | tf_op jit(solution)/shard_map/attention_backward_near/pallas_call | solution.py:747
  328.2 6.5 %qkv_grads.1 = (bf16[512,768]{1,0:T(8,128)(2,1)}, bf16[512,128]{1,0:T(8,128)(2,1)}, bf16[48,2048]{1,0:T(8,128)(2,1)}, bf16[16,512]{1,0:T(8,128)(2,1)}, bf16[16,256]{1,0:T(8,128)(2,1)}) custom-call(s32[16]{0:T(128)} %stack.73.meta, bf16[512,2048]{1,0:T(8,128)(2,1)} %get-tuple-element.80.normed, bf16[512,128]{1,0:T(8,128)(2,1)} %get-tuple-element.81.narrow, ...), custom_call_target="tpu_custom_call" | custom-call | flops 201326592 | bytes 8388608 | tf_op jit(solution)/shard_map/qkv_grads/pallas_call | solution.py:820
  335.6 2.8 collective-permute-start.36
  338.4 7.9 %qkv_backward.1 = bf16[512,2048]{1,0:T(8,128)(2,1)} custom-call(s32[16]{0:T(128)} %stack.73.meta, bf16[512,2048]{1,0:T(8,128)(2,1)} %bitcast.39, bf16[1,2048]{1,0:T(2,128)(2,1)} %broadcast_in_dim.26.gain, bf16[512,768]{1,0:T(8,128)(2,1)} %get-tuple-element.128.grad, bf16[512,128]{1,0:T(8,128)(2,1)} %get-tuple-element.129.low, bf16[512,512]{1,0:T(8,128)(2,1)} %q0.3, ...), custom_call_target="tpu_custom_call" | custom-call | flops 1610612736 | bytes 8388608 | tf_op jit(solution)/shard_map/qkv_backward/pallas_call | solution.py:888
  347.8 3.6 collective-permute-done.37
  351.4 1.4 collective-permute-start.38
  352.8 5.7 %collective-permute-done.38 = bf16[64,256]{1,0:T(8,128)(2,1)S(1)} collective-permute-done((bf16[64,256]{1,0:T(8,128)(2,1)S(1)}, bf16[64,256]{1,0:T(8,128)(2,1)S(1)}, u32[]{:S(2)}, u32[]{:S(2)}) %collective-permute-start.38) | collective-permute-done | bytes 32800 | tf_op jit(solution)/shard_map/ppermute | solution.py:971
  358.5 2.8 close.2
  361.4 1.5 collective-permute-start.39
  362.9 2.4 collective-permute-done.39
  367.3 5.6 %collective-permute-done.40 = bf16[2,64,256]{2,1,0:T(8,128)(2,1)S(1)} collective-permute-done((bf16[2,64,256]{2,1,0:T(8,128)(2,1)S(1)}, bf16[2,64,256]{2,1,0:T(8,128)(2,1)S(1)}, u32[]{:S(2)}, u32[]{:S(2)}) %collective-permute-start.40) | collective-permute-done | bytes 65568 | tf_op jit(solution)/shard_map/ppermute | solution.py:971
  373.3 11.8 %collective-permute-done.41 = bf16[2,64,512]{2,1,0:T(8,128)(2,1)S(1)} collective-permute-done((bf16[2,64,512]{2,1,0:T(8,128)(2,1)S(1)}, bf16[2,64,512]{2,1,0:T(8,128)(2,1)S(1)}, u32[]{:S(2)}, u32[]{:S(2)}) %collective-permute-start.41) | collective-permute-done | bytes 131104 | tf_op jit(solution)/shard_map/ppermute | solution.py:971
  385.4 6.2 %collective-permute-done.42 = bf16[2,64,1024]{2,1,0:T(8,128)(2,1)S(1)} collective-permute-done((bf16[2,64,1024]{2,1,0:T(8,128)(2,1)S(1)}, bf16[2,64,1024]{2,1,0:T(8,128)(2,1)S(1)}, u32[]{:S(2)}, u32[]{:S(2)}) %collective-permute-start.42) | collective-permute-done | bytes 262176 | tf_op jit(solution)/shard_map/ppermute | solution.py:971
  394.9 4.4 %place_sets.3 = (f32[8,16,2048]{2,1,0:T(8,128)}, f32[8,16,2048]{2,1,0:T(8,128)}, f32[8,16,2048]{2,1,0:T(8,128)}, f32[8,16,2048]{2,1,0:T(8,128)}, f32[8,16,512]{2...) custom-call(s32[4]{0:T(128)} %broadcast_select_fusion.17.sets, ...), custom_call_target="tpu_custom_call" | custom-call | flops 8589934592 | bytes 8388608 | tf_op jit(solution)/shard_map/place_sets/pallas_call | solution.py:926
  399.3 2.9 close.3
  (182 shorter events, 41.0 us)
Async XLA Ops:
  7.2 164.6 %all-reduce.3.cloned.1.call-start = ((), (), s32[]{:S(2)}) async-start(), calls=%async_computation.2 | async-start | bytes 4194304 | tf_op jit(solution)/shard_map/psum | solution.py:1153
  7.3 16.5 %collective-permute-start.4 = (bf16[2048,512]{1,0:T(8,128)(2,1)}, bf16[2048,512]{1,0:T(8,128)(2,1)}, u32[]{:S(2)}, u32[]{:S(2)}) collective-permute-start(bf16[2048,512]{1,0:T(8,128)(2,1)} %refs_0_.3), channel_id=1, source_target_pairs={{0,8},{8,0},{16,24},{24,16},{1,9},{9,1},{17,25},{25,17},{2,10},{10... | collective-permute-start | bytes 6291464 | tf_op jit(solution)/shard_map/ppermute | solution.py:971
  7.8 16.0 %collective-permute-start.2 = (bf16[512,2048]{1,0:T(8,128)(2,1)}, bf16[512,2048]{1,0:T(8,128)(2,1)}, u32[]{:S(2)}, u32[]{:S(2)}) collective-permute-start(bf16[512,2048]{1,0:T(8,128)(2,1)} %refs_0_.2), channel_id=1, source_target_pairs={{0,8},{8,0},{16,24},{24,16},{1,9},{9,1},{17,25},{25,17},{2,10},{10... | collective-permute-start | bytes 6291464 | tf_op jit(solution)/shard_map/ppermute | solution.py:971
  7.9 15.9 %collective-permute-start.3 = (bf16[512,2048]{1,0:T(8,128)(2,1)}, bf16[512,2048]{1,0:T(8,128)(2,1)}, u32[]{:S(2)}, u32[]{:S(2)}) collective-permute-start(bf16[512,2048]{1,0:T(8,128)(2,1)} %refs_6_.1), channel_id=1, source_target_pairs={{0,8},{8,0},{16,24},{24,16},{1,9},{9,1},{17,25},{25,17},{2,10},{10... | collective-permute-start | bytes 6291464 | tf_op jit(solution)/shard_map/ppermute | solution.py:971
  8.3 15.3 %collective-permute-start = (bf16[512,512]{1,0:T(8,128)(2,1)}, bf16[512,512]{1,0:T(8,128)(2,1)S(1)}, u32[]{:S(2)}, u32[]{:S(2)}) collective-permute-start(bf16[512,512]{1,0:T(8,128)(2,1)} %q0.3), channel_id=1, source_target_pairs={{0,16},{8,24},{16,0},{24,8},{1,17},{9,25},{17,1},{25,9},{2,18},{10... | collective-permute-start | bytes 1572872 | tf_op jit(solution)/shard_map/ppermute | solution.py:971
  23.5 8.5 %collective-permute-start.6 = (bf16[512,256]{1,0:T(8,128)(2,1)S(1)}, bf16[512,256]{1,0:T(8,128)(2,1)}, u32[]{:S(2)}, u32[]{:S(2)}) collective-permute-start(bf16[512,256]{1,0:T(8,128)(2,1)S(1)} %constant_dynamic-update-slice_fusion.kv0), channel_id=1, source_target_pairs={{0,16},{8,24},{16,0},{24,8},{1,17},{9,25},{17,1},{25,9},{2,18},{10... | collective-permute-start | bytes 786440 | tf_op jit(solution)/shard_map/ppermute | solution.py:971
  23.6 10.4 %collective-permute-start.1 = (bf16[512,512]{1,0:T(8,128)(2,1)S(1)}, bf16[512,512]{1,0:T(8,128)(2,1)S(1)}, u32[]{:S(2)}, u32[]{:S(2)}) collective-permute-start(bf16[512,512]{1,0:T(8,128)(2,1)S(1)} %copy-done.4), channel_id=1, source_target_pairs={{0,8},{8,0},{16,24},{24,16},{1,9},{9,1},{17,25},{25,17},{2,10},{10... | collective-permute-start | bytes 1572872 | tf_op jit(solution)/shard_map/ppermute | solution.py:971
  23.8 10.5 %collective-permute-start.5 = (bf16[512,512]{1,0:T(8,128)(2,1)S(1)}, bf16[512,512]{1,0:T(8,128)(2,1)S(1)}, u32[]{:S(2)}, u32[]{:S(2)}) collective-permute-start(bf16[512,512]{1,0:T(8,128)(2,1)S(1)} %collective-permute-done.q2), channel_id=1, source_target_pairs={{0,8},{8,0},{16,24},{24,16},{1,9},{9,1},{17,25},{25,17},{2,10},{10... | collective-permute-start | bytes 1572872 | tf_op jit(solution)/shard_map/ppermute | solution.py:971
  32.0 2.2 collective-permute-start.8
  32.5 16.2 %collective-permute-start.9 = (bf16[512,512]{1,0:T(8,128)(2,1)S(1)}, bf16[512,512]{1,0:T(8,128)(2,1)S(1)}, u32[]{:S(2)}, u32[]{:S(2)}) collective-permute-start(bf16[512,512]{1,0:T(8,128)(2,1)S(1)} %copy-done), channel_id=1, source_target_pairs={{0,16},{8,24},{16,0},{24,8},{1,17},{9,25},{17,1},{25,9},{2,18},{10... | collective-permute-start | bytes 1572872 | tf_op jit(solution)/shard_map/ppermute | solution.py:971
  42.5 12.4 %collective-permute-start.10 = (bf16[512,384]{1,0:T(8,128)(2,1)}, bf16[512,384]{1,0:T(8,128)(2,1)S(1)}, u32[]{:S(2)}, u32[]{:S(2)}) collective-permute-start(bf16[512,384]{1,0:T(8,128)(2,1)} %get-tuple-element.90.kvn.kvq.kv), channel_id=1, source_target_pairs={{0,4},{1,5},{2,6},{3,7},{8,12},{9,13},{10,14},{11,15},{16,20},{17,... | collective-permute-start | bytes 1179656 | tf_op jit(solution)/shard_map/ppermute | solution.py:1134
  47.3 25.0 %collective-permute-start.13 = (bf16[256,2048]{1,0:T(8,128)(2,1)S(1)}, bf16[256,2048]{1,0:T(8,128)(2,1)S(1)}, u32[]{:S(2)}, u32[]{:S(2)}) collective-permute-start(bf16[256,2048]{1,0:T(8,128)(2,1)S(1)} %constant_dynamic-slice_fusion.8), channel_id=1, source_target_pairs={{0,16},{8,24},{16,0},{24,8},{1,17},{9,25},{17,1},{25,9},{2,18},{10... | collective-permute-start | bytes 3145736 | tf_op jit(solution)/shard_map/ppermute | solution.py:971
  72.3 48.9 %collective-permute-start.19 = (bf16[2048,512]{1,0:T(8,128)(2,1)}, bf16[2048,512]{1,0:T(8,128)(2,1)}, u32[]{:S(2)}, u32[]{:S(2)}) collective-permute-start(bf16[2048,512]{1,0:T(8,128)(2,1)} %refs_0_.3), channel_id=1, source_target_pairs={{0,16},{8,24},{16,0},{24,8},{1,17},{9,25},{17,1},{25,9},{2,18},{10... | collective-permute-start | bytes 6291464 | tf_op jit(solution)/shard_map/ppermute | solution.py:971
  73.2 90.9 %collective-permute-start.17 = (bf16[512,2048]{1,0:T(8,128)(2,1)}, bf16[512,2048]{1,0:T(8,128)(2,1)}, u32[]{:S(2)}, u32[]{:S(2)}) collective-permute-start(bf16[512,2048]{1,0:T(8,128)(2,1)} %refs_6_.1), channel_id=1, source_target_pairs={{0,16},{8,24},{16,0},{24,8},{1,17},{9,25},{17,1},{25,9},{2,18},{10... | collective-permute-start | bytes 6291464 | tf_op jit(solution)/shard_map/ppermute | solution.py:971
  74.3 2.7 collective-permute-start.11
  74.8 89.2 %collective-permute-start.14 = (bf16[256,2048]{1,0:T(8,128)(2,1)S(1)}, bf16[256,2048]{1,0:T(8,128)(2,1)}, u32[]{:S(2)}, u32[]{:S(2)}) collective-permute-start(bf16[256,2048]{1,0:T(8,128)(2,1)S(1)} %collective-permute-done.13.refs_2_), channel_id=1, source_target_pairs={{0,4},{4,0},{1,5},{5,1},{2,6},{6,2},{3,7},{7,3},{8,12},{12,8},{9,1... | collective-permute-start | bytes 3145736 | tf_op jit(solution)/shard_map/ppermute | solution.py:971
  83.6 216.2 %all-reduce.5.cloned.1.call-start = ((), (), s32[]{:S(2)}) async-start(), calls=%async_computation.4 | async-start | bytes 4194304 | tf_op jit(solution)/shard_map/psum | solution.py:1159
  121.2 50.7 %collective-permute-start.20 = (bf16[2048,512]{1,0:T(8,128)(2,1)}, bf16[2048,512]{1,0:T(8,128)(2,1)S(1)}, u32[]{:S(2)}, u32[]{:S(2)}) collective-permute-start(bf16[2048,512]{1,0:T(8,128)(2,1)} %collective-permute-done.19.refs_12_.refs_2_), channel_id=1, source_target_pairs={{0,8},{8,0},{16,24},{24,16},{1,9},{9,1},{17,25},{25,17},{2,10},{10... | collective-permute-start | bytes 6291464 | tf_op jit(solution)/shard_map/ppermute | solution.py:971
  164.1 7.8 %collective-permute-start.18 = (bf16[512,2048]{1,0:T(8,128)(2,1)}, bf16[512,2048]{1,0:T(8,128)(2,1)}, u32[]{:S(2)}, u32[]{:S(2)}) collective-permute-start(bf16[512,2048]{1,0:T(8,128)(2,1)} %collective-permute-done.17.refs_8_), channel_id=1, source_target_pairs={{0,8},{8,0},{16,24},{24,16},{1,9},{9,1},{17,25},{25,17},{2,10},{10... | collective-permute-start | bytes 6291464 | tf_op jit(solution)/shard_map/ppermute | solution.py:971
  164.1 6.8 %collective-permute-start.15 = (bf16[256,2048]{1,0:T(8,128)(2,1)S(1)}, bf16[256,2048]{1,0:T(8,128)(2,1)S(1)}, u32[]{:S(2)}, u32[]{:S(2)}) collective-permute-start(bf16[256,2048]{1,0:T(8,128)(2,1)S(1)} %collective-permute-done.13.refs_2_), channel_id=1, source_target_pairs={{0,8},{8,0},{16,24},{24,16},{1,9},{9,1},{17,25},{25,17},{2,10},{10... | collective-permute-start | bytes 3145736 | tf_op jit(solution)/shard_map/ppermute | solution.py:971
  164.6 7.2 %collective-permute-start.16 = (bf16[256,2048]{1,0:T(8,128)(2,1)}, bf16[256,2048]{1,0:T(8,128)(2,1)}, u32[]{:S(2)}, u32[]{:S(2)}) collective-permute-start(bf16[256,2048]{1,0:T(8,128)(2,1)} %collective-permute-done.14.refs_3_), channel_id=1, source_target_pairs={{0,8},{8,0},{16,24},{24,16},{1,9},{9,1},{17,25},{25,17},{2,10},{10... | collective-permute-start | bytes 3145736 | tf_op jit(solution)/shard_map/ppermute | solution.py:971
  212.2 146.4 %reduce-scatter.3.cloned.1.call-start = ((), (), s32[]{:S(2)}) async-start(), calls=%async_computation.3 | async-start | bytes 2621440 | tf_op jit(solution)/shard_map/reduce_scatter | solution.py:1171
  222.8 5.0 %collective-permute-start.23 = (bf16[48,1024]{1,0:T(8,128)(2,1)S(1)}, bf16[48,1024]{1,0:T(8,128)(2,1)S(1)}, u32[]{:S(2)}, u32[]{:S(2)}) collective-permute-start(bf16[48,1024]{1,0:T(8,128)(2,1)S(1)} %constant_dynamic-slice_fusion.7), channel_id=1, source_target_pairs={{0,4},{4,0},{1,5},{5,1},{2,6},{6,2},{3,7},{7,3},{8,12},{12,8},{9,1... | collective-permute-start | bytes 294920 | tf_op jit(solution)/shard_map/ppermute | solution.py:971
  228.8 8.3 %collective-permute-start.24 = (bf16[48,512]{1,0:T(8,128)(2,1)S(1)}, bf16[48,512]{1,0:T(8,128)(2,1)S(1)}, u32[]{:S(2)}, u32[]{:S(2)}) collective-permute-start(bf16[48,512]{1,0:T(8,128)(2,1)S(1)} %constant_dynamic-slice_fusion.6), channel_id=1, source_target_pairs={{0,1},{1,0},{2,3},{3,2},{4,5},{5,4},{6,7},{7,6},{8,9},{9,8},{10,11... | collective-permute-start | bytes 147464 | tf_op jit(solution)/shard_map/ppermute | solution.py:971
  237.1 12.2 %collective-permute-start.25 = (bf16[48,256]{1,0:T(8,128)(2,1)S(1)}, bf16[48,256]{1,0:T(8,128)(2,1)S(1)}, u32[]{:S(2)}, u32[]{:S(2)}) collective-permute-start(bf16[48,256]{1,0:T(8,128)(2,1)S(1)} %constant_dynamic-slice_fusion.5), channel_id=1, source_target_pairs={{0,2},{1,3},{2,0},{3,1},{4,6},{5,7},{6,4},{7,5},{8,10},{9,11},{10,... | collective-permute-start | bytes 73736 | tf_op jit(solution)/shard_map/ppermute | solution.py:971
  249.2 150.1 %reduce-scatter.5.cloned.1.call-start = ((), (), s32[]{:S(2)}) async-start(), calls=%async_computation.5 | async-start | bytes 2621440 | tf_op jit(solution)/shard_map/reduce_scatter | solution.py:1187
  249.3 3.9 collective-permute-start.26
  251.1 4.7 %collective-permute-start.31 = (bf16[48,1024]{1,0:T(8,128)(2,1)S(1)}, bf16[48,1024]{1,0:T(8,128)(2,1)S(1)}, u32[]{:S(2)}, u32[]{:S(2)}) collective-permute-start(bf16[48,1024]{1,0:T(8,128)(2,1)S(1)} %constant_dynamic-slice_fusion.4), channel_id=1, source_target_pairs={{0,4},{4,0},{1,5},{5,1},{2,6},{6,2},{3,7},{7,3},{8,12},{12,8},{9,1... | collective-permute-start | bytes 294920 | tf_op jit(solution)/shard_map/ppermute | solution.py:971
  253.2 5.1 %collective-permute-start.27 = (bf16[2,48,256]{2,1,0:T(8,128)(2,1)S(1)}, bf16[2,48,256]{2,1,0:T(8,128)(2,1)S(1)}, u32[]{:S(2)}, u32[]{:S(2)}) collective-permute-start(bf16[2,48,256]{2,1,0:T(8,128)(2,1)S(1)} %maximum_select_fusion.10), channel_id=1, source_target_pairs={{0,2},{1,3},{2,0},{3,1},{4,6},{5,7},{6,4},{7,5},{8,10},{9,11},{10,... | collective-permute-start | bytes 147464 | tf_op jit(solution)/shard_map/ppermute | solution.py:971
  255.8 5.6 %collective-permute-start.32 = (bf16[1,48,1024]{2,1,0:T(8,128)(2,1)S(1)}, bf16[1,48,1024]{2,1,0:T(8,128)(2,1)S(1)}, u32[]{:S(2)}, u32[]{:S(2)}) collective-permute-start(bf16[1,48,1024]{2,1,0:T(8,128)(2,1)S(1)} %fusion), channel_id=1, source_target_pairs={{0,16},{8,24},{16,0},{24,8},{1,17},{9,25},{17,1},{25,9},{2,18},{10... | collective-permute-start | bytes 294920 | tf_op jit(solution)/shard_map/ppermute | solution.py:971
  258.3 7.2 %collective-permute-start.28 = (bf16[2,48,512]{2,1,0:T(8,128)(2,1)S(1)}, bf16[2,48,512]{2,1,0:T(8,128)(2,1)S(1)}, u32[]{:S(2)}, u32[]{:S(2)}) collective-permute-start(bf16[2,48,512]{2,1,0:T(8,128)(2,1)S(1)} %maximum_select_fusion.7), channel_id=1, source_target_pairs={{0,1},{1,0},{2,3},{3,2},{4,5},{5,4},{6,7},{7,6},{8,9},{9,8},{10,11... | collective-permute-start | bytes 294920 | tf_op jit(solution)/shard_map/ppermute | solution.py:971
  261.5 6.7 %collective-permute-start.33 = (bf16[2,48,1024]{2,1,0:T(8,128)(2,1)S(1)}, bf16[2,48,1024]{2,1,0:T(8,128)(2,1)S(1)}, u32[]{:S(2)}, u32[]{:S(2)}) collective-permute-start(bf16[2,48,1024]{2,1,0:T(8,128)(2,1)S(1)} %maximum_select_fusion.5), channel_id=1, source_target_pairs={{0,4},{4,0},{1,5},{5,1},{2,6},{6,2},{3,7},{7,3},{8,12},{12,8},{9,1... | collective-permute-start | bytes 589832 | tf_op jit(solution)/shard_map/ppermute | solution.py:971
  263.0 5.3 %collective-permute-start.21 = (s32[1]{0:T(128)}, s32[1]{0:T(128)}, u32[]{:S(2)}, u32[]{:S(2)}) collective-permute-start(s32[1]{0:T(128)} %param.31), channel_id=1, source_target_pairs={{0,8},{8,0},{16,24},{24,16},{1,9},{9,1},{17,25},{25,17},{2,10},{10... | collective-permute-start | bytes 20 | tf_op jit(solution)/shard_map/ppermute | solution.py:971
  265.5 8.3 %collective-permute-start.29 = (bf16[2,48,1024]{2,1,0:T(8,128)(2,1)S(1)}, bf16[2,48,1024]{2,1,0:T(8,128)(2,1)S(1)}, u32[]{:S(2)}, u32[]{:S(2)}) collective-permute-start(bf16[2,48,1024]{2,1,0:T(8,128)(2,1)S(1)} %maximum_select_fusion.4), channel_id=1, source_target_pairs={{0,4},{4,0},{1,5},{5,1},{2,6},{6,2},{3,7},{7,3},{8,12},{12,8},{9,1... | collective-permute-start | bytes 589832 | tf_op jit(solution)/shard_map/ppermute | solution.py:971
  268.3 5.8 %collective-permute-start.34 = (bf16[2,48,2048]{2,1,0:T(8,128)(2,1)S(1)}, bf16[2,48,2048]{2,1,0:T(8,128)(2,1)S(1)}, u32[]{:S(2)}, u32[]{:S(2)}) collective-permute-start(bf16[2,48,2048]{2,1,0:T(8,128)(2,1)S(1)} %maximum_select_fusion.2), channel_id=1, source_target_pairs={{0,8},{8,0},{16,24},{24,16},{1,9},{9,1},{17,25},{25,17},{2,10},{10... | collective-permute-start | bytes 1179656 | tf_op jit(solution)/shard_map/ppermute | solution.py:971
  269.1 4.2 %collective-permute-start.22 = (s32[2]{0:T(128)S(1)}, s32[2]{0:T(128)S(1)}, u32[]{:S(2)}, u32[]{:S(2)}) collective-permute-start(s32[2]{0:T(128)S(1)} %broadcast_select_fusion.16), channel_id=1, source_target_pairs={{0,16},{8,24},{16,0},{24,8},{1,17},{9,25},{17,1},{25,9},{2,18},{10... | collective-permute-start | bytes 32 | tf_op jit(solution)/shard_map/ppermute | solution.py:971
  316.0 11.4 %collective-permute-start.35 = (bf16[512,256]{1,0:T(8,128)(2,1)}, bf16[512,256]{1,0:T(8,128)(2,1)S(1)}, u32[]{:S(2)}, u32[]{:S(2)}) collective-permute-start(bf16[512,256]{1,0:T(8,128)(2,1)} %get-tuple-element.127), channel_id=1, source_target_pairs={{4,0},{5,1},{6,2},{7,3},{12,8},{13,9},{14,10},{15,11},{20,16},{21,... | collective-permute-start | bytes 786440 | tf_op jit(solution)/shard_map/ppermute | solution.py:1179
  335.6 11.4 %collective-permute-start.36 = (bf16[64,1024]{1,0:T(8,128)(2,1)S(1)}, bf16[64,1024]{1,0:T(8,128)(2,1)S(1)}, u32[]{:S(2)}, u32[]{:S(2)}) collective-permute-start(bf16[64,1024]{1,0:T(8,128)(2,1)S(1)} %constant_dynamic-slice_fusion.3), channel_id=1, source_target_pairs={{0,4},{4,0},{1,5},{5,1},{2,6},{6,2},{3,7},{7,3},{8,12},{12,8},{9,1... | collective-permute-start | bytes 393224 | tf_op jit(solution)/shard_map/ppermute | solution.py:971
  347.1 4.3 %collective-permute-start.37 = (bf16[64,512]{1,0:T(8,128)(2,1)S(1)}, bf16[64,512]{1,0:T(8,128)(2,1)S(1)}, u32[]{:S(2)}, u32[]{:S(2)}) collective-permute-start(bf16[64,512]{1,0:T(8,128)(2,1)S(1)} %constant_dynamic-slice_fusion.2), channel_id=1, source_target_pairs={{0,1},{1,0},{2,3},{3,2},{4,5},{5,4},{6,7},{7,6},{8,9},{9,8},{10,11... | collective-permute-start | bytes 196616 | tf_op jit(solution)/shard_map/ppermute | solution.py:971
  351.4 7.1 %collective-permute-start.38 = (bf16[64,256]{1,0:T(8,128)(2,1)S(1)}, bf16[64,256]{1,0:T(8,128)(2,1)S(1)}, u32[]{:S(2)}, u32[]{:S(2)}) collective-permute-start(bf16[64,256]{1,0:T(8,128)(2,1)S(1)} %constant_dynamic-slice_fusion.1), channel_id=1, source_target_pairs={{0,2},{1,3},{2,0},{3,1},{4,6},{5,7},{6,4},{7,5},{8,10},{9,11},{10,... | collective-permute-start | bytes 98312 | tf_op jit(solution)/shard_map/ppermute | solution.py:971
  361.4 3.9 collective-permute-start.39
  362.9 3.8 collective-permute-start.44
  365.3 7.6 %collective-permute-start.40 = (bf16[2,64,256]{2,1,0:T(8,128)(2,1)S(1)}, bf16[2,64,256]{2,1,0:T(8,128)(2,1)S(1)}, u32[]{:S(2)}, u32[]{:S(2)}) collective-permute-start(bf16[2,64,256]{2,1,0:T(8,128)(2,1)S(1)} %maximum_select_fusion.9), channel_id=1, source_target_pairs={{0,2},{1,3},{2,0},{3,1},{4,6},{5,7},{6,4},{7,5},{8,10},{9,11},{10,... | collective-permute-start | bytes 196616 | tf_op jit(solution)/shard_map/ppermute | solution.py:971
  366.7 6.4 %collective-permute-start.45 = (bf16[1,16,640]{2,1,0:T(8,128)(2,1)S(1)}, bf16[1,16,640]{2,1,0:T(8,128)(2,1)S(1)}, u32[]{:S(2)}, u32[]{:S(2)}) collective-permute-start(bf16[1,16,640]{2,1,0:T(8,128)(2,1)S(1)} %fusion.3), channel_id=1, source_target_pairs={{0,16},{8,24},{16,0},{24,8},{1,17},{9,25},{17,1},{25,9},{2,18},{10... | collective-permute-start | bytes 61448 | tf_op jit(solution)/shard_map/ppermute | solution.py:971
  372.9 12.2 %collective-permute-start.41 = (bf16[2,64,512]{2,1,0:T(8,128)(2,1)S(1)}, bf16[2,64,512]{2,1,0:T(8,128)(2,1)S(1)}, u32[]{:S(2)}, u32[]{:S(2)}) collective-permute-start(bf16[2,64,512]{2,1,0:T(8,128)(2,1)S(1)} %maximum_select_fusion.6), channel_id=1, source_target_pairs={{0,1},{1,0},{2,3},{3,2},{4,5},{5,4},{6,7},{7,6},{8,9},{9,8},{10,11... | collective-permute-start | bytes 393224 | tf_op jit(solution)/shard_map/ppermute | solution.py:971
  373.0 12.2 %collective-permute-start.46 = (bf16[2,16,640]{2,1,0:T(8,128)(2,1)S(1)}, bf16[2,16,640]{2,1,0:T(8,128)(2,1)S(1)}, u32[]{:S(2)}, u32[]{:S(2)}) collective-permute-start(bf16[2,16,640]{2,1,0:T(8,128)(2,1)S(1)} %maximum_select_fusion.11), channel_id=1, source_target_pairs={{0,4},{4,0},{1,5},{5,1},{2,6},{6,2},{3,7},{7,3},{8,12},{12,8},{9,1... | collective-permute-start | bytes 122888 | tf_op jit(solution)/shard_map/ppermute | solution.py:971
  385.2 6.4 %collective-permute-start.42 = (bf16[2,64,1024]{2,1,0:T(8,128)(2,1)S(1)}, bf16[2,64,1024]{2,1,0:T(8,128)(2,1)S(1)}, u32[]{:S(2)}, u32[]{:S(2)}) collective-permute-start(bf16[2,64,1024]{2,1,0:T(8,128)(2,1)S(1)} %maximum_select_fusion.3), channel_id=1, source_target_pairs={{0,4},{4,0},{1,5},{5,1},{2,6},{6,2},{3,7},{7,3},{8,12},{12,8},{9,1... | collective-permute-start | bytes 786440 | tf_op jit(solution)/shard_map/ppermute | solution.py:971
  385.3 6.5 %collective-permute-start.47 = (bf16[2,16,1280]{2,1,0:T(8,128)(2,1)S(1)}, bf16[2,16,1280]{2,1,0:T(8,128)(2,1)S(1)}, u32[]{:S(2)}, u32[]{:S(2)}) collective-permute-start(bf16[2,16,1280]{2,1,0:T(8,128)(2,1)S(1)} %maximum_select_fusion.8), channel_id=1, source_target_pairs={{0,8},{8,0},{16,24},{24,16},{1,9},{9,1},{17,25},{25,17},{2,10},{10... | collective-permute-start | bytes 245768 | tf_op jit(solution)/shard_map/ppermute | solution.py:971
  (28 other events, 264.8 us)
Sparse Core Ops, SparseCore 0:
  83.7 86.2 all-reduce.2
  212.3 87.4 all-reduce.4
  302.1 42.8 reduce-scatter.2
  347.2 47.2 reduce-scatter.4
